TPU v7x, 128 devices: a whole 4x4x4 slice. The times are simulated.
128 devices in a mesh: dp: 4 (over z), context: 4 (over x_lo, core), expert: 8 (over x_hi, y).
Axes of the slice: x: 4 (x_hi: 2, x_lo: 2; x = x_hi * 2 + x_lo), y: 4, z: 4, core: 2. Of those that a mesh axis runs over, the one named last changes fastest.
Arguments:
- inputs: bfloat16 [4, 4096, 1024], P('dp', ('context', 'expert')), may hold values from -6 to 6
- prenorm_gain: float32 [1024], replicated, may hold values from 0.1 to 1.9
- query_weight: bfloat16 [1024, 512], replicated, may hold values from -4 to 4
- key_weight: bfloat16 [1024, 256], replicated, may hold values from -4 to 4
- value_weight: bfloat16 [1024, 256], replicated, may hold values from -0.1875 to 0.1875
- output_weight: bfloat16 [512, 1024], replicated, may hold values from -0.75 to 0.75
- midnorm_gain: float32 [1024], replicated, may hold values from 0.1 to 1.9
- router_weight: bfloat16 [1024, 32], replicated, may hold values from -0.1875 to 0.1875
- gate_weight: bfloat16 [32, 1024, 512], P('expert'), may hold values from -0.1875 to 0.1875
- up_weight: bfloat16 [32, 1024, 512], P('expert'), may hold values from -0.1875 to 0.1875
- down_weight: bfloat16 [32, 512, 1024], P('expert'), may hold values from -0.25 to 0.25
- expert_ids: int32 [4, 4096, 8], P('dp', ('context', 'expert')), may hold values from 0 to 31, all different within a row; in each aligned block of 128 rows (0 to 127, 128 to 255, ..., all dimensions but the last counted through in order) at most 64 rows name the same one
- cotangent: bfloat16 [4, 4096, 1024], P('dp', ('context', 'expert')), may hold values from -6 to 6
Outputs:
- outputs: bfloat16 [4, 4096, 1024], P('dp', ('context', 'expert'))
- input_gradient: float32 [4, 4096, 1024], P('dp', ('context', 'expert'))
- prenorm_gradient: float32 [1024], replicated
- query_gradient: float32 [1024, 512], replicated
- key_gradient: float32 [1024, 256], replicated
- value_gradient: float32 [1024, 256], replicated
- output_gradient: float32 [512, 1024], replicated
- midnorm_gradient: float32 [1024], replicated
- router_gradient: float32 [1024, 32], replicated
- gate_gradient: float32 [32, 1024, 512], P('expert', ('dp', 'context'))
- up_gradient: float32 [32, 1024, 512], P('expert', ('dp', 'context'))
- down_gradient: float32 [32, 512, 1024], P('expert', ('dp', 'context'))
Inputs may be any that keep to these rules, and one draw needn't show every extreme that they name: `expert_ids`: in each aligned block of 128 positions of a sequence (the tokens of one device) no expert is named by more than 64 tokens, a bound that some block reaches; the 8 experts of a token are distinct.
All inputs are finite; a program needn't handle non-finite values.
Results may differ from a plain program's by a relative error of at most 0.023.
The roundings to bfloat16 on the way count: a program that leaves them out, or rounds other values in their place, can miss the bound.
Values may be sent and summed in bfloat16 or wider, within the bound.
A program may use at most 192 MiB of HBM per device.

v0:
```python
import jax
import jax.numpy as jnp
from jax import lax
from jax.sharding import PartitionSpec as P

HEADS = 8
KV_HEADS = 4
HEAD_DIM = 64
EXPERTS = 32
TOP = 8
CAP = 64


EPSILON = 1e-06
ROPE_BASE = 10000.0


def product(form, left, right):
    return jnp.einsum(form, left, right, preferred_element_type=jnp.float32)


def rope_tables(positions, head_size):
    half_dim = head_size // 2
    frequency = ROPE_BASE ** (-2.0 * jnp.arange(half_dim, dtype=jnp.float32) / head_size)
    angles = positions.astype(jnp.float32)[:, None] * frequency[None, :]
    angles = jnp.concatenate([angles, angles], axis=1)
    return (jnp.cos(angles), jnp.sin(angles))


def rotate(values, cosine, sine_table):
    half_dim = values.shape[-1] // 2
    turned = jnp.concatenate([-values[..., half_dim:], values[..., :half_dim]], axis=-1)
    return values * cosine[:, None, :] + turned * sine_table[:, None, :]


def rotate_back(grads, cosine, sine_table):
    half_dim = grads.shape[-1] // 2
    scaled = grads * sine_table[:, None, :]
    turned = jnp.concatenate([scaled[..., half_dim:], -scaled[..., :half_dim]], axis=-1)
    return grads * cosine[:, None, :] + turned


def norm_forward(values, gain_vec):
    inverse = lax.rsqrt(jnp.mean(values * values, axis=-1, keepdims=True) + EPSILON)
    normed = values * inverse
    return (inverse, normed, (normed * gain_vec).astype(jnp.bfloat16))


def norm_backward(grad_out, normed, inverse, gain_vec):
    gain_grad = jnp.sum(grad_out * normed, axis=0)
    scaled = grad_out * gain_vec
    inner = jnp.mean(scaled * normed, axis=-1, keepdims=True)
    return (gain_grad, inverse * (scaled - normed * inner))


def score_table(queries, keys_all, query_pos, key_pos):
    factor = queries.shape[-1] ** (-0.5)
    scores = product("tkgd,skd->kgts", queries, keys_all) * factor
    allowed = key_pos[None, :] <= query_pos[:, None]
    return jnp.where(allowed, scores, -jnp.inf)


def attention_forward(queries, keys_all, values_all, query_pos, key_pos):
    scores = score_table(queries, keys_all, query_pos, key_pos)
    maximum = jnp.max(scores, axis=-1, keepdims=True)
    logsum = maximum + jnp.log(jnp.sum(jnp.exp(scores - maximum), axis=-1, keepdims=True))
    soft_round = jnp.exp(scores - logsum).astype(jnp.bfloat16)
    mixture = product("kgts,skd->tkgd", soft_round, values_all)
    return (logsum, mixture.astype(jnp.bfloat16))


def score_grads(queries, keys_all, values_all, query_pos, key_pos, logsum, delta, grad_mix):
    scores = score_table(queries, keys_all, query_pos, key_pos)
    soft_exact = jnp.exp(scores - logsum)
    soft_round = soft_exact.astype(jnp.bfloat16)
    grad_soft = product("tkgd,skd->kgts", grad_mix, values_all)
    grad_score = (soft_exact * (grad_soft - delta)).astype(jnp.bfloat16)
    return (soft_round, grad_score)


def slot_targets(ids_block):
    flat_ids = ids_block.reshape(-1)
    onehot = (flat_ids[:, None] == jnp.arange(EXPERTS, dtype=jnp.int32)[None, :]).astype(jnp.int32)
    before = jnp.cumsum(onehot, axis=0) - onehot
    slot_index = jnp.sum(before * onehot, axis=1)
    return flat_ids * CAP + slot_index


def fill_slots(pair_rows, targets):
    empty = jnp.zeros((EXPERTS * CAP, pair_rows.shape[1]), pair_rows.dtype)
    return empty.at[targets].set(pair_rows)


def local(
    inputs,
    prenorm_gain,
    query_weight,
    key_weight,
    value_weight,
    output_weight,
    midnorm_gain,
    router_weight,
    gate_weight,
    up_weight,
    down_weight,
    expert_ids,
    cotangent,
):
    seq_tokens = inputs.shape[1]
    model_width = inputs.shape[2]
    groups = HEADS // KV_HEADS
    factor = HEAD_DIM ** (-0.5)
    block_index = lax.axis_index(("context", "expert"))
    block_count = lax.axis_size(("context", "expert"))
    own_positions = block_index * seq_tokens + jnp.arange(seq_tokens, dtype=jnp.int32)
    all_positions = jnp.arange(seq_tokens * block_count, dtype=jnp.int32)
    cosine, sine_table = rope_tables(own_positions, HEAD_DIM)
    input_float = inputs[0].astype(jnp.float32)
    inverse_first, normed_first, attn_input = norm_forward(input_float, prenorm_gain)
    query_raw = jnp.dot(attn_input, query_weight, preferred_element_type=jnp.float32).reshape(
        seq_tokens, HEADS, HEAD_DIM
    )
    key_raw = jnp.dot(attn_input, key_weight, preferred_element_type=jnp.float32).reshape(
        seq_tokens, KV_HEADS, HEAD_DIM
    )
    value_raw = jnp.dot(attn_input, value_weight, preferred_element_type=jnp.float32).reshape(
        seq_tokens, KV_HEADS, HEAD_DIM
    )
    query_rot = (
        rotate(query_raw, cosine, sine_table)
        .astype(jnp.bfloat16)
        .reshape(seq_tokens, KV_HEADS, groups, HEAD_DIM)
    )
    key_rot = rotate(key_raw, cosine, sine_table).astype(jnp.bfloat16)
    value_half = value_raw.astype(jnp.bfloat16)
    keys_all, values_all = (
        lax.all_gather(key_rot, ("context", "expert"), axis=0, tiled=True),
        lax.all_gather(value_half, ("context", "expert"), axis=0, tiled=True),
    )
    logsum, mixture = attention_forward(
        query_rot, keys_all, values_all, own_positions, all_positions
    )
    mixture_flat = mixture.reshape(seq_tokens, HEADS * HEAD_DIM)
    after_attn = input_float + jnp.dot(
        mixture_flat, output_weight, preferred_element_type=jnp.float32
    )
    inverse_second, normed_second, moe_input = norm_forward(after_attn, midnorm_gain)
    logits = jnp.dot(moe_input, router_weight, preferred_element_type=jnp.float32)
    ids_local = expert_ids[0]
    chosen = jnp.take_along_axis(logits, ids_local, axis=1)
    gate_probs = jax.nn.softmax(chosen, axis=-1)
    targets = slot_targets(ids_local)
    owners = lax.axis_size("expert")
    local_experts = gate_weight.shape[0]
    send_rows = fill_slots(jnp.repeat(moe_input, TOP, axis=0), targets)
    received = lax.all_to_all(
        send_rows.reshape(owners, local_experts * CAP, model_width),
        "expert",
        split_axis=0,
        concat_axis=0,
        tiled=True,
    )
    received = received.reshape(owners, local_experts, CAP, model_width)
    gate_act = product("secd,edf->secf", received, gate_weight)
    up_act = product("secd,edf->secf", received, up_weight)
    silu_gate = jax.nn.silu(gate_act)
    hidden = (silu_gate * up_act).astype(jnp.bfloat16)
    expert_out = product("secf,efd->secd", hidden, down_weight).astype(jnp.bfloat16)
    returned = lax.all_to_all(
        expert_out.reshape(owners, local_experts * CAP, model_width),
        "expert",
        split_axis=0,
        concat_axis=0,
        tiled=True,
    )
    picked = returned.reshape(EXPERTS * CAP, model_width)[targets].reshape(
        seq_tokens, TOP, model_width
    )
    moe_out = jnp.sum(gate_probs[:, :, None] * picked.astype(jnp.float32), axis=1)
    outputs = (after_attn + moe_out).astype(jnp.bfloat16)
    grad_out = cotangent[0].astype(jnp.float32)
    grad_gates = jnp.sum(grad_out[:, None, :] * picked.astype(jnp.float32), axis=-1)
    grad_pairs = (gate_probs[:, :, None] * grad_out[:, None, :]).astype(jnp.bfloat16)
    grad_send = fill_slots(grad_pairs.reshape(seq_tokens * TOP, model_width), targets)
    grad_expert = lax.all_to_all(
        grad_send.reshape(owners, local_experts * CAP, model_width),
        "expert",
        split_axis=0,
        concat_axis=0,
        tiled=True,
    )
    grad_expert = grad_expert.reshape(owners, local_experts, CAP, model_width)
    grad_hidden = product("secd,efd->secf", grad_expert, down_weight)
    down_grad = product("secf,secd->efd", hidden, grad_expert)
    sigmoid_gate = jax.nn.sigmoid(gate_act)
    silu_slope = sigmoid_gate * (1.0 + gate_act * (1.0 - sigmoid_gate))
    grad_gate = (grad_hidden * up_act * silu_slope).astype(jnp.bfloat16)
    grad_up = (grad_hidden * silu_gate).astype(jnp.bfloat16)
    gate_grad = product("secd,secf->edf", received, grad_gate)
    up_grad = product("secd,secf->edf", received, grad_up)
    grad_buffer = (
        product("secf,edf->secd", grad_gate, gate_weight)
        + product("secf,edf->secd", grad_up, up_weight)
    ).astype(jnp.bfloat16)
    grad_return = lax.all_to_all(
        grad_buffer.reshape(owners, local_experts * CAP, model_width),
        "expert",
        split_axis=0,
        concat_axis=0,
        tiled=True,
    )
    grad_back = grad_return.reshape(EXPERTS * CAP, model_width)[targets].reshape(
        seq_tokens, TOP, model_width
    )
    gate_sum, up_sum, down_sum = (
        lax.psum_scatter(gate_grad, ("dp", "context"), scatter_dimension=1, tiled=True),
        lax.psum_scatter(up_grad, ("dp", "context"), scatter_dimension=1, tiled=True),
        lax.psum_scatter(down_grad, ("dp", "context"), scatter_dimension=1, tiled=True),
    )
    grad_moe_in = jnp.sum(grad_back.astype(jnp.float32), axis=1)
    grad_chosen = gate_probs * (
        grad_gates - jnp.sum(gate_probs * grad_gates, axis=-1, keepdims=True)
    )
    onehot = (ids_local[:, :, None] == jnp.arange(EXPERTS, dtype=jnp.int32)[None, None, :]).astype(
        jnp.float32
    )
    grad_logits = jnp.einsum("tk,tke->te", grad_chosen, onehot)
    router_grad = jnp.einsum(
        "td,te->de", moe_input.astype(jnp.float32), grad_logits, precision=lax.Precision.HIGHEST
    )
    grad_moe_in = grad_moe_in + jnp.einsum(
        "te,de->td", grad_logits, router_weight.astype(jnp.float32), precision=lax.Precision.HIGHEST
    )
    midnorm_grad, grad_after = norm_backward(
        grad_moe_in, normed_second, inverse_second, midnorm_gain
    )
    grad_after = grad_out + grad_after
    grad_after_half = grad_after.astype(jnp.bfloat16)
    output_grad = product("tq,td->qd", mixture_flat, grad_after_half)
    grad_mix = product("td,qd->tq", grad_after_half, output_weight).astype(jnp.bfloat16)
    grad_mix = grad_mix.reshape(seq_tokens, KV_HEADS, groups, HEAD_DIM)
    delta = product("tkgd,tkgd->kgt", grad_mix, mixture)[..., None]
    soft_round, grad_score = score_grads(
        query_rot, keys_all, values_all, own_positions, all_positions, logsum, delta, grad_mix
    )
    grad_query = product("kgts,skd->tkgd", grad_score, keys_all) * factor
    key_terms = product("kgts,tkgd->skd", grad_score, query_rot) * factor
    value_terms = product("kgts,tkgd->skd", soft_round, grad_mix)
    grad_keys, grad_values = (
        lax.psum_scatter(key_terms, ("context", "expert"), scatter_dimension=0, tiled=True),
        lax.psum_scatter(value_terms, ("context", "expert"), scatter_dimension=0, tiled=True),
    )
    query_back = (
        rotate_back(grad_query.reshape(seq_tokens, HEADS, HEAD_DIM), cosine, sine_table)
        .reshape(seq_tokens, HEADS * HEAD_DIM)
        .astype(jnp.bfloat16)
    )
    key_back = (
        rotate_back(grad_keys, cosine, sine_table)
        .reshape(seq_tokens, KV_HEADS * HEAD_DIM)
        .astype(jnp.bfloat16)
    )
    value_back = grad_values.reshape(seq_tokens, KV_HEADS * HEAD_DIM).astype(jnp.bfloat16)
    query_grad = product("td,tq->dq", attn_input, query_back)
    key_grad = product("td,tq->dq", attn_input, key_back)
    value_grad = product("td,tq->dq", attn_input, value_back)
    grad_attn_in = (
        product("tq,dq->td", query_back, query_weight)
        + product("tq,dq->td", key_back, key_weight)
        + product("tq,dq->td", value_back, value_weight)
    )
    prenorm_grad, grad_inputs = norm_backward(
        grad_attn_in, normed_first, inverse_first, prenorm_gain
    )
    grad_inputs = grad_after + grad_inputs
    dense = lax.psum(
        (prenorm_grad, query_grad, key_grad, value_grad, output_grad, midnorm_grad, router_grad),
        ("dp", "context", "expert"),
    )
    return (
        outputs[None],
        grad_inputs[None],
        dense[0],
        dense[1],
        dense[2],
        dense[3],
        dense[4],
        dense[5],
        dense[6],
        gate_sum,
        up_sum,
        down_sum,
    )


def solution(mesh):
    in_specs = (
        P("dp", ("context", "expert"), None),
        P(),
        P(),
        P(),
        P(),
        P(),
        P(),
        P(),
        P("expert", None, None),
        P("expert", None, None),
        P("expert", None, None),
        P("dp", ("context", "expert"), None),
        P("dp", ("context", "expert"), None),
    )
    out_specs = (
        P("dp", ("context", "expert"), None),
        P("dp", ("context", "expert"), None),
        P(),
        P(),
        P(),
        P(),
        P(),
        P(),
        P(),
        P("expert", ("dp", "context"), None),
        P("expert", ("dp", "context"), None),
        P("expert", ("dp", "context"), None),
    )
    return jax.shard_map(local, mesh=mesh, in_specs=in_specs, out_specs=out_specs, check_vma=False)
```

profile of v0, /device:TPU:1, one launch (start us, length us, event | category | flops | bytes accessed | tf_op | source)
XLA Modules:
  0.0 1247.9 jit_solution(5945250231588639050)
XLA Ops:
  16.5 9.0 reduce-window.6
  29.8 61.8 %all-gather.5.cloned.1.call-done = bf16[4096,4,64]{0,2,1:T(8,128)(2,1)} async-done(((bf16[128,4,64]{0,2,1:T(8,128)(2,1)}), bf16[4096,4,64]{0,2,1:T(8,128)(2,1)}) %all-gather.5.cloned.1.call-update) | async-done | bytes 2097168 | tf_op jit(solution)/shard_map/all_gather | solution.py:137
  91.5 10.1 fusion.3
  101.6 9.2 exponential_reduce_fusion
  110.9 58.3 %all-gather.3.cloned.1.call-done = bf16[4096,4,64]{0,2,1:T(8,128)(2,1)} async-done(((bf16[128,4,64]{0,2,1:T(8,128)(2,1)}), bf16[4096,4,64]{0,2,1:T(8,128)(2,1)}) %all-gather.3.cloned.1.call-update) | async-done | bytes 2097168 | tf_op jit(solution)/shard_map/all_gather | solution.py:138
  169.1 10.0 fusion.64
  213.4 28.3 %all-to-all-done = bf16[8,256,1024]{2,1,0:T(8,128)(2,1)} async-done(((bf16[8,256,1024]{2,1,0:T(8,128)(2,1)}), bf16[8,256,1024]{2,1,0:T(8,128)(2,1)}, u32[]{:S(2)}, u32[]{:S(2)}) %all-to-all-start) | async-done | bytes 4194336 | tf_op jit(solution)/shard_map/all_to_all | solution.py:156
  261.6 34.3 %all-to-all-done.2 = bf16[8,256,1024]{2,1,0:T(8,128)(2,1)} async-done(((bf16[8,256,1024]{2,1,0:T(8,128)(2,1)}), bf16[8,256,1024]{2,1,0:T(8,128)(2,1)}, u32[]{:S(2)}, u32[]{:S(2)}) %all-to-all-start.2) | async-done | bytes 4194336 | tf_op jit(solution)/shard_map/all_to_all | solution.py:185
  295.9 11.9 fusion.18
  330.7 35.8 %all-to-all-done.1 = bf16[8,256,1024]{2,1,0:T(8,128)(2,1)} async-done(((bf16[8,256,1024]{2,1,0:T(8,128)(2,1)}), bf16[8,256,1024]{2,1,0:T(8,128)(2,1)}, u32[]{:S(2)}, u32[]{:S(2)}) %all-to-all-start.1) | async-done | bytes 4194336 | tf_op jit(solution)/shard_map/all_to_all | solution.py:169
  372.7 9.2 gather_fusion
  386.8 33.6 %all-to-all-done.3 = bf16[8,256,1024]{2,1,0:T(8,128)(2,1)} async-done(((bf16[8,256,1024]{2,1,0:T(8,128)(2,1)}), bf16[8,256,1024]{2,1,0:T(8,128)(2,1)}, u32[]{:S(2)}, u32[]{:S(2)}) %all-to-all-start.3) | async-done | bytes 4194336 | tf_op jit(solution)/shard_map/all_to_all | solution.py:205
  420.4 8.7 gather_fusion.1
  437.5 10.6 fusion.1
  456.1 11.8 convolution_bitcast_fusion
  478.2 130.0 %reduce-scatter.6.cloned.1.call-done = f32[128,4,64]{0,2,1:T(8,128)} async-done(((f32[4096,4,64]{0,2,1:T(8,128)}), f32[128,4,64]{0,2,1:T(8,128)}) %reduce-scatter.6.cloned.1.call-update) | async-done | bytes 131088 | tf_op jit(solution)/shard_map/reduce_scatter | solution.py:250
  609.1 158.0 %reduce-scatter.8.cloned.1.call-done = f32[128,4,64]{0,2,1:T(8,128)} async-done(((f32[4096,4,64]{0,2,1:T(8,128)}), f32[128,4,64]{0,2,1:T(8,128)}) %reduce-scatter.8.cloned.1.call-update) | async-done | bytes 131088 | tf_op jit(solution)/shard_map/reduce_scatter | solution.py:251
  781.6 8.6 convolution_bitcast_fusion.3
  790.5 8.5 convolution_bitcast_fusion.2
  802.6 70.4 %all-reduce = (f32[1024]{0:T(1024)}, f32[1024]{0:T(1024)}) all-reduce(f32[1024]{0:T(1024)S(1)} %get-tuple-element.16, f32[1024]{0:T(1024)S(1)} %get-tuple-element.14), channel_id=1, replica_groups=mesh['dp'=4,'context'=4,'expert'=8] {'dp','context','expert'}, use_global_device_ids=true, to_apply=%region_20.21 | all-reduce | flops 2048 | bytes 16384 | tf_op jit(solution)/shard_map/psum | solution.py:276
  874.0 62.8 %all-reduce.4.cloned.1.call-done = (f32[1024,512]{1,0:T(8,128)}, f32[1024,256]{1,0:T(8,128)}, f32[1024,256]{1,0:T(8,128)}, f32[512,1024]{1,0:T(8,128)}, f32[1024,32]{0,1:T(8,128)}) async-done(((f32[1024,512]{1,0:T(8,128)}, f32[1024,256]{1,0:T(8,128)}, f32[1024,256]{1,0:T(8,128)}, f32[512,1024]{1,0:T(8,128)}, f32[1024,32]{0,1:T(8,128)}), (f32[1024,512]{1,0:T(8,128)}, f32[1024,256]{1,0:T(8,128)}, ...) | async-done | bytes 6422544 | tf_op jit(solution)/shard_map/psum | solution.py:276
  936.7 97.5 %reduce-scatter.14.cloned.1.call-done = f32[4,32,1024]{2,1,0:T(8,128)} async-done(((f32[4,512,1024]{2,1,0:T(8,128)}), f32[4,32,1024]{2,1,0:T(8,128)}) %reduce-scatter.14.cloned.1.call-update) | async-done | bytes 524304 | tf_op jit(solution)/shard_map/reduce_scatter | solution.py:218
  1034.2 99.7 %reduce-scatter.10.cloned.1.call-done = f32[4,64,512]{2,1,0:T(8,128)} async-done(((f32[4,1024,512]{2,1,0:T(8,128)}), f32[4,64,512]{2,1,0:T(8,128)}) %reduce-scatter.10.cloned.1.call-update) | async-done | bytes 524304 | tf_op jit(solution)/shard_map/reduce_scatter | solution.py:216
  1133.9 99.7 %reduce-scatter.12.cloned.1.call-done = f32[4,64,512]{2,1,0:T(8,128)} async-done(((f32[4,1024,512]{2,1,0:T(8,128)}), f32[4,64,512]{2,1,0:T(8,128)}) %reduce-scatter.12.cloned.1.call-update) | async-done | bytes 524304 | tf_op jit(solution)/shard_map/reduce_scatter | solution.py:217
  (177 shorter events, 155.2 us)
Async XLA Ops:
  7.2 172.0 %copy-start = (bf16[512,1024]{1,0:T(8,128)(2,1)S(1)}, bf16[512,1024]{1,0:T(8,128)(2,1)}, u32[]{:S(2)}) copy-start(bf16[512,1024]{1,0:T(8,128)(2,1)} %param.18) | copy-start | bytes 3145732
  7.2 19.4 %copy-start.3 = (bf16[1024,512]{1,0:T(8,128)(2,1)S(1)}, bf16[1024,512]{1,0:T(8,128)(2,1)}, u32[]{:S(2)}) copy-start(bf16[1024,512]{1,0:T(8,128)(2,1)} %param.15) | copy-start | bytes 3145732
  7.2 84.3 %all-gather.5.cloned.1.call-start = ((), (), s32[]{:S(2)}) async-start(), calls=%async_computation.10 | async-start | bytes 2162688 | tf_op jit(solution)/shard_map/all_gather | solution.py:137
  8.7 20.1 %copy-start.2 = (bf16[1,128,1024]{2,1,0:T(8,128)(2,1)S(1)}, bf16[1,128,1024]{2,1,0:T(8,128)(2,1)}, u32[]{:S(2)}) copy-start(bf16[1,128,1024]{2,1,0:T(8,128)(2,1)} %param.13) | copy-start | bytes 786436
  8.7 20.1 %copy-start.19 = (f32[1024]{0:T(1024)S(1)}, f32[1024]{0:T(1024)}, u32[]{:S(2)}) copy-start(f32[1024]{0:T(1024)} %param.14) | copy-start | bytes 12292
  12.0 157.1 %all-gather.3.cloned.1.call-start = ((), (), s32[]{:S(2)}) async-start(), calls=%async_computation.9 | async-start | bytes 2162688 | tf_op jit(solution)/shard_map/all_gather | solution.py:138
  28.8 150.9 %copy-start.23 = (s32[1024,1]{0,1:T(1,128)}, s32[1024,1]{0,1:T(1,128)S(1)}, u32[]{:S(2)}) copy-start(s32[1024,1]{0,1:T(1,128)S(1)} %compare_select_fusion.1) | copy-start | bytes 12292
  110.8 68.3 %copy-start.25 = (f32[1,8,128]{2,1,0:T(8,128)}, f32[1,8,128]{2,1,0:T(8,128)S(1)}, u32[]{:S(2)}) copy-start(f32[1,8,128]{2,1,0:T(8,128)S(1)} %log_add_fusion) | copy-start | bytes 12292
  169.1 10.5 copy-start.21
  187.8 53.9 %all-to-all-start = ((bf16[8,256,1024]{2,1,0:T(8,128)(2,1)}), bf16[8,256,1024]{2,1,0:T(8,128)(2,1)}, u32[]{:S(2)}, u32[]{:S(2)}) async-start(bf16[8,256,1024]{2,1,0:T(8,128)(2,1)} %bitcast.324), calls=%async_computation | async-start | bytes 8388608 | tf_op jit(solution)/shard_map/all_to_all | solution.py:156
  194.3 10.8 copy-start.24
  201.5 40.3 %copy-start.11 = (f32[128,8]{1,0:T(8,128)}, f32[128,8]{1,0:T(8,128)S(1)}, u32[]{:S(2)}) copy-start(f32[128,8]{1,0:T(8,128)S(1)} %reshape.477) | copy-start | bytes 12292
  241.8 54.2 %all-to-all-start.2 = ((bf16[8,256,1024]{2,1,0:T(8,128)(2,1)}), bf16[8,256,1024]{2,1,0:T(8,128)(2,1)}, u32[]{:S(2)}, u32[]{:S(2)}) async-start(bf16[8,256,1024]{2,1,0:T(8,128)(2,1)} %bitcast.326), calls=%async_computation.2 | async-start | bytes 8388608 | tf_op jit(solution)/shard_map/all_to_all | solution.py:185
  295.9 11.9 copy-start.27
  312.6 53.8 %all-to-all-start.1 = ((bf16[8,256,1024]{2,1,0:T(8,128)(2,1)}), bf16[8,256,1024]{2,1,0:T(8,128)(2,1)}, u32[]{:S(2)}, u32[]{:S(2)}) async-start(bf16[8,256,1024]{2,1,0:T(8,128)(2,1)} %bitcast.327), calls=%async_computation.1 | async-start | bytes 8388608 | tf_op jit(solution)/shard_map/all_to_all | solution.py:169
  366.5 53.9 %all-to-all-start.3 = ((bf16[8,256,1024]{2,1,0:T(8,128)(2,1)}), bf16[8,256,1024]{2,1,0:T(8,128)(2,1)}, u32[]{:S(2)}, u32[]{:S(2)}) async-start(bf16[8,256,1024]{2,1,0:T(8,128)(2,1)} %bitcast.325), calls=%async_computation.3 | async-start | bytes 8388608 | tf_op jit(solution)/shard_map/all_to_all | solution.py:205
  371.7 236.5 %reduce-scatter.6.cloned.1.call-start = ((), (), s32[]{:S(2)}) async-start(), calls=%async_computation.11 | async-start | bytes 4325376 | tf_op jit(solution)/shard_map/reduce_scatter | solution.py:250
  455.9 311.3 %reduce-scatter.8.cloned.1.call-start = ((), (), s32[]{:S(2)}) async-start(), calls=%async_computation.12 | async-start | bytes 4325376 | tf_op jit(solution)/shard_map/reduce_scatter | solution.py:251
  467.9 468.8 %all-reduce.4.cloned.1.call-start = ((), (), s32[]{:S(2)}) async-start(), calls=%async_computation.16 | async-start | bytes 12845056 | tf_op jit(solution)/shard_map/psum | solution.py:276
  773.0 261.2 %reduce-scatter.14.cloned.1.call-start = ((), (), s32[]{:S(2)}) async-start(), calls=%async_computation.15 | async-start | bytes 8912896 | tf_op jit(solution)/shard_map/reduce_scatter | solution.py:218
  781.6 352.4 %reduce-scatter.10.cloned.1.call-start = ((), (), s32[]{:S(2)}) async-start(), calls=%async_computation.13 | async-start | bytes 8912896 | tf_op jit(solution)/shard_map/reduce_scatter | solution.py:216
  790.2 443.4 %reduce-scatter.12.cloned.1.call-start = ((), (), s32[]{:S(2)}) async-start(), calls=%async_computation.14 | async-start | bytes 8912896 | tf_op jit(solution)/shard_map/reduce_scatter | solution.py:217
  936.7 300.1 %copy-start.13 = (f32[1024,256]{1,0:T(8,128)S(1)}, f32[1024,256]{1,0:T(8,128)}, u32[]{:S(2)}) copy-start(f32[1024,256]{1,0:T(8,128)} %get-tuple-element.52) | copy-start | bytes 3145732
  936.7 301.1 %copy-start.12 = (f32[1024,256]{1,0:T(8,128)S(1)}, f32[1024,256]{1,0:T(8,128)}, u32[]{:S(2)}) copy-start(f32[1024,256]{1,0:T(8,128)} %get-tuple-element.53) | copy-start | bytes 3145732
  (17 other events, 77.1 us)
Sparse Core Ops, SparseCore 0:
  12.2 79.3 all-gather.4
  93.7 75.3 all-gather.2
  456.0 152.1 reduce-scatter.5
  610.4 156.6 reduce-scatter.7
  773.5 163.1 all-reduce.3
  939.7 94.5 reduce-scatter.13
  1037.3 96.5 reduce-scatter.9
  1137.0 96.5 reduce-scatter.11
where the time goes:
time: 1260 us; the launch traced here: 1250 us
  waiting for transfers between devices  900 us (71%)
  matrix products  136 us (11%)
  blocking collectives  70.4 us (6%)
  local copies, waits for them, and re-layouts  57.8 us (5%)
  other arithmetic  47.7 us (4%)
  starting transfers between devices  21.5 us (2%)
  between operations  15 us (1%)
    reduce_scatter x1, waiting for transfers between devices, local(): lax.psum_scatter(value_terms, ('context', 'expert'), scatter_dimension=0,...  158 us
    reduce_scatter x1, waiting for transfers between devices, local(): lax.psum_scatter(key_terms, ('context', 'expert'), scatter_dimension=0, t...  130 us
    dot_general x23, matrix products, product(): return jnp.einsum(form, left, right, preferred_element_type=jnp.float32)  128 us
    reduce_scatter x1, waiting for transfers between devices, local(): lax.psum_scatter(up_grad, ('dp', 'context'), scatter_dimension=1, tiled=T...  99.7 us
    reduce_scatter x1, waiting for transfers between devices, local(): lax.psum_scatter(gate_grad, ('dp', 'context'), scatter_dimension=1, tiled...  99.7 us
    reduce_scatter x1, waiting for transfers between devices, local(): lax.psum_scatter(down_grad, ('dp', 'context'), scatter_dimension=1, tiled...  97.5 us
    psum x1, blocking collectives, local(): lax.psum((prenorm_grad, query_grad, key_grad, value_grad, output_grad, mi...  70.4 us
    psum x1, waiting for transfers between devices, local(): lax.psum((prenorm_grad, query_grad, key_grad, value_grad, output_grad, mi...  62.8 us
  transfers between devices with their start and end apart: 12, of which 12 were waited for; matrix products, arithmetic and copies ran while one was open for 12% of the time, Pallas kernels for 0%

commit v1 on v0

v1 whole, which is shorter than its diff:
```python
import functools

import jax
import jax.numpy as jnp
from jax import lax
from jax.experimental import pallas as pl
from jax.experimental.pallas import tpu as pltpu
from jax.sharding import PartitionSpec as P

HEADS = 8
KV_HEADS = 4
HEAD_DIM = 64
EXPERTS = 32
TOP = 8
CAP = 64
EPSILON = 1e-06
ROPE_BASE = 10000.0
F32 = jnp.float32
BF16 = jnp.bfloat16
MESH_ID = pl.DeviceIdType.MESH
SEQ_AXES = ("context", "expert")


def dot(left, right):
    return jnp.dot(left, right, preferred_element_type=F32)


def dot_t(left, right):
    return lax.dot_general(left, right, (((1,), (1,)), ((), ())), preferred_element_type=F32)


def t_dot(left, right):
    return lax.dot_general(left, right, (((0,), (0,)), ((), ())), preferred_element_type=F32)


def coords_of(axes, sizes, index):
    out = {}
    for name in reversed(axes):
        out[name] = lax.rem(index, sizes[name])
        index = index // sizes[name]
    return out


def exchange_body(items, sizes, *refs):
    count = len(items)
    ins, outs, sems = refs[:count], refs[count : 2 * count], refs[2 * count :]
    widest = max((item[0] for item in items), key=len)

    def own_index(axes):
        index = 0
        for name in axes:
            index = index * sizes[name] + lax.axis_index(name)
        return index

    def group_size(axes):
        total = 1
        for name in axes:
            total *= sizes[name]
        return total

    barrier = pltpu.get_barrier_semaphore()
    me, total = own_index(widest), group_size(widest)
    for step in range(1, total):
        peer = coords_of(widest, sizes, lax.rem(me + step, total))
        pl.semaphore_signal(barrier, inc=1, device_id=peer, device_id_type=MESH_ID)
    pl.semaphore_wait(barrier, total - 1)

    waits = []
    for number, (axes, pick) in enumerate(items):
        me, total = own_index(axes), group_size(axes)
        send, recv = sems[2 * number], sems[2 * number + 1]
        for step in range(1, total):
            target = lax.rem(me + step, total)
            peer = coords_of(axes, sizes, target)
            copy = pltpu.make_async_remote_copy(
                src_ref=pick(ins[number], target, peer),
                dst_ref=outs[number].at[me],
                send_sem=send.at[step],
                recv_sem=recv.at[step],
                device_id=peer,
                device_id_type=MESH_ID,
            )
            copy.start()
            waits.append(copy)
        own = pltpu.make_async_copy(
            pick(ins[number], me, coords_of(axes, sizes, me)), outs[number].at[me], send.at[0]
        )
        own.start()
        waits.append(own)
    for copy in waits:
        copy.wait()


def pick_whole(ref, target, peer):
    return ref


def pick_target(ref, target, peer):
    return ref.at[target]


def pick_context(ref, target, peer):
    return ref.at[peer["context"]]


def exchange(cid, sizes, name, *specs):
    arrays = [spec[0] for spec in specs]
    items = [(spec[1], spec[2]) for spec in specs]
    shapes, scratch = [], []
    for array, axes, pick in specs:
        total = 1
        for axis in axes:
            total *= sizes[axis]
        chunk = array.shape if pick is pick_whole else array.shape[1:]
        shapes.append(jax.ShapeDtypeStruct((total, *chunk), array.dtype))
        scratch += [pltpu.SemaphoreType.DMA((total,)), pltpu.SemaphoreType.DMA((total,))]
    space = pl.BlockSpec(memory_space=pltpu.VMEM)
    return pl.pallas_call(
        functools.partial(exchange_body, items, sizes),
        out_shape=shapes,
        in_specs=[space] * len(specs),
        out_specs=[space] * len(specs),
        scratch_shapes=scratch,
        name=name,
        compiler_params=pltpu.CompilerParams(collective_id=cid, has_side_effects=True),
    )(*arrays)


def shift(array, axes, sizes, step):
    total = 1
    for name in axes:
        total *= sizes[name]
    return lax.ppermute(array, axes, [(i, (i + step) % total) for i in range(total)])


def flip(array, axis, size, bit):
    return lax.ppermute(array, axis, [(i, i ^ bit) for i in range(size)])


def rope_tables(positions, head_size):
    half_dim = head_size // 2
    frequency = ROPE_BASE ** (-2.0 * jnp.arange(half_dim, dtype=F32) / head_size)
    angles = positions.astype(F32)[:, None] * frequency[None, :]
    angles = jnp.concatenate([angles, angles], axis=1)
    return (jnp.cos(angles), jnp.sin(angles))


def rotate(values, cosine, sine_table):
    half_dim = values.shape[-1] // 2
    turned = jnp.concatenate([-values[..., half_dim:], values[..., :half_dim]], axis=-1)
    return values * cosine[:, None, :] + turned * sine_table[:, None, :]


def rotate_back(grads, cosine, sine_table):
    half_dim = grads.shape[-1] // 2
    scaled = grads * sine_table[:, None, :]
    turned = jnp.concatenate([scaled[..., half_dim:], -scaled[..., :half_dim]], axis=-1)
    return grads * cosine[:, None, :] + turned


def norm_forward(values, gain_vec):
    inverse = lax.rsqrt(jnp.mean(values * values, axis=-1, keepdims=True) + EPSILON)
    normed = values * inverse
    return (inverse, normed, (normed * gain_vec).astype(BF16))


def norm_backward(grad_out, normed, inverse, gain_vec):
    gain_grad = jnp.sum(grad_out * normed, axis=0)
    scaled = grad_out * gain_vec
    inner = jnp.mean(scaled * normed, axis=-1, keepdims=True)
    return (gain_grad, inverse * (scaled - normed * inner))


def stack_heads(block):
    return jnp.concatenate([block[:, :HEAD_DIM], block[:, HEAD_DIM:]], axis=0)


def side_heads(rows):
    half = rows.shape[0] // 2
    return jnp.concatenate([rows[:half], rows[half:]], axis=1)


def chunk_scores(rows, keys, number, offset):
    tokens = rows.shape[0] // 2
    scores = dot_t(rows, keys) * (HEAD_DIM ** (-0.5))
    last = scores[:, number * 8 * tokens :]
    row_pos = offset * tokens + lax.rem(lax.broadcasted_iota(jnp.int32, last.shape, 0), tokens)
    key_pos = lax.broadcasted_iota(jnp.int32, last.shape, 1)
    last = jnp.where(key_pos <= row_pos, last, -jnp.inf)
    return jnp.concatenate([scores[:, : number * 8 * tokens], last], axis=1)


def attention_forward(queries, kv_all, offset):
    blocks, tokens = queries.shape[:2]
    outs, sums = [], []
    for number in range(blocks):
        width = (number + 1) * 8 * tokens
        rows = stack_heads(queries[number])
        scores = chunk_scores(rows, kv_all[:width, :HEAD_DIM], number, offset)
        maximum = jnp.max(scores, axis=-1, keepdims=True)
        logsum = maximum + jnp.log(jnp.sum(jnp.exp(scores - maximum), axis=-1, keepdims=True))
        soft = jnp.exp(scores - logsum).astype(BF16)
        outs.append(side_heads(dot(soft, kv_all[:width, HEAD_DIM:]).astype(BF16)))
        sums.append(logsum)
    return jnp.stack(outs), sums


def attention_backward(queries, kv_all, mixtures, grad_mix, sums, offset):
    blocks, tokens = queries.shape[:2]
    factor = HEAD_DIM ** (-0.5)
    grad_queries, key_terms, value_terms = [], 0.0, 0.0
    for number in range(blocks):
        width = (number + 1) * 8 * tokens
        rows = stack_heads(queries[number])
        grads = stack_heads(grad_mix[number])
        mixed = stack_heads(mixtures[number])
        keys, values = kv_all[:width, :HEAD_DIM], kv_all[:width, HEAD_DIM:]
        delta = jnp.sum(grads.astype(F32) * mixed.astype(F32), axis=-1, keepdims=True)
        soft = jnp.exp(chunk_scores(rows, keys, number, offset) - sums[number])
        grad_soft = dot_t(grads, values)
        grad_score = (soft * (grad_soft - delta)).astype(BF16)
        soft_round = soft.astype(BF16)
        grad_queries.append(side_heads(dot(grad_score, keys) * factor))
        pad = ((0, blocks * 8 * tokens - width), (0, 0))
        key_terms = key_terms + jnp.pad(t_dot(grad_score, rows) * factor, pad)
        value_terms = value_terms + jnp.pad(t_dot(soft_round, grads), pad)
    return jnp.stack(grad_queries), jnp.concatenate([key_terms, value_terms], axis=1)


def reduce_experts(grads, sizes):
    dp, context = lax.axis_index("dp"), lax.axis_index("context")
    core, side = lax.rem(context, 2), context // 2
    experts, rows, columns = grads.shape
    part = rows // 16
    grads = grads.reshape(experts, 4, 2, 2, part, columns)

    def take(array, index, axis):
        return lax.dynamic_index_in_dim(array, index, axis, keepdims=False)

    other = flip(take(grads, 1 - core, 3).astype(BF16), "context", 4, 1)
    held = take(grads, core, 3) + other.astype(F32)

    def over_dp(array):
        total = take(array, dp, 1)
        for step in range(1, 4):
            sent = take(array, lax.rem(dp + step, 4), 1).astype(BF16)
            total = total + shift(sent, ("dp",), sizes, step).astype(F32)
        return total

    def over_side(array, axis):
        sent = take(array, 1 - side, axis).astype(BF16)
        return take(array, side, axis) + flip(sent, "context", 4, 2).astype(F32)

    half = experts // 2
    first = over_side(over_dp(held[:half]), 1)
    second = over_dp(over_side(held[half:], 2))
    return jnp.concatenate([first, second], axis=0)


def local(
    sizes,
    inputs,
    prenorm_gain,
    query_weight,
    key_weight,
    value_weight,
    output_weight,
    midnorm_gain,
    router_weight,
    gate_weight,
    up_weight,
    down_weight,
    expert_ids,
    cotangent,
):
    tokens, width = inputs.shape[1:]
    owners = sizes["expert"]
    mine = gate_weight.shape[0]
    context, owner = lax.axis_index("context"), lax.axis_index("expert")
    block = context * owners + owner
    positions = block * tokens + jnp.arange(tokens, dtype=jnp.int32)
    cosine, sine_table = rope_tables(positions, HEAD_DIM)

    sent = [shift(cotangent[0], ("expert",), sizes, step) for step in range(1, owners)]
    grad_group = jnp.stack([cotangent[0]] + sent)

    input_float = inputs[0].astype(F32)
    inverse_first, normed_first, attn_input = norm_forward(input_float, prenorm_gain)
    query_raw = dot(attn_input, query_weight).reshape(tokens, HEADS, HEAD_DIM)
    key_raw = dot(attn_input, key_weight).reshape(tokens, KV_HEADS, HEAD_DIM)
    value_raw = dot(attn_input, value_weight).reshape(tokens, KV_HEADS, HEAD_DIM)
    query_rot = rotate(query_raw, cosine, sine_table).astype(BF16)
    key_rot = rotate(key_raw, cosine, sine_table).astype(BF16)
    query_send = query_rot.reshape(tokens, KV_HEADS, 2 * HEAD_DIM).transpose(1, 0, 2)
    kv_send = jnp.concatenate([key_rot, value_raw.astype(BF16)], axis=2).transpose(1, 0, 2)
    kv_all, queries = exchange(
        0, sizes, "send_qkv", (kv_send, SEQ_AXES, pick_context), (query_send, ("context",), pick_target)
    )
    kv_all = kv_all.reshape(-1, 2 * HEAD_DIM)
    mixtures, sums = attention_forward(queries, kv_all, owner)
    (mixture,) = exchange(1, sizes, "send_mixture", (mixtures, ("context",), pick_target))
    mixture_flat = mixture.transpose(1, 0, 2).reshape(tokens, HEADS * HEAD_DIM)

    after_attn = input_float + dot(mixture_flat, output_weight)
    inverse_second, normed_second, moe_input = norm_forward(after_attn, midnorm_gain)
    logits = lax.dot_general(
        router_weight, moe_input, (((0,), (1,)), ((), ())), preferred_element_type=F32
    )
    numbers = jnp.arange(EXPERTS, dtype=jnp.int32)[:, None, None]
    chosen = jnp.any(expert_ids[0].T[None] == numbers, axis=1)
    masked = jnp.where(chosen, logits, -jnp.inf)
    powers = jnp.exp(masked - jnp.max(masked, axis=0, keepdims=True))
    gates = powers / jnp.sum(powers, axis=0, keepdims=True)
    gate_table = jnp.where(chosen, gates, -1.0)

    moe_all, table_all = exchange(
        2, sizes, "send_tokens", (moe_input, ("expert",), pick_whole), (gate_table, ("expert",), pick_whole)
    )
    order = lax.rem(owner - jnp.arange(owners) + owners, owners)
    grad_all = jnp.zeros_like(grad_group).at[order].set(grad_group)
    table = lax.dynamic_slice_in_dim(table_all, owner * mine, mine, axis=1)
    named = table >= 0.0
    before = jnp.triu(jnp.ones((tokens, tokens), BF16), 1)
    slots = jnp.einsum("skt,tu->sku", named.astype(BF16), before, preferred_element_type=F32)
    places = jnp.arange(CAP, dtype=F32)[None, None, :, None]
    pick = named[:, :, None, :] & (slots[:, :, None, :] == places)
    onehot = pick.astype(BF16)
    slot_gates = jnp.sum(jnp.where(pick, table[:, :, None, :], 0.0), axis=3)

    received = jnp.einsum("skct,std->skcd", onehot, moe_all)
    grad_slots = jnp.einsum("skct,std->skcd", onehot, grad_all)

    def product(form, left, right):
        return jnp.einsum(form, left, right, preferred_element_type=F32)

    gate_act = product("secd,edf->secf", received, gate_weight)
    up_act = product("secd,edf->secf", received, up_weight)
    silu_gate = jax.nn.silu(gate_act)
    hidden = (silu_gate * up_act).astype(BF16)
    expert_out = product("secf,efd->secd", hidden, down_weight).astype(BF16)
    grad_expert = (slot_gates[..., None] * grad_slots.astype(F32)).astype(BF16)
    slot_dots = jnp.sum(grad_slots.astype(F32) * expert_out.astype(F32), axis=-1)
    grad_hidden = product("secd,efd->secf", grad_expert, down_weight)
    down_grad = product("secf,secd->efd", hidden, grad_expert)
    sigmoid_gate = jax.nn.sigmoid(gate_act)
    silu_slope = sigmoid_gate * (1.0 + gate_act * (1.0 - sigmoid_gate))
    grad_gate = (grad_hidden * up_act * silu_slope).astype(BF16)
    grad_up = (grad_hidden * silu_gate).astype(BF16)
    gate_grad = product("secd,secf->edf", received, grad_gate)
    up_grad = product("secd,secf->edf", received, grad_up)
    grad_buffer = (
        product("secf,edf->secd", grad_gate, gate_weight)
        + product("secf,edf->secd", grad_up, up_weight)
    ).astype(BF16)

    weights = jnp.where(pick, table[:, :, None, :], 0.0)
    high = weights.astype(BF16)
    low = (weights - high.astype(F32)).astype(BF16)
    moe_terms = (
        product("skct,skcd->std", high, expert_out) + product("skct,skcd->std", low, expert_out)
    ).astype(BF16)
    grad_terms = product("skct,skcd->std", onehot, grad_buffer).astype(BF16)
    dot_terms = jnp.sum(jnp.where(pick, slot_dots[..., None], 0.0), axis=2)
    dot_terms = jnp.concatenate([dot_terms, jnp.zeros_like(dot_terms)], axis=1)
    moe_back, grad_back, dot_back = exchange(
        3,
        sizes,
        "send_results",
        (moe_terms, ("expert",), pick_target),
        (grad_terms, ("expert",), pick_target),
        (dot_terms, ("expert",), pick_target),
    )
    gate_sum, up_sum, down_sum = (
        reduce_experts(gate_grad, sizes),
        reduce_experts(up_grad, sizes),
        reduce_experts(down_grad, sizes),
    )

    outputs = (after_attn + jnp.sum(moe_back.astype(F32), axis=0)).astype(BF16)
    grad_gates = dot_back[:, :mine].reshape(EXPERTS, tokens)
    grad_logits = gates * (grad_gates - jnp.sum(gates * grad_gates, axis=0, keepdims=True))
    router_grad = jnp.einsum(
        "td,et->de", moe_input.astype(F32), grad_logits, precision=lax.Precision.HIGHEST
    )
    grad_moe_in = jnp.sum(grad_back.astype(F32), axis=0) + jnp.einsum(
        "et,de->td", grad_logits, router_weight.astype(F32), precision=lax.Precision.HIGHEST
    )
    grad_out = cotangent[0].astype(F32)
    midnorm_grad, grad_after = norm_backward(grad_moe_in, normed_second, inverse_second, midnorm_gain)
    grad_after = grad_out + grad_after
    grad_after_half = grad_after.astype(BF16)
    output_grad = t_dot(mixture_flat, grad_after_half)
    grad_mix = dot_t(grad_after_half, output_weight).astype(BF16)
    grad_mix = grad_mix.reshape(tokens, KV_HEADS, 2 * HEAD_DIM).transpose(1, 0, 2)
    (grad_mixtures,) = exchange(4, sizes, "send_grad_mixture", (grad_mix, ("context",), pick_target))
    grad_queries, kv_terms = attention_backward(queries, kv_all, mixtures, grad_mixtures, sums, owner)
    kv_terms = kv_terms.astype(BF16).reshape(-1, tokens, 2 * HEAD_DIM)
    kv_back, grad_query = exchange(
        5, sizes, "send_grad_qkv", (kv_terms, SEQ_AXES, pick_target), (grad_queries, ("context",), pick_target)
    )
    grad_kv = jnp.sum(kv_back.astype(F32).reshape(KV_HEADS, owners, tokens, 2 * HEAD_DIM), axis=1)
    grad_kv = grad_kv.transpose(1, 0, 2)
    grad_query = grad_query.transpose(1, 0, 2).reshape(tokens, HEADS, HEAD_DIM)
    query_back = rotate_back(grad_query, cosine, sine_table).reshape(tokens, -1).astype(BF16)
    key_back = rotate_back(grad_kv[..., :HEAD_DIM], cosine, sine_table).reshape(tokens, -1).astype(BF16)
    value_back = grad_kv[..., HEAD_DIM:].reshape(tokens, -1).astype(BF16)
    query_grad = t_dot(attn_input, query_back)
    key_grad = t_dot(attn_input, key_back)
    value_grad = t_dot(attn_input, value_back)
    grad_attn_in = (
        dot_t(query_back, query_weight) + dot_t(key_back, key_weight) + dot_t(value_back, value_weight)
    )
    prenorm_grad, grad_inputs = norm_backward(grad_attn_in, normed_first, inverse_first, prenorm_gain)
    grad_inputs = grad_after + grad_inputs
    dense = lax.psum(
        (prenorm_grad, query_grad, key_grad, value_grad, output_grad, midnorm_grad, router_grad),
        ("dp", "context", "expert"),
    )
    return (outputs[None], grad_inputs[None], *dense, gate_sum, up_sum, down_sum)


def solution(mesh):
    split = P("dp", ("context", "expert"), None)
    owned = P("expert", None, None)
    summed = P("expert", ("dp", "context"), None)
    in_specs = (split, *([P()] * 7), owned, owned, owned, split, split)
    out_specs = (split, split, *([P()] * 7), summed, summed, summed)
    return jax.shard_map(
        functools.partial(local, dict(mesh.shape)),
        mesh=mesh,
        in_specs=in_specs,
        out_specs=out_specs,
        check_vma=False,
    )
```

time: 1260 us -> 560 us (0.44)
  waiting for transfers between devices: 900 us -> 61.7 us
  Pallas kernels: 0 us -> 159 us
  matrix products: 136 us -> 95.5 us
  starting transfers between devices: 21.5 us -> 42.6 us
    reduce_scatter x5 -> x0, waiting for transfers between devices: 585 us -> none  [the longest x1 158 us: local(): lax.psum_scatter(value_terms, ('context', 'expert'), scatter_dimension=0,...]
    pallas_call x0 -> x6, Pallas kernels: none -> 159 us  [exchange(): pl.pallas_call(functools.partial(exchange_body, items, sizes), out_shape=...]
    all_to_all x4 -> x0, waiting for transfers between devices: 132 us -> none  [the longest x1 35.8 us: local(): lax.all_to_all(expert_out.reshape(owners, local_experts * CAP, model_widt...]
    all_gather x2 -> x0, waiting for transfers between devices: 120 us -> none  [the longest x1 61.8 us: local(): lax.all_gather(key_rot, ('context', 'expert'), axis=0, tiled=True)]
    psum x1, waiting for transfers between devices: 62.8 us -> 9.34 us  [local(): lax.psum((prenorm_grad, query_grad, key_grad, value_grad, output_grad, mi...]
    ppermute x0 -> x34, waiting for transfers between devices: none -> 52.3 us  [the longest x25 33.2 us: shift(): lax.ppermute(array, axes, [(i, (i + step) % total) for i in range(total)])]
    ppermute x0 -> x34, starting transfers between devices: none -> 42.5 us  [the longest x25 38.2 us: shift(): lax.ppermute(array, axes, [(i, (i + step) % total) for i in range(total)])]
    dot_general x31 -> x54, matrix products: 136 us -> 95.5 us  [the longest x12 47.6 us: product(): return jnp.einsum(form, left, right, preferred_element_type=F32)]
  transfers between devices with their start and end apart: 12 -> 35, of which waited for: 12 -> 12; matrix products, arithmetic and copies ran while one was open for 12% -> 18% of each run, Pallas kernels for 0% -> 12%
where the time goes in v1:
time: 560 us; the launch traced here: 553 us
  Pallas kernels  159 us (28%)
  matrix products  95.5 us (17%)
  local copies, waits for them, and re-layouts  66.2 us (12%)
  blocking collectives  65.8 us (12%)
  waiting for transfers between devices  61.7 us (11%)
  other arithmetic  46.4 us (8%)
  starting transfers between devices  42.6 us (8%)
  between operations  16.4 us (3%)
    pallas_call x6, Pallas kernels, exchange(): pl.pallas_call(functools.partial(exchange_body, items, sizes), out_shape=...  159 us
    psum x1, blocking collectives, local(): lax.psum((prenorm_grad, query_grad, key_grad, value_grad, output_grad, mi...  65.8 us
    dot_general x12, matrix products, product(): return jnp.einsum(form, left, right, preferred_element_type=F32)  47.6 us
    ppermute x25, starting transfers between devices, shift(): lax.ppermute(array, axes, [(i, (i + step) % total) for i in range(total)])  38.2 us
    ppermute x25, waiting for transfers between devices, shift(): lax.ppermute(array, axes, [(i, (i + step) % total) for i in range(total)])  33.2 us
    unnamed x263, local copies, waits for them, and re-layouts  28.6 us
    dot_general x12, matrix products, t_dot(): lax.dot_general(left, right, (((0,), (0,)), ((), ())), preferred_element_...  19.6 us
    ppermute x9, waiting for transfers between devices, flip(): return lax.ppermute(array, axis, [(i, i ^ bit) for i in range(size)])  19.1 us
  transfers between devices with their start and end apart: 35, of which 12 were waited for; matrix products, arithmetic and copies ran while one was open for 18% of the time, Pallas kernels for 12%

profile of v1, /device:TPU:1, one launch (start us, length us, event | category | flops | bytes accessed | tf_op | source)
XLA Modules:
  0.0 553.4 jit_solution(8128218727140483137)
XLA Ops:
  7.3 6.1 %collective-permute-start.6 = (bf16[128,1024]{1,0:T(8,128)(2,1)}, bf16[128,1024]{1,0:T(8,128)(2,1)}, u32[]{:S(2)}, u32[]{:S(2)}) collective-permute-start(bf16[128,1024]{1,0:T(8,128)(2,1)} %bitcast.453), channel_id=1, source_target_pairs={{0,7},{1,0},{2,1},{3,2},{4,3},{5,4},{6,5},{7,6},{8,15},{9,8},{10,9... | collective-permute-start | bytes 786440 | tf_op jit(solution)/shard_map/ppermute | solution.py:133
  32.9 25.8 %send_qkv.1 = (bf16[32,128,128]{2,1,0:T(8,128)(2,1)}, bf16[4,128,128]{2,1,0:T(8,128)(2,1)}) custom-call(bf16[4,128,128]{2,1,0:T(8,128)(2,1)} %maximum_bitcast_fusion.refs_0_, bf16[4,128,128]{2,1,0:T(8,128)(2,1)} %bitcast.466), custom_call_target="tpu_custom_call" | custom-call | tf_op jit(solution)/shard_map/send_qkv/pallas_call | solution.py:118
  74.5 5.9 %send_mixture.1 = bf16[4,128,128]{2,1,0:T(8,128)(2,1)} custom-call(bf16[4,128,128]{2,1,0:T(8,128)(2,1)} %pad_maximum_fusion.9.refs_0_), custom_call_target="tpu_custom_call" | custom-call | tf_op jit(solution)/shard_map/send_mixture/pallas_call | solution.py:118
  83.7 36.4 %send_tokens.1 = (bf16[8,128,1024]{2,1,0:T(8,128)(2,1)}, f32[8,32,128]{2,1,0:T(8,128)}) custom-call(bf16[128,1024]{1,0:T(8,128)(2,1)} %copy-done.31, f32[32,128]{1,0:T(8,128)} %broadcast_select_fusion.refs_1_), custom_call_target="tpu_custom_call" | custom-call | tf_op jit(solution)/shard_map/send_tokens/pallas_call | solution.py:118
  127.7 4.6 fusion.22
  149.6 4.2 collective-permute-done.3
  168.0 5.9 %fusion.41 = f32[4,512,1024,1]{2,1,3,0:T(8,128)} fusion(bf16[8,4,64,512]{3,2,0,1:T(8,128)(2,1)S(1)} %copy-done.121, bf16[8,4,64,1024]{3,2,0,1:T(8,128)(2,1)S(1)} %get-tuple-element.150, f32[8,4,64]{2,0,1:T(8,128)S(1)} %copy.238), kind=kOutput, calls=%fused_computation.70 | convolution fusion | flops 2153775104 | bytes 14688256 | tf_op jit(solution)/shard_map/secf,secd->efd/dot_general | solution.py:334
  173.9 8.8 %fusion.16 = (bf16[8,4,64,512]{3,2,0,1:T(8,128)(2,1)}, bf16[8,4,64,512]{3,2,0,1:T(8,128)(2,1)S(1)}) fusion(f32[4,8,64,512]{3,2,1,0:T(8,128)} %copy-done.119, f32[4,8,64,512]{3,2,1,0:T(8,128)} %get-tuple-element.148, bf16[4,512,1024]{2,1,0:T(8,128)(2,1)} %param.23, bf16[8,4,64,1024]{3,2,0,1:T(8,128)(2,1)S(1)} %get-tuple-element.150, f32[8,4,64]{2,0,1:T(8,128)S(1)} %copy.238), kind=kOutput, calls=%fused_computation.33 | convolution fusion | flops 2167406592 | bytes 20979712 | tf_op jit(solution)/shard_map/secd,efd->secf/dot_general | solution.py:334
  182.8 5.7 %fusion.64 = f32[4,1024,512,1]{2,1,0,3:T(8,128)} fusion(bf16[8,4,64,1024]{3,2,1,0:T(8,128)(2,1)S(1)} %copy-done.27, bf16[8,4,64,512]{3,2,0,1:T(8,128)(2,1)S(1)} %get-tuple-element.52), kind=kOutput, calls=%fused_computation.96 | convolution fusion | flops 2147483648 | bytes 14680064 | tf_op jit(solution)/shard_map/secd,secf->edf/dot_general | solution.py:334
  190.9 5.7 %fusion.61 = f32[4,1024,512,1]{2,1,0,3:T(8,128)} fusion(bf16[8,4,64,1024]{3,2,1,0:T(8,128)(2,1)S(1)} %copy-done.27, bf16[8,4,64,512]{3,2,0,1:T(8,128)(2,1)S(1)} %copy-done.37), kind=kOutput, calls=%fused_computation.93 | convolution fusion | flops 2147483648 | bytes 14680064 | tf_op jit(solution)/shard_map/secd,secf->edf/dot_general | solution.py:334
  196.6 4.0 fusion.23
  203.6 58.6 %send_results.1 = (bf16[8,128,1024]{2,1,0:T(8,128)(2,1)}, bf16[8,128,1024]{2,1,0:T(8,128)(2,1)}, f32[8,8,128]{2,1,0:T(8,128)}) custom-call(bf16[8,128,1024]{2,1,0:T(8,128)(2,1)} %fusion.21.refs_0_, bf16[8,128,1024]{2,1,0:T(8,128)(2,1)} %bitcast_convert_fusion.refs_1_, f32[8,8,128]{2,1,0:T(8,128)} %concatenate.132.refs_2_), custom_call_target="tpu_custom_call" | custom-call | tf_op jit(solution)/shard_map/send_results/pallas_call | solution.py:118
  273.2 8.1 %send_grad_mixture.1 = bf16[4,128,128]{2,1,0:T(8,128)(2,1)} custom-call(bf16[4,128,128]{2,1,0:T(8,128)(2,1)} %bitcast.469), custom_call_target="tpu_custom_call" | custom-call | tf_op jit(solution)/shard_map/send_grad_mixture/pallas_call | solution.py:118
  302.5 4.0 fusion.6
  314.1 24.1 %send_grad_qkv.1 = (bf16[32,128,128]{2,1,0:T(8,128)(2,1)}, f32[4,128,128]{2,1,0:T(8,128)}) custom-call(bf16[32,128,128]{2,1,0:T(8,128)(2,1)} %pad_maximum_fusion.3.refs_0_, f32[4,128,128]{2,1,0:T(8,128)} %pad_maximum_fusion.7.refs_1_), custom_call_target="tpu_custom_call" | custom-call | tf_op jit(solution)/shard_map/send_grad_qkv/pallas_call | solution.py:118
  372.5 65.8 %all-reduce.7 = (f32[1024]{0:T(1024)}, f32[1024]{0:T(1024)}) all-reduce(f32[1024]{0:T(1024)S(1)} %get-tuple-element.32, f32[1024]{0:T(1024)S(1)} %copy-done.104), channel_id=1, replica_groups=mesh['dp'=4,'context'=4,'expert'=8] {'dp','context','expert'}, use_global_device_ids=true, to_apply=%region_31.32 | all-reduce | flops 2048 | bytes 16384 | tf_op jit(solution)/shard_map/psum | solution.py:415
  459.8 5.3 collective-permute-done.17
  465.2 5.6 %collective-permute-start.10 = (bf16[2,2,64,512]{3,2,0,1:T(8,128)(2,1)S(1)}, bf16[2,2,64,512]{3,2,0,1:T(8,128)(2,1)S(1)}, u32[]{:S(2)}, u32[]{:S(2)}) collective-permute-start(bf16[2,2,64,512]{3,2,0,1:T(8,128)(2,1)S(1)} %get-tuple-element.70), channel_id=1, source_target_pairs={{0,96},{32,0},{64,32},{96,64},{1,97},{33,1},{65,33},{97,65},{2,98}... | collective-permute-start | bytes 786440 | tf_op jit(solution)/shard_map/ppermute | solution.py:133
  471.1 5.3 collective-permute-done.8
  476.4 5.3 collective-permute-done.10
  483.4 13.9 %collective-permute-done.29 = bf16[2,32,1024]{2,1,0:T(8,128)(2,1)S(1)} collective-permute-done((bf16[2,32,1024]{2,1,0:T(8,128)(2,1)S(1)}, bf16[2,32,1024]{2,1,0:T(8,128)(2,1)S(1)}, u32[]{:S(2)}, u32[]{:S(2)}) %collective-permute-start.29) | collective-permute-done | bytes 131104 | tf_op jit(solution)/shard_map/ppermute | solution.py:137
  516.3 4.2 collective-permute-done.23
  522.3 6.7 %collective-permute-done.14 = bf16[2,64,512]{2,1,0:T(8,128)(2,1)S(1)} collective-permute-done((bf16[2,64,512]{2,1,0:T(8,128)(2,1)S(1)}, bf16[2,64,512]{2,1,0:T(8,128)(2,1)S(1)}, u32[]{:S(2)}, u32[]{:S(2)}) %collective-permute-start.14) | collective-permute-done | bytes 131104 | tf_op jit(solution)/shard_map/ppermute | solution.py:133
  529.8 9.3 %all-reduce.11.cloned.1.call-done = (f32[1024,512]{1,0:T(8,128)}, f32[1024,256]{1,0:T(8,128)}, f32[1024,256]{1,0:T(8,128)}, f32[512,1024]{1,0:T(8,128)}, f32[1024,32]{0,1:T(8,128)}) async-done(((f32[1024,512]{1,0:T(8,128)}, f32[1024,256]{1,0:T(8,128)}, f32[1024,256]{1,0:T(8,128)}, f32[512,1024]{1,0:T(8,128)}, f32[1024,32]{0,1:T(8,128)}), (f32[1024,512]{1,0:T(8,128)}, f32[1024,256]{1,0:T(8,128)}, ...) | async-done | bytes 6422544 | tf_op jit(solution)/shard_map/psum | solution.py:415
  (510 shorter events, 207.7 us)
Async XLA Ops:
  7.2 531.9 %all-reduce.11.cloned.1.call-start = ((), (), s32[]{:S(2)}) async-start(), calls=%async_computation | async-start | bytes 12845056 | tf_op jit(solution)/shard_map/psum | solution.py:415
  7.3 150.6 %collective-permute-start.6 = (bf16[128,1024]{1,0:T(8,128)(2,1)}, bf16[128,1024]{1,0:T(8,128)(2,1)}, u32[]{:S(2)}, u32[]{:S(2)}) collective-permute-start(bf16[128,1024]{1,0:T(8,128)(2,1)} %bitcast.453), channel_id=1, source_target_pairs={{0,7},{1,0},{2,1},{3,2},{4,3},{5,4},{6,5},{7,6},{8,15},{9,8},{10,9... | collective-permute-start | bytes 786440 | tf_op jit(solution)/shard_map/ppermute | solution.py:133
  13.4 142.9 %collective-permute-start.5 = (bf16[128,1024]{1,0:T(8,128)(2,1)}, bf16[128,1024]{1,0:T(8,128)(2,1)}, u32[]{:S(2)}, u32[]{:S(2)}) collective-permute-start(bf16[128,1024]{1,0:T(8,128)(2,1)} %bitcast.454), channel_id=1, source_target_pairs={{0,6},{1,7},{2,0},{3,1},{4,2},{5,3},{6,4},{7,5},{8,14},{9,15},{10,... | collective-permute-start | bytes 786440 | tf_op jit(solution)/shard_map/ppermute | solution.py:133
  13.7 140.8 %collective-permute-start.4 = (bf16[128,1024]{1,0:T(8,128)(2,1)}, bf16[128,1024]{1,0:T(8,128)(2,1)}, u32[]{:S(2)}, u32[]{:S(2)}) collective-permute-start(bf16[128,1024]{1,0:T(8,128)(2,1)} %bitcast.455), channel_id=1, source_target_pairs={{0,5},{1,6},{2,7},{3,0},{4,1},{5,2},{6,3},{7,4},{8,13},{9,14},{10,... | collective-permute-start | bytes 786440 | tf_op jit(solution)/shard_map/ppermute | solution.py:133
  14.4 131.4 %collective-permute-start.1 = (bf16[128,1024]{1,0:T(8,128)(2,1)}, bf16[128,1024]{1,0:T(8,128)(2,1)}, u32[]{:S(2)}, u32[]{:S(2)}) collective-permute-start(bf16[128,1024]{1,0:T(8,128)(2,1)} %bitcast.456), channel_id=1, source_target_pairs={{0,2},{1,3},{2,4},{3,5},{4,6},{5,7},{6,0},{7,1},{8,10},{9,11},{10,... | collective-permute-start | bytes 786440 | tf_op jit(solution)/shard_map/ppermute | solution.py:133
  16.3 124.2 %collective-permute-start = (bf16[128,1024]{1,0:T(8,128)(2,1)}, bf16[128,1024]{1,0:T(8,128)(2,1)}, u32[]{:S(2)}, u32[]{:S(2)}) collective-permute-start(bf16[128,1024]{1,0:T(8,128)(2,1)} %bitcast.457), channel_id=1, source_target_pairs={{0,1},{1,2},{2,3},{3,4},{4,5},{5,6},{6,7},{7,0},{8,9},{9,10},{10,1... | collective-permute-start | bytes 786440 | tf_op jit(solution)/shard_map/ppermute | solution.py:133
  346.2 92.1 %collective-permute-start.25 = (bf16[4,4,2,32,1024]{4,3,0,1,2:T(8,128)(2,1)}, bf16[4,4,2,32,1024]{4,3,0,1,2:T(8,128)(2,1)}, u32[]{:S(2)}, u32[]{:S(2)}) collective-permute-start(bf16[4,4,2,32,1024]{4,3,0,1,2:T(8,128)(2,1)} %fusion.53), channel_id=1, source_target_pairs={{0,8},{8,0},{16,24},{24,16},{1,9},{9,1},{17,25},{25,17},{2,10},{10... | collective-permute-start | bytes 6291464 | tf_op jit(solution)/shard_map/ppermute | solution.py:137
  350.4 95.5 %collective-permute-start.16 = (bf16[4,4,2,64,512]{4,3,0,1,2:T(8,128)(2,1)}, bf16[4,4,2,64,512]{4,3,0,1,2:T(8,128)(2,1)}, u32[]{:S(2)}, u32[]{:S(2)}) collective-permute-start(bf16[4,4,2,64,512]{4,3,0,1,2:T(8,128)(2,1)} %fusion.52), channel_id=1, source_target_pairs={{0,8},{8,0},{16,24},{24,16},{1,9},{9,1},{17,25},{25,17},{2,10},{10... | collective-permute-start | bytes 6291464 | tf_op jit(solution)/shard_map/ppermute | solution.py:137
  354.8 96.7 %collective-permute-start.7 = (bf16[4,4,2,64,512]{4,3,0,1,2:T(8,128)(2,1)}, bf16[4,4,2,64,512]{4,3,0,1,2:T(8,128)(2,1)}, u32[]{:S(2)}, u32[]{:S(2)}) collective-permute-start(bf16[4,4,2,64,512]{4,3,0,1,2:T(8,128)(2,1)} %fusion.51), channel_id=1, source_target_pairs={{0,8},{8,0},{16,24},{24,16},{1,9},{9,1},{17,25},{25,17},{2,10},{10... | collective-permute-start | bytes 6291464 | tf_op jit(solution)/shard_map/ppermute | solution.py:137
  442.6 14.1 %collective-permute-start.26 = (bf16[2,2,32,1024]{3,2,0,1:T(8,128)(2,1)S(1)}, bf16[2,2,32,1024]{3,2,0,1:T(8,128)(2,1)S(1)}, u32[]{:S(2)}, u32[]{:S(2)}) collective-permute-start(bf16[2,2,32,1024]{3,2,0,1:T(8,128)(2,1)S(1)} %get-tuple-element.63), channel_id=1, source_target_pairs={{0,32},{32,64},{64,96},{96,0},{1,33},{33,65},{65,97},{97,1},{2,34}... | collective-permute-start | bytes 786440 | tf_op jit(solution)/shard_map/ppermute | solution.py:133
  443.4 14.6 %collective-permute-start.28 = (bf16[2,2,32,1024]{3,2,0,1:T(8,128)(2,1)S(1)}, bf16[2,2,32,1024]{3,2,0,1:T(8,128)(2,1)S(1)}, u32[]{:S(2)}, u32[]{:S(2)}) collective-permute-start(bf16[2,2,32,1024]{3,2,0,1:T(8,128)(2,1)S(1)} %get-tuple-element.64), channel_id=1, source_target_pairs={{0,96},{32,0},{64,32},{96,64},{1,97},{33,1},{65,33},{97,65},{2,98}... | collective-permute-start | bytes 786440 | tf_op jit(solution)/shard_map/ppermute | solution.py:133
  445.3 13.6 %collective-permute-start.27 = (bf16[2,2,32,1024]{3,2,0,1:T(8,128)(2,1)S(1)}, bf16[2,2,32,1024]{3,2,0,1:T(8,128)(2,1)S(1)}, u32[]{:S(2)}, u32[]{:S(2)}) collective-permute-start(bf16[2,2,32,1024]{3,2,0,1:T(8,128)(2,1)S(1)} %get-tuple-element.65), channel_id=1, source_target_pairs={{0,64},{32,96},{64,0},{96,32},{1,65},{33,97},{65,1},{97,33},{2,66}... | collective-permute-start | bytes 786440 | tf_op jit(solution)/shard_map/ppermute | solution.py:133
  450.5 14.5 %collective-permute-start.17 = (bf16[2,2,64,512]{3,2,0,1:T(8,128)(2,1)S(1)}, bf16[2,2,64,512]{3,2,0,1:T(8,128)(2,1)S(1)}, u32[]{:S(2)}, u32[]{:S(2)}) collective-permute-start(bf16[2,2,64,512]{3,2,0,1:T(8,128)(2,1)S(1)} %get-tuple-element.66), channel_id=1, source_target_pairs={{0,32},{32,64},{64,96},{96,0},{1,33},{33,65},{65,97},{97,1},{2,34}... | collective-permute-start | bytes 786440 | tf_op jit(solution)/shard_map/ppermute | solution.py:133
  451.5 13.8 %collective-permute-start.19 = (bf16[2,2,64,512]{3,2,0,1:T(8,128)(2,1)S(1)}, bf16[2,2,64,512]{3,2,0,1:T(8,128)(2,1)S(1)}, u32[]{:S(2)}, u32[]{:S(2)}) collective-permute-start(bf16[2,2,64,512]{3,2,0,1:T(8,128)(2,1)S(1)} %get-tuple-element.67), channel_id=1, source_target_pairs={{0,96},{32,0},{64,32},{96,64},{1,97},{33,1},{65,33},{97,65},{2,98}... | collective-permute-start | bytes 786440 | tf_op jit(solution)/shard_map/ppermute | solution.py:133
  456.7 14.2 %collective-permute-start.18 = (bf16[2,2,64,512]{3,2,0,1:T(8,128)(2,1)S(1)}, bf16[2,2,64,512]{3,2,0,1:T(8,128)(2,1)S(1)}, u32[]{:S(2)}, u32[]{:S(2)}) collective-permute-start(bf16[2,2,64,512]{3,2,0,1:T(8,128)(2,1)S(1)} %get-tuple-element.68), channel_id=1, source_target_pairs={{0,64},{32,96},{64,0},{96,32},{1,65},{33,97},{65,1},{97,33},{2,66}... | collective-permute-start | bytes 786440 | tf_op jit(solution)/shard_map/ppermute | solution.py:133
  458.1 44.8 %collective-permute-start.30 = (bf16[2,4,32,1024]{3,2,0,1:T(8,128)(2,1)S(1)}, bf16[2,4,32,1024]{3,2,0,1:T(8,128)(2,1)S(1)}, u32[]{:S(2)}, u32[]{:S(2)}) collective-permute-start(bf16[2,4,32,1024]{3,2,0,1:T(8,128)(2,1)S(1)} %fusion.100), channel_id=1, source_target_pairs={{0,16},{8,24},{16,0},{24,8},{1,17},{9,25},{17,1},{25,9},{2,18},{10... | collective-permute-start | bytes 1572872 | tf_op jit(solution)/shard_map/ppermute | solution.py:137
  459.0 47.6 %collective-permute-start.21 = (bf16[2,4,64,512]{3,2,0,1:T(8,128)(2,1)S(1)}, bf16[2,4,64,512]{3,2,0,1:T(8,128)(2,1)S(1)}, u32[]{:S(2)}, u32[]{:S(2)}) collective-permute-start(bf16[2,4,64,512]{3,2,0,1:T(8,128)(2,1)S(1)} %fusion.99), channel_id=1, source_target_pairs={{0,16},{8,24},{16,0},{24,8},{1,17},{9,25},{17,1},{25,9},{2,18},{10... | collective-permute-start | bytes 1572872 | tf_op jit(solution)/shard_map/ppermute | solution.py:137
  465.1 11.3 %collective-permute-start.8 = (bf16[2,2,64,512]{3,2,0,1:T(8,128)(2,1)S(1)}, bf16[2,2,64,512]{3,2,0,1:T(8,128)(2,1)S(1)}, u32[]{:S(2)}, u32[]{:S(2)}) collective-permute-start(bf16[2,2,64,512]{3,2,0,1:T(8,128)(2,1)S(1)} %get-tuple-element.69), channel_id=1, source_target_pairs={{0,32},{32,64},{64,96},{96,0},{1,33},{33,65},{65,97},{97,1},{2,34}... | collective-permute-start | bytes 786440 | tf_op jit(solution)/shard_map/ppermute | solution.py:133
  465.2 16.4 %collective-permute-start.10 = (bf16[2,2,64,512]{3,2,0,1:T(8,128)(2,1)S(1)}, bf16[2,2,64,512]{3,2,0,1:T(8,128)(2,1)S(1)}, u32[]{:S(2)}, u32[]{:S(2)}) collective-permute-start(bf16[2,2,64,512]{3,2,0,1:T(8,128)(2,1)S(1)} %get-tuple-element.70), channel_id=1, source_target_pairs={{0,96},{32,0},{64,32},{96,64},{1,97},{33,1},{65,33},{97,65},{2,98}... | collective-permute-start | bytes 786440 | tf_op jit(solution)/shard_map/ppermute | solution.py:133
  476.4 30.6 %collective-permute-start.12 = (bf16[2,4,64,512]{3,2,0,1:T(8,128)(2,1)S(1)}, bf16[2,4,64,512]{3,2,0,1:T(8,128)(2,1)S(1)}, u32[]{:S(2)}, u32[]{:S(2)}) collective-permute-start(bf16[2,4,64,512]{3,2,0,1:T(8,128)(2,1)S(1)} %fusion.98), channel_id=1, source_target_pairs={{0,16},{8,24},{16,0},{24,8},{1,17},{9,25},{17,1},{25,9},{2,18},{10... | collective-permute-start | bytes 1572872 | tf_op jit(solution)/shard_map/ppermute | solution.py:137
  481.7 15.5 %collective-permute-start.29 = (bf16[2,32,1024]{2,1,0:T(8,128)(2,1)S(1)}, bf16[2,32,1024]{2,1,0:T(8,128)(2,1)S(1)}, u32[]{:S(2)}, u32[]{:S(2)}) collective-permute-start(bf16[2,32,1024]{2,1,0:T(8,128)(2,1)S(1)} %fusion.161), channel_id=1, source_target_pairs={{0,16},{8,24},{16,0},{24,8},{1,17},{9,25},{17,1},{25,9},{2,18},{10... | collective-permute-start | bytes 393224 | tf_op jit(solution)/shard_map/ppermute | solution.py:137
  481.7 18.4 %collective-permute-start.20 = (bf16[2,64,512]{2,1,0:T(8,128)(2,1)S(1)}, bf16[2,64,512]{2,1,0:T(8,128)(2,1)S(1)}, u32[]{:S(2)}, u32[]{:S(2)}) collective-permute-start(bf16[2,64,512]{2,1,0:T(8,128)(2,1)S(1)} %fusion.157), channel_id=1, source_target_pairs={{0,16},{8,24},{16,0},{24,8},{1,17},{9,25},{17,1},{25,9},{2,18},{10... | collective-permute-start | bytes 393224 | tf_op jit(solution)/shard_map/ppermute | solution.py:137
  511.0 11.3 %collective-permute-start.13 = (bf16[2,64,512]{2,1,0:T(8,128)(2,1)S(1)}, bf16[2,64,512]{2,1,0:T(8,128)(2,1)S(1)}, u32[]{:S(2)}, u32[]{:S(2)}) collective-permute-start(bf16[2,64,512]{2,1,0:T(8,128)(2,1)S(1)} %get-tuple-element.80), channel_id=1, source_target_pairs={{0,32},{32,64},{64,96},{96,0},{1,33},{33,65},{65,97},{97,1},{2,34}... | collective-permute-start | bytes 393224 | tf_op jit(solution)/shard_map/ppermute | solution.py:133
  515.2 13.7 %collective-permute-start.14 = (bf16[2,64,512]{2,1,0:T(8,128)(2,1)S(1)}, bf16[2,64,512]{2,1,0:T(8,128)(2,1)S(1)}, u32[]{:S(2)}, u32[]{:S(2)}) collective-permute-start(bf16[2,64,512]{2,1,0:T(8,128)(2,1)S(1)} %get-tuple-element.82), channel_id=1, source_target_pairs={{0,64},{32,96},{64,0},{96,32},{1,65},{33,97},{65,1},{97,33},{2,66}... | collective-permute-start | bytes 393224 | tf_op jit(solution)/shard_map/ppermute | solution.py:133
  (135 other events, 1089.2 us)
Sparse Core Ops, SparseCore 0:
  372.0 167.1 all-reduce.10

commit v2 on v1

--- a/solution.py
+++ b/solution.py
@@ -137,6 +137,320 @@
     return lax.ppermute(array, axis, [(i, i ^ bit) for i in range(size)])
 
 
+def moe_copies(sizes, refs):
+    d_send, d_back, dots, dot_back, g_sends, g_backs, sems = refs
+    owners = sizes["expert"]
+    owner, context = lax.axis_index("expert"), lax.axis_index("context")
+
+    def results(step):
+        target = lax.rem(owner + step, owners)
+        pairs = ((d_send, d_back, sems[0], sems[1]), (dots, dot_back, sems[2], sems[3]))
+        return [
+            pltpu.make_async_remote_copy(
+                src_ref=src.at[target],
+                dst_ref=dst.at[owner],
+                send_sem=send.at[step],
+                recv_sem=recv.at[step],
+                device_id={"expert": target},
+                device_id_type=MESH_ID,
+            )
+            for src, dst, send, recv in pairs
+        ]
+
+    def own_results():
+        return [
+            pltpu.make_async_copy(d_send.at[owner], d_back.at[owner], sems[0].at[0]),
+            pltpu.make_async_copy(dots.at[owner], dot_back.at[owner], sems[2].at[0]),
+        ]
+
+    def halves(number):
+        partner = context + 1 - 2 * lax.rem(context, 2)
+        return [
+            pltpu.make_async_remote_copy(
+                src_ref=g_sends[i].at[number],
+                dst_ref=g_backs[i].at[number],
+                send_sem=sems[4].at[3 * number + i],
+                recv_sem=sems[5].at[3 * number + i],
+                device_id={"context": partner},
+                device_id_type=MESH_ID,
+            )
+            for i in range(3)
+        ]
+
+    return results, own_results, halves
+
+
+def moe_body(
+    sizes,
+    moe_ref,
+    grad_ref,
+    table_ref,
+    wg_ref,
+    wu_ref,
+    wd_ref,
+    own_g,
+    own_u,
+    own_d,
+    back_g,
+    back_u,
+    back_d,
+    y_out,
+    d_back,
+    dot_back,
+    x_all,
+    g_now,
+    deo_all,
+    dgu_all,
+    eh_all,
+    eo_all,
+    dbuf_all,
+    picks,
+    highs,
+    lows,
+    gate_col,
+    dot_col,
+    dots,
+    y_send,
+    d_send,
+    send_g,
+    send_u,
+    send_d,
+    *sems,
+):
+    step = pl.program_id(0)
+    owners = sizes["expert"]
+    owner, context = lax.axis_index("expert"), lax.axis_index("context")
+    core = lax.rem(context, 2)
+    mine = 4
+    tokens, width = moe_ref.shape[1:]
+    hidden_width = wg_ref.shape[2]
+    rows = owners * CAP
+    tile = rows // 2
+    barrier = pltpu.get_barrier_semaphore()
+    results, own_results, halves = moe_copies(
+        sizes, (d_send, d_back, dots, dot_back, (send_g, send_u, send_d), (back_g, back_u, back_d), sems)
+    )
+
+    @pl.when(step == 0)
+    def _():
+        for shift_by in range(1, owners):
+            pl.semaphore_signal(
+                barrier,
+                inc=1,
+                device_id={"expert": lax.rem(owner + shift_by, owners)},
+                device_id_type=MESH_ID,
+            )
+        pl.semaphore_signal(
+            barrier, inc=1, device_id={"context": context + 1 - 2 * core}, device_id_type=MESH_ID
+        )
+        dots[...] = jnp.zeros_like(dots)
+
+    @pl.when(step == 4)
+    def _():
+        pl.semaphore_wait(barrier, owners)
+        for shift_by in range(1, owners):
+            for copy in results(shift_by):
+                copy.start()
+        for copy in own_results():
+            copy.start()
+        pltpu.make_async_copy(y_send, y_out, sems[6].at[0]).start()
+
+    for number in range(mine):
+
+        @pl.when(step == 5 + number)
+        def _(number=number):
+            for copy in halves(number):
+                copy.start()
+
+    @pl.when(step < mine)
+    def _():
+        place = pl.multiple_of(step * CAP, CAP)
+        table = jnp.concatenate(
+            [table_ref[s, pl.ds(owner * mine + step, 1), :] for s in range(owners)], axis=0
+        )
+        named = table >= 0.0
+        above = lax.broadcasted_iota(jnp.int32, (tokens, tokens), 0)
+        beside = lax.broadcasted_iota(jnp.int32, (tokens, tokens), 1)
+        before = (above < beside).astype(F32).astype(BF16)
+        slots = dot(named.astype(F32).astype(BF16), before)
+        slots = jnp.where(named, slots, -1.0)
+        counts = lax.broadcasted_iota(jnp.int32, (CAP, tokens), 0).astype(F32)
+        for s in range(owners):
+            chosen = counts == slots[s : s + 1]
+            onehot = jnp.where(chosen, 1.0, 0.0).astype(BF16)
+            weight = jnp.where(chosen, table[s : s + 1], 0.0)
+            high = weight.astype(BF16)
+            picks[s, pl.ds(place, CAP), :] = onehot
+            highs[s, pl.ds(place, CAP), :] = high
+            lows[s, pl.ds(place, CAP), :] = (weight - high.astype(F32)).astype(BF16)
+            gate_col[s * CAP : (s + 1) * CAP, :] = jnp.sum(weight, axis=1, keepdims=True)
+            x_all[step, s * CAP : (s + 1) * CAP, :] = dot(onehot, moe_ref[s]).astype(BF16)
+            g_now[s * CAP : (s + 1) * CAP, :] = dot(onehot, grad_ref[s]).astype(BF16)
+
+        def run_tile(r, carry):
+            here = pl.ds(pl.multiple_of(r * tile, tile), tile)
+            part = pl.ds(r * (owners // 2), owners // 2)
+            spot = pl.ds(place, CAP)
+            rows_in = x_all[step, here, :]
+            gate_act = dot(rows_in, wg_ref[0])
+            up_act = dot(rows_in, wu_ref[0])
+            sigma = jax.nn.sigmoid(gate_act)
+            silu = gate_act * sigma
+            hidden = (silu * up_act).astype(BF16)
+            eh_all[step, here, :] = hidden
+            expert_out = dot(hidden, wd_ref[0]).astype(BF16)
+            eo_all[part, spot, :] = expert_out.reshape(owners // 2, CAP, width)
+            grads = g_now[here, :].astype(F32)
+            dot_col[here, :] = jnp.sum(grads * expert_out.astype(F32), axis=1, keepdims=True)
+            grad_expert = (gate_col[here, :] * grads).astype(BF16)
+            deo_all[step, here, :] = grad_expert
+            grad_hidden = dot_t(grad_expert, wd_ref[0])
+            slope = sigma * (1.0 + gate_act * (1.0 - sigma))
+            grad_gate = (grad_hidden * up_act * slope).astype(BF16)
+            grad_up = (grad_hidden * silu).astype(BF16)
+            dgu_all[step, here, :hidden_width] = grad_gate
+            dgu_all[step, here, hidden_width:] = grad_up
+            grad_buffer = (dot_t(grad_gate, wg_ref[0]) + dot_t(grad_up, wu_ref[0])).astype(BF16)
+            dbuf_all[part, spot, :] = grad_buffer.reshape(owners // 2, CAP, width)
+            return carry
+
+        lax.fori_loop(0, 2, run_tile, 0)
+        for s in range(owners):
+            onehot = picks[s, pl.ds(place, CAP), :].astype(F32)
+            line = jnp.sum(onehot * dot_col[s * CAP : (s + 1) * CAP, :], axis=0, keepdims=True)
+            dots[s, pl.ds(step, 1), :] = line
+
+    @pl.when(step == mine - 1)
+    def _():
+        def combine(s, carry):
+            moved = t_dot(highs[s], eo_all[s]) + t_dot(lows[s], eo_all[s])
+            y_send[s] = moved.astype(BF16)
+            d_send[s] = t_dot(picks[s], dbuf_all[s]).astype(BF16)
+            return carry
+
+        lax.fori_loop(0, owners, combine, 0)
+
+    @pl.when((step >= mine) & (step < 2 * mine))
+    def _():
+        number = step - mine
+        blocks = width // 256
+        per = width // 16
+
+        def gate_rows(j, carry):
+            columns = pl.ds(pl.multiple_of(j * 256, 256), 256)
+            rows_in = x_all[number, :, columns]
+            for half, own, send in ((0, own_g, send_g), (1, own_u, send_u)):
+                grads = dgu_all[number, :, half * hidden_width : (half + 1) * hidden_width]
+                terms = t_dot(rows_in, grads).reshape(128 // per, 2, per, hidden_width)
+                first, second = terms[:, 0], terms[:, 1]
+                group = pl.ds(j * (128 // per), 128 // per)
+                own[0, group] = jnp.where(core == 0, first, second)
+                send[number, group] = jnp.where(core == 0, second, first).astype(BF16)
+            return carry
+
+        lax.fori_loop(0, blocks, gate_rows, 0)
+        less = hidden_width // 16
+
+        def down_rows(j, carry):
+            columns = pl.ds(pl.multiple_of(j * 256, 256), 256)
+            terms = t_dot(eh_all[number, :, columns], deo_all[number])
+            terms = terms.reshape(128 // less, 2, less, width)
+            first, second = terms[:, 0], terms[:, 1]
+            group = pl.ds(j * (128 // less), 128 // less)
+            own_d[0, group] = jnp.where(core == 0, first, second)
+            send_d[number, group] = jnp.where(core == 0, second, first).astype(BF16)
+            return carry
+
+        lax.fori_loop(0, hidden_width // 256, down_rows, 0)
+
+    @pl.when(step == 2 * mine)
+    def _():
+        for shift_by in range(1, owners):
+            for copy in results(shift_by):
+                copy.wait()
+        for copy in own_results():
+            copy.wait()
+        pltpu.make_async_copy(y_send, y_out, sems[6].at[0]).wait()
+        for number in range(mine):
+            for copy in halves(number):
+                copy.wait()
+
+
+def run_experts(cid, sizes, moe_all, grad_all, table_all, gate_weight, up_weight, down_weight):
+    owners, tokens, width = moe_all.shape
+    mine, _, inner = gate_weight.shape
+    rows = owners * CAP
+    part, less = width // 16, inner // 16
+
+    def fixed(array):
+        return pl.BlockSpec(array.shape, lambda i: (0, 0, 0), pipeline_mode=pl.Buffered(1))
+
+    def expert_block(array):
+        return pl.BlockSpec((1, *array.shape[1:]), lambda i: (jnp.minimum(i, mine - 1), 0, 0))
+
+    def own_block(*shape):
+        return pl.BlockSpec((1, *shape), lambda i: (jnp.clip(i - mine, 0, mine - 1), 0, 0, 0))
+
+    anywhere = pl.BlockSpec(memory_space=pl.ANY)
+    wide, tall = (8, part, inner), (8, less, width)
+    dma = pltpu.SemaphoreType.DMA
+    return pl.pallas_call(
+        functools.partial(moe_body, sizes),
+        grid=(2 * mine + 1,),
+        out_shape=[
+            jax.ShapeDtypeStruct((mine, *wide), F32),
+            jax.ShapeDtypeStruct((mine, *wide), F32),
+            jax.ShapeDtypeStruct((mine, *tall), F32),
+            jax.ShapeDtypeStruct((mine, *wide), BF16),
+            jax.ShapeDtypeStruct((mine, *wide), BF16),
+            jax.ShapeDtypeStruct((mine, *tall), BF16),
+            jax.ShapeDtypeStruct((owners, tokens, width), BF16),
+            jax.ShapeDtypeStruct((owners, tokens, width), BF16),
+            jax.ShapeDtypeStruct((owners, 8, tokens), F32),
+        ],
+        in_specs=[
+            fixed(moe_all),
+            fixed(grad_all),
+            fixed(table_all),
+            expert_block(gate_weight),
+            expert_block(up_weight),
+            expert_block(down_weight),
+        ],
+        out_specs=[own_block(*wide), own_block(*wide), own_block(*tall), *([anywhere] * 6)],
+        scratch_shapes=[
+            pltpu.VMEM((mine, rows, width), BF16),
+            pltpu.VMEM((rows, width), BF16),
+            pltpu.VMEM((mine, rows, width), BF16),
+            pltpu.VMEM((mine, rows, 2 * inner), BF16),
+            pltpu.VMEM((mine, rows, inner), BF16),
+            pltpu.VMEM((owners, mine * CAP, width), BF16),
+            pltpu.VMEM((owners, mine * CAP, width), BF16),
+            pltpu.VMEM((owners, mine * CAP, tokens), BF16),
+            pltpu.VMEM((owners, mine * CAP, tokens), BF16),
+            pltpu.VMEM((owners, mine * CAP, tokens), BF16),
+            pltpu.VMEM((rows, 1), F32),
+            pltpu.VMEM((rows, 1), F32),
+            pltpu.VMEM((owners, 8, tokens), F32),
+            pltpu.VMEM((owners, tokens, width), BF16),
+            pltpu.VMEM((owners, tokens, width), BF16),
+            pltpu.VMEM((mine, *wide), BF16),
+            pltpu.VMEM((mine, *wide), BF16),
+            pltpu.VMEM((mine, *tall), BF16),
+            dma((owners,)),
+            dma((owners,)),
+            dma((owners,)),
+            dma((owners,)),
+            dma((3 * mine,)),
+            dma((3 * mine,)),
+            dma((1,)),
+        ],
+        name="run_experts",
+        compiler_params=pltpu.CompilerParams(
+            collective_id=cid, has_side_effects=True, vmem_limit_bytes=67_043_328
+        ),
+    )(moe_all, grad_all, table_all, gate_weight, up_weight, down_weight)
+
+
 def rope_tables(positions, head_size):
     half_dim = head_size // 2
     frequency = ROPE_BASE ** (-2.0 * jnp.arange(half_dim, dtype=F32) / head_size)
@@ -227,18 +541,13 @@
     return jnp.stack(grad_queries), jnp.concatenate([key_terms, value_terms], axis=1)
 
 
-def reduce_experts(grads, sizes):
-    dp, context = lax.axis_index("dp"), lax.axis_index("context")
-    core, side = lax.rem(context, 2), context // 2
-    experts, rows, columns = grads.shape
-    part = rows // 16
-    grads = grads.reshape(experts, 4, 2, 2, part, columns)
+def reduce_experts(own, other, sizes):
+    dp, side = lax.axis_index("dp"), lax.axis_index("context") // 2
+    experts, _, part, columns = own.shape
+    held = (own + other.astype(F32)).reshape(experts, 4, 2, part, columns)
 
     def take(array, index, axis):
         return lax.dynamic_index_in_dim(array, index, axis, keepdims=False)
-
-    other = flip(take(grads, 1 - core, 3).astype(BF16), "context", 4, 1)
-    held = take(grads, core, 3) + other.astype(F32)
 
     def over_dp(array):
         total = take(array, dp, 1)
@@ -281,9 +590,6 @@
     positions = block * tokens + jnp.arange(tokens, dtype=jnp.int32)
     cosine, sine_table = rope_tables(positions, HEAD_DIM)
 
-    sent = [shift(cotangent[0], ("expert",), sizes, step) for step in range(1, owners)]
-    grad_group = jnp.stack([cotangent[0]] + sent)
-
     input_float = inputs[0].astype(F32)
     inverse_first, normed_first, attn_input = norm_forward(input_float, prenorm_gain)
     query_raw = dot(attn_input, query_weight).reshape(tokens, HEADS, HEAD_DIM)
@@ -293,8 +599,13 @@
     key_rot = rotate(key_raw, cosine, sine_table).astype(BF16)
     query_send = query_rot.reshape(tokens, KV_HEADS, 2 * HEAD_DIM).transpose(1, 0, 2)
     kv_send = jnp.concatenate([key_rot, value_raw.astype(BF16)], axis=2).transpose(1, 0, 2)
-    kv_all, queries = exchange(
-        0, sizes, "send_qkv", (kv_send, SEQ_AXES, pick_context), (query_send, ("context",), pick_target)
+    kv_all, queries, grad_all = exchange(
+        0,
+        sizes,
+        "send_qkv",
+        (kv_send, SEQ_AXES, pick_context),
+        (query_send, ("context",), pick_target),
+        (cotangent[0], ("expert",), pick_whole),
     )
     kv_all = kv_all.reshape(-1, 2 * HEAD_DIM)
     mixtures, sums = attention_forward(queries, kv_all, owner)
@@ -316,64 +627,14 @@
     moe_all, table_all = exchange(
         2, sizes, "send_tokens", (moe_input, ("expert",), pick_whole), (gate_table, ("expert",), pick_whole)
     )
-    order = lax.rem(owner - jnp.arange(owners) + owners, owners)
-    grad_all = jnp.zeros_like(grad_group).at[order].set(grad_group)
-    table = lax.dynamic_slice_in_dim(table_all, owner * mine, mine, axis=1)
-    named = table >= 0.0
-    before = jnp.triu(jnp.ones((tokens, tokens), BF16), 1)
-    slots = jnp.einsum("skt,tu->sku", named.astype(BF16), before, preferred_element_type=F32)
-    places = jnp.arange(CAP, dtype=F32)[None, None, :, None]
-    pick = named[:, :, None, :] & (slots[:, :, None, :] == places)
-    onehot = pick.astype(BF16)
-    slot_gates = jnp.sum(jnp.where(pick, table[:, :, None, :], 0.0), axis=3)
-
-    received = jnp.einsum("skct,std->skcd", onehot, moe_all)
-    grad_slots = jnp.einsum("skct,std->skcd", onehot, grad_all)
-
-    def product(form, left, right):
-        return jnp.einsum(form, left, right, preferred_element_type=F32)
-
-    gate_act = product("secd,edf->secf", received, gate_weight)
-    up_act = product("secd,edf->secf", received, up_weight)
-    silu_gate = jax.nn.silu(gate_act)
-    hidden = (silu_gate * up_act).astype(BF16)
-    expert_out = product("secf,efd->secd", hidden, down_weight).astype(BF16)
-    grad_expert = (slot_gates[..., None] * grad_slots.astype(F32)).astype(BF16)
-    slot_dots = jnp.sum(grad_slots.astype(F32) * expert_out.astype(F32), axis=-1)
-    grad_hidden = product("secd,efd->secf", grad_expert, down_weight)
-    down_grad = product("secf,secd->efd", hidden, grad_expert)
-    sigmoid_gate = jax.nn.sigmoid(gate_act)
-    silu_slope = sigmoid_gate * (1.0 + gate_act * (1.0 - sigmoid_gate))
-    grad_gate = (grad_hidden * up_act * silu_slope).astype(BF16)
-    grad_up = (grad_hidden * silu_gate).astype(BF16)
-    gate_grad = product("secd,secf->edf", received, grad_gate)
-    up_grad = product("secd,secf->edf", received, grad_up)
-    grad_buffer = (
-        product("secf,edf->secd", grad_gate, gate_weight)
-        + product("secf,edf->secd", grad_up, up_weight)
-    ).astype(BF16)
-
-    weights = jnp.where(pick, table[:, :, None, :], 0.0)
-    high = weights.astype(BF16)
-    low = (weights - high.astype(F32)).astype(BF16)
-    moe_terms = (
-        product("skct,skcd->std", high, expert_out) + product("skct,skcd->std", low, expert_out)
-    ).astype(BF16)
-    grad_terms = product("skct,skcd->std", onehot, grad_buffer).astype(BF16)
-    dot_terms = jnp.sum(jnp.where(pick, slot_dots[..., None], 0.0), axis=2)
-    dot_terms = jnp.concatenate([dot_terms, jnp.zeros_like(dot_terms)], axis=1)
-    moe_back, grad_back, dot_back = exchange(
-        3,
-        sizes,
-        "send_results",
-        (moe_terms, ("expert",), pick_target),
-        (grad_terms, ("expert",), pick_target),
-        (dot_terms, ("expert",), pick_target),
-    )
+    own_g, own_u, own_d, other_g, other_u, other_d, moe_terms, grad_back, dot_back = run_experts(
+        3, sizes, moe_all, grad_all, table_all, gate_weight, up_weight, down_weight
+    )
+    (moe_back,) = exchange(6, sizes, "send_outputs", (moe_terms, ("expert",), pick_target))
     gate_sum, up_sum, down_sum = (
-        reduce_experts(gate_grad, sizes),
-        reduce_experts(up_grad, sizes),
-        reduce_experts(down_grad, sizes),
+        reduce_experts(own_g, other_g, sizes),
+        reduce_experts(own_u, other_u, sizes),
+        reduce_experts(own_d, other_d, sizes),
     )
 
     outputs = (after_attn + jnp.sum(moe_back.astype(F32), axis=0)).astype(BF16)
@@ -412,9 +673,18 @@
     )
     prenorm_grad, grad_inputs = norm_backward(grad_attn_in, normed_first, inverse_first, prenorm_gain)
     grad_inputs = grad_after + grad_inputs
-    dense = lax.psum(
-        (prenorm_grad, query_grad, key_grad, value_grad, output_grad, midnorm_grad, router_grad),
-        ("dp", "context", "expert"),
+    narrow = jnp.concatenate([router_grad, prenorm_grad[:, None], midnorm_grad[:, None]], axis=1)
+    query_grad, key_grad, value_grad, output_grad, narrow = lax.psum(
+        (query_grad, key_grad, value_grad, output_grad, narrow), ("dp", "context", "expert")
+    )
+    dense = (
+        narrow[:, EXPERTS],
+        query_grad,
+        key_grad,
+        value_grad,
+        output_grad,
+        narrow[:, EXPERTS + 1],
+        narrow[:, :EXPERTS],
     )
     return (outputs[None], grad_inputs[None], *dense, gate_sum, up_sum, down_sum)
 

time: 560 us -> 522 us (0.932)
  blocking collectives: 65.8 us -> 0 us
  Pallas kernels: 159 us -> 224 us
  matrix products: 95.5 us -> 32.2 us
  waiting for transfers between devices: 61.7 us -> 123 us
  local copies, waits for them, and re-layouts: 66.2 us -> 50.3 us
  starting transfers between devices: 42.6 us -> 29.2 us
  other arithmetic: 46.4 us -> 36.7 us
    psum x1, waiting for transfers between devices: 9.34 us -> 78.9 us  [local(): lax.psum((query_grad, key_grad, value_grad, output_grad, narrow), ('dp',...]
    psum x1 -> x0, blocking collectives: 65.8 us -> none  [local(): lax.psum((prenorm_grad, query_grad, key_grad, value_grad, output_grad, mi...]
    pallas_call x0 -> x1, Pallas kernels: none -> 59 us  [run_experts(): pl.pallas_call(functools.partial(moe_body, sizes), grid=(2 * mine + 1,),...]
    dot_general x15 -> x0, matrix products: 54.6 us -> none  [the longest x12 47.6 us: product(): return jnp.einsum(form, left, right, preferred_element_type=F32)]
    ppermute x25 -> x18, starting transfers between devices: 38.2 us -> 23.1 us  [shift(): lax.ppermute(array, axes, [(i, (i + step) % total) for i in range(total)])]
    ppermute x25 -> x18, waiting for transfers between devices: 33.2 us -> 19.7 us  [shift(): lax.ppermute(array, axes, [(i, (i + step) % total) for i in range(total)])]
    convert_element_type x3 -> x0, local copies, waits for them, and re-layouts: 11.5 us -> none  [reduce_experts(): other = flip(take(grads, 1 - core, 3).astype(BF16), 'context', 4, 1)]
    pallas_call x6, Pallas kernels: 159 us -> 165 us  [exchange(): pl.pallas_call(functools.partial(exchange_body, items, sizes), out_shape=...]
  transfers between devices with their start and end apart: 35 -> 25, of which waited for: 12 -> 12; matrix products, arithmetic and copies ran while one was open for 18% -> 14% of each run, Pallas kernels for 12% -> 13%
where the time goes in v2:
time: 522 us; the launch traced here: 512 us
  Pallas kernels  224 us (43%)
  waiting for transfers between devices  123 us (24%)
  local copies, waits for them, and re-layouts  50.3 us (10%)
  other arithmetic  36.7 us (7%)
  matrix products  32.2 us (6%)
  starting transfers between devices  29.2 us (6%)
  between operations  16.5 us (3%)
    pallas_call x6, Pallas kernels, exchange(): pl.pallas_call(functools.partial(exchange_body, items, sizes), out_shape=...  165 us
    psum x1, waiting for transfers between devices, local(): lax.psum((query_grad, key_grad, value_grad, output_grad, narrow), ('dp',...  78.9 us
    pallas_call x1, Pallas kernels, run_experts(): pl.pallas_call(functools.partial(moe_body, sizes), grid=(2 * mine + 1,),...  59 us
    ppermute x6, waiting for transfers between devices, flip(): return lax.ppermute(array, axis, [(i, i ^ bit) for i in range(size)])  24.8 us
    ppermute x18, starting transfers between devices, shift(): lax.ppermute(array, axes, [(i, (i + step) % total) for i in range(total)])  23.1 us
    unnamed x250, local copies, waits for them, and re-layouts  22.5 us
    ppermute x18, waiting for transfers between devices, shift(): lax.ppermute(array, axes, [(i, (i + step) % total) for i in range(total)])  19.7 us
    dot_general x12, matrix products, t_dot(): lax.dot_general(left, right, (((0,), (0,)), ((), ())), preferred_element_...  15.6 us
  transfers between devices with their start and end apart: 25, of which 12 were waited for; matrix products, arithmetic and copies ran while one was open for 14% of the time, Pallas kernels for 13%

profile of v2, /device:TPU:1, one launch (start us, length us, event | category | flops | bytes accessed | tf_op | source)
XLA Modules:
  0.0 512.2 jit_solution(15431191247294372147)
XLA Ops:
  15.6 49.6 %send_qkv.1 = (bf16[32,128,128]{2,1,0:T(8,128)(2,1)}, bf16[4,128,128]{2,1,0:T(8,128)(2,1)}, bf16[8,128,1024]{2,1,0:T(8,128)(2,1)}) custom-call(bf16[4,128,128]{2,1,0:T(8,128)(2,1)} %maximum_bitcast_fusion.refs_0_, bf16[4,128,128]{2,1,0:T(8,128)(2,1)} %bitcast.322, bf16[128,1024]{1,0:T(8,128)(2,1)} %bitcast.312), custom_call_target="tpu_custom_call" | custom-call | tf_op jit(solution)/shard_map/send_qkv/pallas_call | solution.py:118
  79.8 7.3 %send_mixture.1 = bf16[4,128,128]{2,1,0:T(8,128)(2,1)} custom-call(bf16[4,128,128]{2,1,0:T(8,128)(2,1)} %pad_maximum_fusion.10.refs_0_), custom_call_target="tpu_custom_call" | custom-call | tf_op jit(solution)/shard_map/send_mixture/pallas_call | solution.py:118
  90.4 40.2 %send_tokens.1 = (bf16[8,128,1024]{2,1,0:T(8,128)(2,1)}, f32[8,32,128]{2,1,0:T(8,128)}) custom-call(bf16[128,1024]{1,0:T(8,128)(2,1)} %copy-done.35, f32[32,128]{1,0:T(8,128)} %broadcast_select_fusion.refs_1_), custom_call_target="tpu_custom_call" | custom-call | tf_op jit(solution)/shard_map/send_tokens/pallas_call | solution.py:118
  130.6 59.0 %run_experts.1 = (f32[4,8,64,512]{3,2,1,0:T(8,128)}, f32[4,8,64,512]{3,2,1,0:T(8,128)}, f32[4,8,32,1024]{3,2,1,0:T(8,128)}, bf16[4,8,64,512]{3,2,1,0:T(8,128)(2,...) custom-call(bf16[8,128,1024]{2,1,0:T(8,128)(2,1)} %get-tuple-element, ...), custom_call_target="tpu_custom_call" | custom-call | tf_op jit(solution)/shard_map/run_experts/pallas_call | solution.py:397
  189.6 3.6 convert_add_fusion
  198.4 3.0 collective-permute-start.17
  203.0 3.0 convert_add_fusion.1
  212.9 36.1 %send_outputs.1 = bf16[8,128,1024]{2,1,0:T(8,128)(2,1)} custom-call(bf16[8,128,1024]{2,1,0:T(8,128)(2,1)} %get-tuple-element.33.refs_0_), custom_call_target="tpu_custom_call" | custom-call | tf_op jit(solution)/shard_map/send_outputs/pallas_call | solution.py:118
  249.1 2.2 convert_reduce_fusion.1
  256.6 8.5 %send_grad_mixture.1 = bf16[4,128,128]{2,1,0:T(8,128)(2,1)} custom-call(bf16[4,128,128]{2,1,0:T(8,128)(2,1)} %bitcast.321), custom_call_target="tpu_custom_call" | custom-call | tf_op jit(solution)/shard_map/send_grad_mixture/pallas_call | solution.py:118
  282.1 2.4 copy.169
  284.4 3.4 fusion.4
  293.0 23.2 %send_grad_qkv.1 = (bf16[32,128,128]{2,1,0:T(8,128)(2,1)}, f32[4,128,128]{2,1,0:T(8,128)}) custom-call(bf16[32,128,128]{2,1,0:T(8,128)(2,1)} %pad_maximum_fusion.3.refs_0_, f32[4,128,128]{2,1,0:T(8,128)} %pad_maximum_fusion.7.refs_1_), custom_call_target="tpu_custom_call" | custom-call | tf_op jit(solution)/shard_map/send_grad_qkv/pallas_call | solution.py:118
  326.9 2.9 convert_add_fusion.2
  329.8 2.7 fusion.147
  347.2 2.9 collective-permute-start.1
  352.2 5.4 %collective-permute-done = bf16[2,2,64,512]{3,2,0,1:T(8,128)(2,1)S(1)} collective-permute-done((bf16[2,2,64,512]{3,2,0,1:T(8,128)(2,1)}, bf16[2,2,64,512]{3,2,0,1:T(8,128)(2,1)S(1)}, u32[]{:S(2)}, u32[]{:S(2)}) %collective-permute-start) | collective-permute-done | bytes 262176 | tf_op jit(solution)/shard_map/ppermute | solution.py:133
  359.6 6.9 %collective-permute-done.1 = bf16[2,2,64,512]{3,2,0,1:T(8,128)(2,1)S(1)} collective-permute-done((bf16[2,2,64,512]{3,2,0,1:T(8,128)(2,1)}, bf16[2,2,64,512]{3,2,0,1:T(8,128)(2,1)S(1)}, u32[]{:S(2)}, u32[]{:S(2)}) %collective-permute-start.1) | collective-permute-done | bytes 262176 | tf_op jit(solution)/shard_map/ppermute | solution.py:133
  369.2 21.0 %collective-permute-done.19 = bf16[2,32,1024]{2,1,0:T(8,128)(2,1)S(1)} collective-permute-done((bf16[2,32,1024]{2,1,0:T(8,128)(2,1)S(1)}, bf16[2,32,1024]{2,1,0:T(8,128)(2,1)S(1)}, u32[]{:S(2)}, u32[]{:S(2)}) %collective-permute-start.19) | collective-permute-done | bytes 131104 | tf_op jit(solution)/shard_map/ppermute | solution.py:137
  391.0 2.1 collective-permute-done.11
  396.3 2.7 collective-permute-start.22
  413.1 2.5 collective-permute-done.6
  416.5 78.9 %all-reduce.9.cloned.1.call-done = (f32[1024,34]{0,1:T(8,128)}, f32[1024,512]{1,0:T(8,128)}, f32[1024,256]{1,0:T(8,128)}, f32[1024,256]{1,0:T(8,128)}, f32[512,1024]{1,0:T(8,128)}) async-done(((f32[1024,34]{0,1:T(8,128)}, f32[1024,512]{1,0:T(8,128)}, f32[1024,256]{1,0:T(8,128)}, f32[1024,256]{1,0:T(8,128)}, f32[512,1024]{1,0:T(8,128)}), (f32[1024,34]{0,1:T(8,128)}, f32[1024,512]{1,0:T(8,128)}, ...) | async-done | bytes 6430736 | tf_op jit(solution)/shard_map/psum | solution.py:677
  498.4 3.2 copy.274
  (452 shorter events, 123.2 us)
Async XLA Ops:
  7.2 488.2 %all-reduce.9.cloned.1.call-start = ((), (), s32[]{:S(2)}) async-start(), calls=%async_computation | async-start | bytes 12910592 | tf_op jit(solution)/shard_map/psum | solution.py:677
  195.8 142.2 %collective-permute-start.16 = (bf16[2,2,32,1024]{3,2,0,1:T(8,128)(2,1)}, bf16[2,2,32,1024]{3,2,0,1:T(8,128)(2,1)}, u32[]{:S(2)}, u32[]{:S(2)}) collective-permute-start(bf16[2,2,32,1024]{3,2,0,1:T(8,128)(2,1)} %bitcast.271), channel_id=1, source_target_pairs={{0,32},{32,64},{64,96},{96,0},{1,33},{33,65},{65,97},{97,1},{2,34}... | collective-permute-start | bytes 786440 | tf_op jit(solution)/shard_map/ppermute | solution.py:133
  198.4 144.7 %collective-permute-start.17 = (bf16[2,2,32,1024]{3,2,0,1:T(8,128)(2,1)}, bf16[2,2,32,1024]{3,2,0,1:T(8,128)(2,1)}, u32[]{:S(2)}, u32[]{:S(2)}) collective-permute-start(bf16[2,2,32,1024]{3,2,0,1:T(8,128)(2,1)} %bitcast.272), channel_id=1, source_target_pairs={{0,64},{32,96},{64,0},{96,32},{1,65},{33,97},{65,1},{97,33},{2,66}... | collective-permute-start | bytes 786440 | tf_op jit(solution)/shard_map/ppermute | solution.py:133
  202.1 142.7 %collective-permute-start.18 = (bf16[2,2,32,1024]{3,2,0,1:T(8,128)(2,1)}, bf16[2,2,32,1024]{3,2,0,1:T(8,128)(2,1)}, u32[]{:S(2)}, u32[]{:S(2)}) collective-permute-start(bf16[2,2,32,1024]{3,2,0,1:T(8,128)(2,1)} %bitcast.273), channel_id=1, source_target_pairs={{0,96},{32,0},{64,32},{96,64},{1,97},{33,1},{65,33},{97,65},{2,98}... | collective-permute-start | bytes 786440 | tf_op jit(solution)/shard_map/ppermute | solution.py:133
  210.7 135.7 %collective-permute-start.10 = (bf16[2,2,64,512]{3,2,0,1:T(8,128)(2,1)}, bf16[2,2,64,512]{3,2,0,1:T(8,128)(2,1)}, u32[]{:S(2)}, u32[]{:S(2)}) collective-permute-start(bf16[2,2,64,512]{3,2,0,1:T(8,128)(2,1)} %bitcast.270), channel_id=1, source_target_pairs={{0,96},{32,0},{64,32},{96,64},{1,97},{33,1},{65,33},{97,65},{2,98}... | collective-permute-start | bytes 786440 | tf_op jit(solution)/shard_map/ppermute | solution.py:133
  211.4 135.7 %collective-permute-start.8 = (bf16[2,2,64,512]{3,2,0,1:T(8,128)(2,1)}, bf16[2,2,64,512]{3,2,0,1:T(8,128)(2,1)}, u32[]{:S(2)}, u32[]{:S(2)}) collective-permute-start(bf16[2,2,64,512]{3,2,0,1:T(8,128)(2,1)} %bitcast.268), channel_id=1, source_target_pairs={{0,32},{32,64},{64,96},{96,0},{1,33},{33,65},{65,97},{97,1},{2,34}... | collective-permute-start | bytes 786440 | tf_op jit(solution)/shard_map/ppermute | solution.py:133
  338.0 12.1 %collective-permute-start.9 = (bf16[2,2,64,512]{3,2,0,1:T(8,128)(2,1)}, bf16[2,2,64,512]{3,2,0,1:T(8,128)(2,1)}, u32[]{:S(2)}, u32[]{:S(2)}) collective-permute-start(bf16[2,2,64,512]{3,2,0,1:T(8,128)(2,1)} %bitcast.269), channel_id=1, source_target_pairs={{0,64},{32,96},{64,0},{96,32},{1,65},{33,97},{65,1},{97,33},{2,66}... | collective-permute-start | bytes 786440 | tf_op jit(solution)/shard_map/ppermute | solution.py:133
  343.1 51.8 %collective-permute-start.20 = (bf16[2,4,32,1024]{3,2,0,1:T(8,128)(2,1)}, bf16[2,4,32,1024]{3,2,0,1:T(8,128)(2,1)S(1)}, u32[]{:S(2)}, u32[]{:S(2)}) collective-permute-start(bf16[2,4,32,1024]{3,2,0,1:T(8,128)(2,1)} %fusion.42), channel_id=1, source_target_pairs={{0,16},{8,24},{16,0},{24,8},{1,17},{9,25},{17,1},{25,9},{2,18},{10... | collective-permute-start | bytes 1572872 | tf_op jit(solution)/shard_map/ppermute | solution.py:137
  344.8 55.1 %collective-permute-start.12 = (bf16[2,4,64,512]{3,2,0,1:T(8,128)(2,1)S(1)}, bf16[2,4,64,512]{3,2,0,1:T(8,128)(2,1)S(1)}, u32[]{:S(2)}, u32[]{:S(2)}) collective-permute-start(bf16[2,4,64,512]{3,2,0,1:T(8,128)(2,1)S(1)} %fusion.41), channel_id=1, source_target_pairs={{0,16},{8,24},{16,0},{24,8},{1,17},{9,25},{17,1},{25,9},{2,18},{10... | collective-permute-start | bytes 1572872 | tf_op jit(solution)/shard_map/ppermute | solution.py:137
  346.4 11.2 %collective-permute-start = (bf16[2,2,64,512]{3,2,0,1:T(8,128)(2,1)}, bf16[2,2,64,512]{3,2,0,1:T(8,128)(2,1)S(1)}, u32[]{:S(2)}, u32[]{:S(2)}) collective-permute-start(bf16[2,2,64,512]{3,2,0,1:T(8,128)(2,1)} %bitcast.330), channel_id=1, source_target_pairs={{0,32},{32,64},{64,96},{96,0},{1,33},{33,65},{65,97},{97,1},{2,34}... | collective-permute-start | bytes 786440 | tf_op jit(solution)/shard_map/ppermute | solution.py:133
  347.2 19.3 %collective-permute-start.1 = (bf16[2,2,64,512]{3,2,0,1:T(8,128)(2,1)}, bf16[2,2,64,512]{3,2,0,1:T(8,128)(2,1)S(1)}, u32[]{:S(2)}, u32[]{:S(2)}) collective-permute-start(bf16[2,2,64,512]{3,2,0,1:T(8,128)(2,1)} %bitcast.329), channel_id=1, source_target_pairs={{0,64},{32,96},{64,0},{96,32},{1,65},{33,97},{65,1},{97,33},{2,66}... | collective-permute-start | bytes 786440 | tf_op jit(solution)/shard_map/ppermute | solution.py:133
  350.1 17.6 %collective-permute-start.2 = (bf16[2,2,64,512]{3,2,0,1:T(8,128)(2,1)}, bf16[2,2,64,512]{3,2,0,1:T(8,128)(2,1)S(1)}, u32[]{:S(2)}, u32[]{:S(2)}) collective-permute-start(bf16[2,2,64,512]{3,2,0,1:T(8,128)(2,1)} %bitcast.328), channel_id=1, source_target_pairs={{0,96},{32,0},{64,32},{96,64},{1,97},{33,1},{65,33},{97,65},{2,98}... | collective-permute-start | bytes 786440 | tf_op jit(solution)/shard_map/ppermute | solution.py:133
  357.6 43.2 %collective-permute-start.4 = (bf16[2,4,64,512]{3,2,0,1:T(8,128)(2,1)S(1)}, bf16[2,4,64,512]{3,2,0,1:T(8,128)(2,1)S(1)}, u32[]{:S(2)}, u32[]{:S(2)}) collective-permute-start(bf16[2,4,64,512]{3,2,0,1:T(8,128)(2,1)S(1)} %copy-done.60), channel_id=1, source_target_pairs={{0,16},{8,24},{16,0},{24,8},{1,17},{9,25},{17,1},{25,9},{2,18},{10... | collective-permute-start | bytes 1572872 | tf_op jit(solution)/shard_map/ppermute | solution.py:137
  366.5 23.7 %collective-permute-start.19 = (bf16[2,32,1024]{2,1,0:T(8,128)(2,1)S(1)}, bf16[2,32,1024]{2,1,0:T(8,128)(2,1)S(1)}, u32[]{:S(2)}, u32[]{:S(2)}) collective-permute-start(bf16[2,32,1024]{2,1,0:T(8,128)(2,1)S(1)} %fusion.98), channel_id=1, source_target_pairs={{0,16},{8,24},{16,0},{24,8},{1,17},{9,25},{17,1},{25,9},{2,18},{10... | collective-permute-start | bytes 393224 | tf_op jit(solution)/shard_map/ppermute | solution.py:137
  367.6 25.4 %collective-permute-start.11 = (bf16[2,64,512]{2,1,0:T(8,128)(2,1)S(1)}, bf16[2,64,512]{2,1,0:T(8,128)(2,1)S(1)}, u32[]{:S(2)}, u32[]{:S(2)}) collective-permute-start(bf16[2,64,512]{2,1,0:T(8,128)(2,1)S(1)} %fusion.94), channel_id=1, source_target_pairs={{0,16},{8,24},{16,0},{24,8},{1,17},{9,25},{17,1},{25,9},{2,18},{10... | collective-permute-start | bytes 393224 | tf_op jit(solution)/shard_map/ppermute | solution.py:137
  395.2 6.5 %collective-permute-start.21 = (bf16[2,32,1024]{2,1,0:T(8,128)(2,1)S(1)}, bf16[2,32,1024]{2,1,0:T(8,128)(2,1)S(1)}, u32[]{:S(2)}, u32[]{:S(2)}) collective-permute-start(bf16[2,32,1024]{2,1,0:T(8,128)(2,1)S(1)} %get-tuple-element.80), channel_id=1, source_target_pairs={{0,32},{32,64},{64,96},{96,0},{1,33},{33,65},{65,97},{97,1},{2,34}... | collective-permute-start | bytes 393224 | tf_op jit(solution)/shard_map/ppermute | solution.py:133
  396.3 7.5 %collective-permute-start.22 = (bf16[2,32,1024]{2,1,0:T(8,128)(2,1)S(1)}, bf16[2,32,1024]{2,1,0:T(8,128)(2,1)S(1)}, u32[]{:S(2)}, u32[]{:S(2)}) collective-permute-start(bf16[2,32,1024]{2,1,0:T(8,128)(2,1)S(1)} %get-tuple-element.82), channel_id=1, source_target_pairs={{0,64},{32,96},{64,0},{96,32},{1,65},{33,97},{65,1},{97,33},{2,66}... | collective-permute-start | bytes 393224 | tf_op jit(solution)/shard_map/ppermute | solution.py:133
  399.0 4.9 collective-permute-start.23
  400.2 7.0 %collective-permute-start.13 = (bf16[2,64,512]{2,1,0:T(8,128)(2,1)S(1)}, bf16[2,64,512]{2,1,0:T(8,128)(2,1)S(1)}, u32[]{:S(2)}, u32[]{:S(2)}) collective-permute-start(bf16[2,64,512]{2,1,0:T(8,128)(2,1)S(1)} %get-tuple-element.83), channel_id=1, source_target_pairs={{0,32},{32,64},{64,96},{96,0},{1,33},{33,65},{65,97},{97,1},{2,34}... | collective-permute-start | bytes 393224 | tf_op jit(solution)/shard_map/ppermute | solution.py:133
  400.8 9.0 %collective-permute-start.14 = (bf16[2,64,512]{2,1,0:T(8,128)(2,1)S(1)}, bf16[2,64,512]{2,1,0:T(8,128)(2,1)S(1)}, u32[]{:S(2)}, u32[]{:S(2)}) collective-permute-start(bf16[2,64,512]{2,1,0:T(8,128)(2,1)S(1)} %get-tuple-element.85), channel_id=1, source_target_pairs={{0,64},{32,96},{64,0},{96,32},{1,65},{33,97},{65,1},{97,33},{2,66}... | collective-permute-start | bytes 393224 | tf_op jit(solution)/shard_map/ppermute | solution.py:133
  401.7 8.5 %collective-permute-start.15 = (bf16[2,64,512]{2,1,0:T(8,128)(2,1)S(1)}, bf16[2,64,512]{2,1,0:T(8,128)(2,1)S(1)}, u32[]{:S(2)}, u32[]{:S(2)}) collective-permute-start(bf16[2,64,512]{2,1,0:T(8,128)(2,1)S(1)} %get-tuple-element.84), channel_id=1, source_target_pairs={{0,96},{32,0},{64,32},{96,64},{1,97},{33,1},{65,33},{97,65},{2,98}... | collective-permute-start | bytes 393224 | tf_op jit(solution)/shard_map/ppermute | solution.py:133
  403.9 9.2 %collective-permute-start.5 = (bf16[2,64,512]{2,1,0:T(8,128)(2,1)S(1)}, bf16[2,64,512]{2,1,0:T(8,128)(2,1)S(1)}, u32[]{:S(2)}, u32[]{:S(2)}) collective-permute-start(bf16[2,64,512]{2,1,0:T(8,128)(2,1)S(1)} %get-tuple-element.86), channel_id=1, source_target_pairs={{0,32},{32,64},{64,96},{96,0},{1,33},{33,65},{65,97},{97,1},{2,34}... | collective-permute-start | bytes 393224 | tf_op jit(solution)/shard_map/ppermute | solution.py:133
  403.9 11.7 %collective-permute-start.6 = (bf16[2,64,512]{2,1,0:T(8,128)(2,1)S(1)}, bf16[2,64,512]{2,1,0:T(8,128)(2,1)S(1)}, u32[]{:S(2)}, u32[]{:S(2)}) collective-permute-start(bf16[2,64,512]{2,1,0:T(8,128)(2,1)S(1)} %get-tuple-element.88), channel_id=1, source_target_pairs={{0,64},{32,96},{64,0},{96,32},{1,65},{33,97},{65,1},{97,33},{2,66}... | collective-permute-start | bytes 393224 | tf_op jit(solution)/shard_map/ppermute | solution.py:133
  407.2 8.4 %collective-permute-start.7 = (bf16[2,64,512]{2,1,0:T(8,128)(2,1)S(1)}, bf16[2,64,512]{2,1,0:T(8,128)(2,1)S(1)}, u32[]{:S(2)}, u32[]{:S(2)}) collective-permute-start(bf16[2,64,512]{2,1,0:T(8,128)(2,1)S(1)} %get-tuple-element.87), channel_id=1, source_target_pairs={{0,96},{32,0},{64,32},{96,64},{1,97},{33,1},{65,33},{97,65},{2,98}... | collective-permute-start | bytes 393224 | tf_op jit(solution)/shard_map/ppermute | solution.py:133
  (118 other events, 713.3 us)
Sparse Core Ops, SparseCore 0:
  325.5 169.8 all-reduce.8

commit v3 on v2

--- a/solution.py
+++ b/solution.py
@@ -19,6 +19,7 @@
 BF16 = jnp.bfloat16
 MESH_ID = pl.DeviceIdType.MESH
 SEQ_AXES = ("context", "expert")
+EVERY = ("dp", "context", "expert")
 
 
 def dot(left, right):
@@ -31,43 +32,76 @@
 
 def t_dot(left, right):
     return lax.dot_general(left, right, (((0,), (0,)), ((), ())), preferred_element_type=F32)
+
+
+def axis_size(sizes, name):
+    return 2 if name == "side" else sizes[name]
+
+
+def group_size(axes, sizes):
+    total = 1
+    for name in axes:
+        total *= axis_size(sizes, name)
+    return total
+
+
+def own_index(axes, sizes):
+    index = 0
+    for name in axes:
+        own = lax.axis_index("context") // 2 if name == "side" else lax.axis_index(name)
+        index = index * axis_size(sizes, name) + own
+    return index
 
 
 def coords_of(axes, sizes, index):
     out = {}
     for name in reversed(axes):
-        out[name] = lax.rem(index, sizes[name])
-        index = index // sizes[name]
+        place = lax.rem(index, axis_size(sizes, name))
+        if name == "side":
+            out["context"] = place * 2 + lax.rem(lax.axis_index("context"), 2)
+        else:
+            out[name] = place
+        index = index // axis_size(sizes, name)
     return out
 
 
-def exchange_body(items, sizes, *refs):
+def pick_whole(ref, target, peer):
+    return ref
+
+
+def pick_target(ref, target, peer):
+    return ref.at[target]
+
+
+def pick_context(ref, target, peer):
+    return ref.at[peer["context"]]
+
+
+def exchange_body(items, sizes, compute, more_ins, more_outs, *refs):
     count = len(items)
-    ins, outs, sems = refs[:count], refs[count : 2 * count], refs[2 * count :]
-    widest = max((item[0] for item in items), key=len)
-
-    def own_index(axes):
-        index = 0
-        for name in axes:
-            index = index * sizes[name] + lax.axis_index(name)
-        return index
-
-    def group_size(axes):
-        total = 1
-        for name in axes:
-            total *= sizes[name]
-        return total
+    ins, refs = refs[:count], refs[count:]
+    data_ins, refs = refs[:more_ins], refs[more_ins:]
+    outs, refs = refs[:count], refs[count:]
+    data_outs, refs = refs[:more_outs], refs[more_outs:]
+    sems, scratch = refs[: 2 * count], refs[2 * count :]
 
     barrier = pltpu.get_barrier_semaphore()
-    me, total = own_index(widest), group_size(widest)
-    for step in range(1, total):
-        peer = coords_of(widest, sizes, lax.rem(me + step, total))
-        pl.semaphore_signal(barrier, inc=1, device_id=peer, device_id_type=MESH_ID)
-    pl.semaphore_wait(barrier, total - 1)
+    groups = []
+    for axes, _, _ in items:
+        if not any(set(axes) <= set(other) for other in groups):
+            groups = [other for other in groups if not set(other) <= set(axes)] + [axes]
+    signals = 0
+    for axes in groups:
+        me, total = own_index(axes, sizes), group_size(axes, sizes)
+        for step in range(1, total):
+            peer = coords_of(axes, sizes, lax.rem(me + step, total))
+            pl.semaphore_signal(barrier, inc=1, device_id=peer, device_id_type=MESH_ID)
+        signals += total - 1
+    pl.semaphore_wait(barrier, signals)
 
     waits = []
-    for number, (axes, pick) in enumerate(items):
-        me, total = own_index(axes), group_size(axes)
+    for number, (axes, pick, keep) in enumerate(items):
+        me, total = own_index(axes, sizes), group_size(axes, sizes)
         send, recv = sems[2 * number], sems[2 * number + 1]
         for step in range(1, total):
             target = lax.rem(me + step, total)
@@ -82,59 +116,140 @@
             )
             copy.start()
             waits.append(copy)
-        own = pltpu.make_async_copy(
-            pick(ins[number], me, coords_of(axes, sizes, me)), outs[number].at[me], send.at[0]
-        )
-        own.start()
-        waits.append(own)
+        if keep:
+            own = pltpu.make_async_copy(
+                pick(ins[number], me, coords_of(axes, sizes, me)), outs[number].at[me], send.at[0]
+            )
+            own.start()
+            waits.append(own)
+    if compute is not None:
+        compute(data_ins, data_outs, scratch)
     for copy in waits:
         copy.wait()
 
 
-def pick_whole(ref, target, peer):
-    return ref
-
-
-def pick_target(ref, target, peer):
-    return ref.at[target]
-
-
-def pick_context(ref, target, peer):
-    return ref.at[peer["context"]]
-
-
-def exchange(cid, sizes, name, *specs):
-    arrays = [spec[0] for spec in specs]
-    items = [(spec[1], spec[2]) for spec in specs]
-    shapes, scratch = [], []
-    for array, axes, pick in specs:
-        total = 1
-        for axis in axes:
-            total *= sizes[axis]
+def exchange(cid, sizes, name, *specs, compute=None, data=(), results=(), scratch=(), cost=None):
+    vmem, hbm = pl.BlockSpec(memory_space=pltpu.VMEM), pl.BlockSpec(memory_space=pl.ANY)
+    items, shapes, spaces, sems = [], [], [], []
+    for array, axes, pick, *large in specs:
+        total = group_size(axes, sizes)
         chunk = array.shape if pick is pick_whole else array.shape[1:]
         shapes.append(jax.ShapeDtypeStruct((total, *chunk), array.dtype))
-        scratch += [pltpu.SemaphoreType.DMA((total,)), pltpu.SemaphoreType.DMA((total,))]
-    space = pl.BlockSpec(memory_space=pltpu.VMEM)
+        spaces.append(hbm if large else vmem)
+        items.append((axes, pick, not large))
+        sems += [pltpu.SemaphoreType.DMA((total,)), pltpu.SemaphoreType.DMA((total,))]
     return pl.pallas_call(
-        functools.partial(exchange_body, items, sizes),
-        out_shape=shapes,
-        in_specs=[space] * len(specs),
-        out_specs=[space] * len(specs),
-        scratch_shapes=scratch,
+        functools.partial(exchange_body, items, sizes, compute, len(data), len(results)),
+        out_shape=[*shapes, *results],
+        in_specs=[*spaces, *([vmem] * len(data))],
+        out_specs=[*spaces, *([vmem] * len(results))],
+        scratch_shapes=[*sems, *scratch],
         name=name,
-        compiler_params=pltpu.CompilerParams(collective_id=cid, has_side_effects=True),
-    )(*arrays)
-
-
-def shift(array, axes, sizes, step):
-    total = 1
-    for name in axes:
-        total *= sizes[name]
-    return lax.ppermute(array, axes, [(i, (i + step) % total) for i in range(total)])
-
-
-def flip(array, axis, size, bit):
-    return lax.ppermute(array, axis, [(i, i ^ bit) for i in range(size)])
+        compiler_params=pltpu.CompilerParams(
+            collective_id=cid, has_side_effects=True, vmem_limit_bytes=60_000_000
+        ),
+    )(*[spec[0] for spec in specs], *data)
+
+
+def stack_heads(block, low):
+    tokens = block.shape[0]
+    zero = jnp.zeros((tokens, HEAD_DIM), block.dtype)
+    parts = [block[:, :HEAD_DIM], block[:, HEAD_DIM:]]
+    return jnp.concatenate(
+        [jnp.concatenate([part, zero] if low else [zero, part], axis=1) for part in parts], axis=0
+    )
+
+
+def causal(shape, tokens):
+    keys = lax.broadcasted_iota(jnp.int32, shape, 0)
+    queries = lax.rem(lax.broadcasted_iota(jnp.int32, shape, 1), tokens)
+    return keys - queries <= lax.axis_index("expert") * tokens
+
+
+def identity(size):
+    shape = (size, size)
+    return lax.broadcasted_iota(jnp.int32, shape, 0) == lax.broadcasted_iota(jnp.int32, shape, 1)
+
+
+def attention_forward(data, results, scratch):
+    query_ref, kv_ref = data
+    out_ref, sum_ref = results
+    (score_ref,) = scratch
+    blocks, tokens = query_ref.shape[:2]
+    chunk, columns = 8 * tokens, 2 * tokens
+
+    def block(number, carry):
+        rows = stack_heads(query_ref[number], True) * (HEAD_DIM ** (-0.5))
+        rows = rows.astype(BF16)
+
+        def keys_of(j):
+            return pl.ds(pl.multiple_of(j * chunk, chunk), chunk)
+
+        def first(j, top):
+            scores = dot_t(kv_ref[keys_of(j), :], rows)
+            score_ref[keys_of(j), :] = scores
+            return jnp.maximum(top, jnp.max(scores, axis=0, keepdims=True))
+
+        top = lax.fori_loop(0, number, first, jnp.full((1, columns), -jnp.inf, F32))
+        scores = dot_t(kv_ref[keys_of(number), :], rows)
+        scores = jnp.where(causal(scores.shape, tokens), scores, -jnp.inf)
+        score_ref[keys_of(number), :] = scores
+        top = jnp.maximum(top, jnp.max(scores, axis=0, keepdims=True))
+
+        def second(j, held):
+            total, mixed = held
+            powers = jnp.exp(score_ref[keys_of(j), :] - top)
+            total = total + jnp.sum(powers, axis=0, keepdims=True)
+            return total, mixed + t_dot(powers.astype(BF16), kv_ref[keys_of(j), :])
+
+        start = (jnp.zeros((1, columns), F32), jnp.zeros((columns, 2 * HEAD_DIM), F32))
+        total, mixed = lax.fori_loop(0, number + 1, second, start)
+        sum_ref[number] = top + jnp.log(total)
+        inverse = jnp.sum(jnp.where(identity(columns), 1.0 / total, 0.0), axis=1, keepdims=True)
+        mixed = (mixed * inverse)[:, HEAD_DIM:]
+        out_ref[number] = jnp.concatenate([mixed[:tokens], mixed[tokens:]], axis=1).astype(BF16)
+        return carry
+
+    lax.fori_loop(0, blocks, block, 0)
+
+
+def attention_backward(data, results, scratch):
+    query_ref, kv_ref, mix_ref, grad_ref, sum_ref = data
+    grad_query_ref, terms_ref = results
+    (sum_kv,) = scratch
+    blocks, tokens = query_ref.shape[:2]
+    chunk, columns = 8 * tokens, 2 * tokens
+    factor = HEAD_DIM ** (-0.5)
+    sum_kv[...] = jnp.zeros_like(sum_kv)
+
+    def block(number, carry):
+        rows = (stack_heads(query_ref[number], True) * factor).astype(BF16)
+        grads = stack_heads(grad_ref[number], False)
+        both = jnp.concatenate([rows, grads], axis=0)
+        pairs = dot_t(stack_heads(mix_ref[number], False), grads)
+        delta = jnp.sum(jnp.where(identity(columns), pairs, 0.0), axis=0, keepdims=True)
+        logsum = sum_ref[number]
+
+        def unit(j, total, masked):
+            keys = pl.ds(pl.multiple_of(j * chunk, chunk), chunk)
+            kv = kv_ref[keys, :]
+            products = dot_t(kv, both)
+            soft = jnp.exp(products[:, :columns] - logsum)
+            if masked:
+                soft = jnp.where(causal(soft.shape, tokens), soft, 0.0)
+            scores = (soft * (products[:, columns:] - delta)).astype(BF16)
+            sum_kv[keys, :] += dot(jnp.concatenate([scores, soft.astype(BF16)], axis=1), both)
+            return total + t_dot(scores, kv)
+
+        total = lax.fori_loop(
+            0, number, lambda j, held: unit(j, held, False), jnp.zeros((columns, 2 * HEAD_DIM), F32)
+        )
+        total = unit(number, total, True)[:, :HEAD_DIM] * factor
+        grad_query_ref[number] = jnp.concatenate([total[:tokens], total[tokens:]], axis=1)
+        return carry
+
+    lax.fori_loop(0, blocks, block, 0)
+    terms_ref[...] = sum_kv[...].astype(BF16)
 
 
 def moe_copies(sizes, refs):
@@ -485,85 +600,13 @@
     return (gain_grad, inverse * (scaled - normed * inner))
 
 
-def stack_heads(block):
-    return jnp.concatenate([block[:, :HEAD_DIM], block[:, HEAD_DIM:]], axis=0)
-
-
-def side_heads(rows):
-    half = rows.shape[0] // 2
-    return jnp.concatenate([rows[:half], rows[half:]], axis=1)
-
-
-def chunk_scores(rows, keys, number, offset):
-    tokens = rows.shape[0] // 2
-    scores = dot_t(rows, keys) * (HEAD_DIM ** (-0.5))
-    last = scores[:, number * 8 * tokens :]
-    row_pos = offset * tokens + lax.rem(lax.broadcasted_iota(jnp.int32, last.shape, 0), tokens)
-    key_pos = lax.broadcasted_iota(jnp.int32, last.shape, 1)
-    last = jnp.where(key_pos <= row_pos, last, -jnp.inf)
-    return jnp.concatenate([scores[:, : number * 8 * tokens], last], axis=1)
-
-
-def attention_forward(queries, kv_all, offset):
-    blocks, tokens = queries.shape[:2]
-    outs, sums = [], []
-    for number in range(blocks):
-        width = (number + 1) * 8 * tokens
-        rows = stack_heads(queries[number])
-        scores = chunk_scores(rows, kv_all[:width, :HEAD_DIM], number, offset)
-        maximum = jnp.max(scores, axis=-1, keepdims=True)
-        logsum = maximum + jnp.log(jnp.sum(jnp.exp(scores - maximum), axis=-1, keepdims=True))
-        soft = jnp.exp(scores - logsum).astype(BF16)
-        outs.append(side_heads(dot(soft, kv_all[:width, HEAD_DIM:]).astype(BF16)))
-        sums.append(logsum)
-    return jnp.stack(outs), sums
-
-
-def attention_backward(queries, kv_all, mixtures, grad_mix, sums, offset):
-    blocks, tokens = queries.shape[:2]
-    factor = HEAD_DIM ** (-0.5)
-    grad_queries, key_terms, value_terms = [], 0.0, 0.0
-    for number in range(blocks):
-        width = (number + 1) * 8 * tokens
-        rows = stack_heads(queries[number])
-        grads = stack_heads(grad_mix[number])
-        mixed = stack_heads(mixtures[number])
-        keys, values = kv_all[:width, :HEAD_DIM], kv_all[:width, HEAD_DIM:]
-        delta = jnp.sum(grads.astype(F32) * mixed.astype(F32), axis=-1, keepdims=True)
-        soft = jnp.exp(chunk_scores(rows, keys, number, offset) - sums[number])
-        grad_soft = dot_t(grads, values)
-        grad_score = (soft * (grad_soft - delta)).astype(BF16)
-        soft_round = soft.astype(BF16)
-        grad_queries.append(side_heads(dot(grad_score, keys) * factor))
-        pad = ((0, blocks * 8 * tokens - width), (0, 0))
-        key_terms = key_terms + jnp.pad(t_dot(grad_score, rows) * factor, pad)
-        value_terms = value_terms + jnp.pad(t_dot(soft_round, grads), pad)
-    return jnp.stack(grad_queries), jnp.concatenate([key_terms, value_terms], axis=1)
-
-
-def reduce_experts(own, other, sizes):
-    dp, side = lax.axis_index("dp"), lax.axis_index("context") // 2
-    experts, _, part, columns = own.shape
-    held = (own + other.astype(F32)).reshape(experts, 4, 2, part, columns)
-
-    def take(array, index, axis):
-        return lax.dynamic_index_in_dim(array, index, axis, keepdims=False)
-
-    def over_dp(array):
-        total = take(array, dp, 1)
-        for step in range(1, 4):
-            sent = take(array, lax.rem(dp + step, 4), 1).astype(BF16)
-            total = total + shift(sent, ("dp",), sizes, step).astype(F32)
-        return total
-
-    def over_side(array, axis):
-        sent = take(array, 1 - side, axis).astype(BF16)
-        return take(array, side, axis) + flip(sent, "context", 4, 2).astype(F32)
-
-    half = experts // 2
-    first = over_side(over_dp(held[:half]), 1)
-    second = over_dp(over_side(held[half:], 2))
-    return jnp.concatenate([first, second], axis=0)
+def sum_others(received, own, index):
+    numbers = jnp.arange(received.shape[0]).reshape(-1, *([1] * own.ndim))
+    return own + jnp.sum(jnp.where(numbers == index, 0.0, received.astype(F32)), axis=0)
+
+
+def own_part(array, index):
+    return lax.dynamic_index_in_dim(array, index, 0, keepdims=False)
 
 
 def local(
@@ -599,16 +642,24 @@
     key_rot = rotate(key_raw, cosine, sine_table).astype(BF16)
     query_send = query_rot.reshape(tokens, KV_HEADS, 2 * HEAD_DIM).transpose(1, 0, 2)
     kv_send = jnp.concatenate([key_rot, value_raw.astype(BF16)], axis=2).transpose(1, 0, 2)
-    kv_all, queries, grad_all = exchange(
-        0,
+    kv_all, queries = exchange(
+        0, sizes, "send_qkv", (kv_send, SEQ_AXES, pick_context), (query_send, ("context",), pick_target)
+    )
+    kv_all = kv_all.reshape(-1, 2 * HEAD_DIM)
+    columns = 2 * tokens
+    grad_all, mixtures, sums = exchange(
+        7,
         sizes,
-        "send_qkv",
-        (kv_send, SEQ_AXES, pick_context),
-        (query_send, ("context",), pick_target),
+        "attention_forward",
         (cotangent[0], ("expert",), pick_whole),
-    )
-    kv_all = kv_all.reshape(-1, 2 * HEAD_DIM)
-    mixtures, sums = attention_forward(queries, kv_all, owner)
+        compute=attention_forward,
+        data=(queries, kv_all),
+        results=(
+            jax.ShapeDtypeStruct(queries.shape, BF16),
+            jax.ShapeDtypeStruct((KV_HEADS, 1, columns), F32),
+        ),
+        scratch=(pltpu.VMEM((kv_all.shape[0], columns), F32),),
+    )
     (mixture,) = exchange(1, sizes, "send_mixture", (mixtures, ("context",), pick_target))
     mixture_flat = mixture.transpose(1, 0, 2).reshape(tokens, HEADS * HEAD_DIM)
 
@@ -630,14 +681,15 @@
     own_g, own_u, own_d, other_g, other_u, other_d, moe_terms, grad_back, dot_back = run_experts(
         3, sizes, moe_all, grad_all, table_all, gate_weight, up_weight, down_weight
     )
-    (moe_back,) = exchange(6, sizes, "send_outputs", (moe_terms, ("expert",), pick_target))
-    gate_sum, up_sum, down_sum = (
-        reduce_experts(own_g, other_g, sizes),
-        reduce_experts(own_u, other_u, sizes),
-        reduce_experts(own_d, other_d, sizes),
-    )
-
-    outputs = (after_attn + jnp.sum(moe_back.astype(F32), axis=0)).astype(BF16)
+    dp, side = lax.axis_index("dp"), context // 2
+
+    def chip_sum(own, other):
+        held = own + other.astype(F32)
+        return held.reshape(mine, sizes["dp"], 2, *held.shape[2:])
+
+    held_g = chip_sum(own_g, other_g).transpose(1, 0, 2, 3, 4)
+    held_u = chip_sum(own_u, other_u).transpose(1, 0, 2, 3, 4)
+    held_d = chip_sum(own_d, other_d).transpose(2, 0, 1, 3, 4)
     grad_gates = dot_back[:, :mine].reshape(EXPERTS, tokens)
     grad_logits = gates * (grad_gates - jnp.sum(gates * grad_gates, axis=0, keepdims=True))
     router_grad = jnp.einsum(
@@ -654,11 +706,44 @@
     grad_mix = dot_t(grad_after_half, output_weight).astype(BF16)
     grad_mix = grad_mix.reshape(tokens, KV_HEADS, 2 * HEAD_DIM).transpose(1, 0, 2)
     (grad_mixtures,) = exchange(4, sizes, "send_grad_mixture", (grad_mix, ("context",), pick_target))
-    grad_queries, kv_terms = attention_backward(queries, kv_all, mixtures, grad_mixtures, sums, owner)
-    kv_terms = kv_terms.astype(BF16).reshape(-1, tokens, 2 * HEAD_DIM)
-    kv_back, grad_query = exchange(
-        5, sizes, "send_grad_qkv", (kv_terms, SEQ_AXES, pick_target), (grad_queries, ("context",), pick_target)
-    )
+    got_g, got_u, got_d, moe_back, grad_queries, kv_terms = exchange(
+        8,
+        sizes,
+        "attention_backward",
+        (held_g.astype(BF16), ("dp",), pick_target, True),
+        (held_u.astype(BF16), ("dp",), pick_target, True),
+        (held_d.astype(BF16), ("side",), pick_target, True),
+        (moe_terms, ("expert",), pick_target),
+        compute=attention_backward,
+        data=(queries, kv_all, mixtures, grad_mixtures, sums),
+        results=(
+            jax.ShapeDtypeStruct(queries.shape, F32),
+            jax.ShapeDtypeStruct(kv_all.shape, BF16),
+        ),
+        scratch=(pltpu.VMEM(kv_all.shape, F32),),
+    )
+    outputs = (after_attn + jnp.sum(moe_back.astype(F32), axis=0)).astype(BF16)
+    half_g = sum_others(got_g, own_part(held_g, dp), dp).transpose(1, 0, 2, 3)
+    half_u = sum_others(got_u, own_part(held_u, dp), dp).transpose(1, 0, 2, 3)
+    half_d = sum_others(got_d, own_part(held_d, side), side).transpose(1, 0, 2, 3)
+    kv_terms = kv_terms.reshape(-1, tokens, 2 * HEAD_DIM)
+    output_grad, narrow = lax.psum(
+        (output_grad, jnp.concatenate([router_grad, midnorm_grad[:, None]], axis=1)), EVERY
+    )
+    kv_terms, output_grad, narrow = lax.optimization_barrier((kv_terms, output_grad, narrow))
+    kv_back, grad_query, got_g, got_u, got_d = exchange(
+        5,
+        sizes,
+        "send_grad_qkv",
+        (kv_terms, SEQ_AXES, pick_target),
+        (grad_queries, ("context",), pick_target),
+        (half_g.astype(BF16), ("side",), pick_target, True),
+        (half_u.astype(BF16), ("side",), pick_target, True),
+        (half_d.astype(BF16), ("dp",), pick_target, True),
+    )
+    gate_sum = sum_others(got_g, own_part(half_g, side), side)
+    up_sum = sum_others(got_u, own_part(half_u, side), side)
+    down_sum = sum_others(got_d, own_part(half_d, dp), dp)
     grad_kv = jnp.sum(kv_back.astype(F32).reshape(KV_HEADS, owners, tokens, 2 * HEAD_DIM), axis=1)
     grad_kv = grad_kv.transpose(1, 0, 2)
     grad_query = grad_query.transpose(1, 0, 2).reshape(tokens, HEADS, HEAD_DIM)
@@ -673,17 +758,16 @@
     )
     prenorm_grad, grad_inputs = norm_backward(grad_attn_in, normed_first, inverse_first, prenorm_gain)
     grad_inputs = grad_after + grad_inputs
-    narrow = jnp.concatenate([router_grad, prenorm_grad[:, None], midnorm_grad[:, None]], axis=1)
-    query_grad, key_grad, value_grad, output_grad, narrow = lax.psum(
-        (query_grad, key_grad, value_grad, output_grad, narrow), ("dp", "context", "expert")
+    query_grad, key_grad, value_grad, prenorm_grad = lax.psum(
+        (query_grad, key_grad, value_grad, jnp.pad(prenorm_grad[:, None], ((0, 0), (0, EXPERTS)))), EVERY
     )
     dense = (
-        narrow[:, EXPERTS],
+        prenorm_grad[:, 0],
         query_grad,
         key_grad,
         value_grad,
         output_grad,
-        narrow[:, EXPERTS + 1],
+        narrow[:, EXPERTS],
         narrow[:, :EXPERTS],
     )
     return (outputs[None], grad_inputs[None], *dense, gate_sum, up_sum, down_sum)

time: 522 us -> 594 us (1.14); the launches traced: 512 us -> 594 us
  waiting for transfers between devices: 123 us -> 230 us
  Pallas kernels: 224 us -> 269 us
  starting transfers between devices: 29.2 us -> 0.26 us
  local copies, waits for them, and re-layouts: 50.3 us -> 27.1 us
  matrix products: 32.2 us -> 14.5 us
    psum x1 -> x2, waiting for transfers between devices: 78.9 us -> 230 us  [the longest x1 144 us: local(): lax.psum((query_grad, key_grad, value_grad, jnp.pad(prenorm_grad[:, None]...]
    pallas_call x6 -> x7, Pallas kernels: 165 us -> 211 us  [exchange(): pl.pallas_call(functools.partial(exchange_body, items, sizes, compute, le...]
    ppermute x24 -> x0, waiting for transfers between devices: 44.6 us -> none  [the longest x6 24.8 us: flip(): return lax.ppermute(array, axis, [(i, i ^ bit) for i in range(size)])]
    ppermute x24 -> x0, starting transfers between devices: 29.1 us -> none  [the longest x18 23.1 us: shift(): lax.ppermute(array, axes, [(i, (i + step) % total) for i in range(total)])]
    dot_general x12 -> x4, matrix products: 15.6 us -> 6.33 us  [t_dot(): lax.dot_general(left, right, (((0,), (0,)), ((), ())), preferred_element_...]
    slice x18 -> x2, local copies, waits for them, and re-layouts: 10.2 us -> 1.95 us  [the longest x1 1.35 us: local(): prenorm_grad[:, 0]]
    unnamed x250 -> x123, local copies, waits for them, and re-layouts: 22.5 us -> 14.4 us
    convert_element_type x2 -> x3, other arithmetic: 1.02 us -> 7.24 us  [the longest x1 2.62 us: local(): half_g.astype(BF16)]
  transfers between devices with their start and end apart: 25 -> 2, of which waited for: 12 -> 2; matrix products, arithmetic and copies ran while one was open for 14% -> 6% of each run, Pallas kernels for 13% -> 12%
where the time goes in v3:
time: 594 us
  Pallas kernels  269 us (45%)
  waiting for transfers between devices  230 us (39%)
  other arithmetic  37.4 us (6%)
  local copies, waits for them, and re-layouts  27.1 us (5%)
  between operations  15.1 us (3%)
  matrix products  14.5 us (2%)
    pallas_call x7, Pallas kernels, exchange(): pl.pallas_call(functools.partial(exchange_body, items, sizes, compute, le...  211 us
    psum x1, waiting for transfers between devices, local(): lax.psum((query_grad, key_grad, value_grad, jnp.pad(prenorm_grad[:, None]...  144 us
    psum x1, waiting for transfers between devices, local(): lax.psum((output_grad, jnp.concatenate([router_grad, midnorm_grad[:, None...  86.1 us
    pallas_call x1, Pallas kernels, run_experts(): pl.pallas_call(functools.partial(moe_body, sizes), grid=(2 * mine + 1,),...  58.4 us
    unnamed x123, local copies, waits for them, and re-layouts  14.4 us
  transfers between devices with their start and end apart: 2, of which 2 were waited for; matrix products, arithmetic and copies ran while one was open for 6% of the time, Pallas kernels for 12%

profile of v3, /device:TPU:1, one launch (start us, length us, event | category | flops | bytes accessed | tf_op | source)
XLA Modules:
  0.0 593.7 jit_solution(11629655060924324559)
XLA Ops:
  15.6 23.4 %send_qkv.1 = (bf16[32,128,128]{2,1,0:T(8,128)(2,1)}, bf16[4,128,128]{2,1,0:T(8,128)(2,1)}) custom-call(bf16[4,128,128]{2,1,0:T(8,128)(2,1)} %maximum_bitcast_fusion.refs_0_, bf16[4,128,128]{2,1,0:T(8,128)(2,1)} %bitcast.178), custom_call_target="tpu_custom_call" | custom-call | tf_op jit(solution)/shard_map/send_qkv/pallas_call | solution.py:141
  39.1 30.8 %attention_forward.1 = (bf16[8,128,1024]{2,1,0:T(8,128)(2,1)}, bf16[4,128,128]{2,1,0:T(8,128)(2,1)}, f32[4,1,256]{2,1,0:T(1,128)}) custom-call(bf16[128,1024]{1,0:T(8,128)(2,1)} %bitcast.171, bf16[4,128,128]{2,1,0:T(8,128)(2,1)} %get-tuple-element.42.refs_1_.refs_4_, bf16[4096,128]{1,0:T(8,128)(2,1)} %bitcast.160), custom_call_target="tpu_custom_call" | custom-call | tf_op jit(solution)/shard_map/attention_forward/pallas_call | solution.py:141
  69.9 8.8 %send_mixture.1 = bf16[4,128,128]{2,1,0:T(8,128)(2,1)} custom-call(bf16[4,128,128]{2,1,0:T(8,128)(2,1)} %get-tuple-element.44.refs_0_.refs_6_), custom_call_target="tpu_custom_call" | custom-call | tf_op jit(solution)/shard_map/send_mixture/pallas_call | solution.py:141
  82.0 42.0 %send_tokens.1 = (bf16[8,128,1024]{2,1,0:T(8,128)(2,1)}, f32[8,32,128]{2,1,0:T(8,128)}) custom-call(bf16[128,1024]{1,0:T(8,128)(2,1)} %copy-done.12, f32[32,128]{1,0:T(8,128)} %broadcast_select_fusion.refs_1_), custom_call_target="tpu_custom_call" | custom-call | tf_op jit(solution)/shard_map/send_tokens/pallas_call | solution.py:141
  124.1 58.4 %run_experts.1 = (f32[4,8,64,512]{3,2,1,0:T(8,128)}, f32[4,8,64,512]{3,2,1,0:T(8,128)}, f32[4,8,32,1024]{3,2,1,0:T(8,128)}, bf16[4,8,64,512]{3,2,1,0:T(8,128)(2,...) custom-call(bf16[8,128,1024]{2,1,0:T(8,128)(2,1)} %get-tuple-element, ...), custom_call_target="tpu_custom_call" | custom-call | tf_op jit(solution)/shard_map/run_experts/pallas_call | solution.py:512
  184.2 2.1 convert_reduce_fusion.1
  187.4 1.8 fusion.37
  191.6 6.8 %send_grad_mixture.1.refs_7_ = bf16[4,128,128]{2,1,0:T(8,128)(2,1)} custom-call(bf16[4,128,128]{2,1,0:T(8,128)(2,1)} %bitcast.180), custom_call_target="tpu_custom_call" | custom-call | tf_op jit(solution)/shard_map/send_grad_mixture/pallas_call | solution.py:141
  198.4 3.6 convert_add_fusion
  206.4 5.0 convert_add_fusion.1
  211.4 1.9 copy.160
  217.0 64.9 %attention_backward.1 = (bf16[4,4,2,64,512]{4,3,2,1,0:T(8,128)(2,1)}, bf16[4,4,2,64,512]{4,3,2,1,0:T(8,128)(2,1)}, bf16[2,4,4,32,1024]{4,3,2,1,0:T(8,128)(2,1)},...) custom-call(bf16[4,4,2,64,512]{4,3,2,1,0:T(8,128)(2,1)} %bitcast.158, ...), custom_call_target="tpu_custom_call" | custom-call | tf_op jit(solution)/shard_map/attention_backward/pallas_call | solution.py:141
  281.9 3.6 select_reduce_fusion.1
  286.2 2.4 convert_bitcast_fusion.2
  288.6 2.6 convert_bitcast_fusion.3
  291.2 2.2 convert_bitcast_fusion
  293.4 86.1 %all-reduce.8.cloned.1.call-done = (f32[512,1024]{1,0:T(8,128)}, f32[1024,33]{0,1:T(8,128)}) async-done(((f32[512,1024]{1,0:T(8,128)}, f32[1024,33]{0,1:T(8,128)}), (f32[512,1024]{1,0:T(8,128)}, f32[1024,33]{0,1:T(8,128)})) %all-reduce.8.cloned.1.call-update) | async-done | bytes 2232336 | tf_op jit(solution)/shard_map/psum | solution.py:730
  379.5 34.1 %send_grad_qkv.1 = (bf16[32,128,128]{2,1,0:T(8,128)(2,1)}, f32[4,128,128]{2,1,0:T(8,128)}, bf16[2,4,64,512]{3,2,1,0:T(8,128)(2,1)}, bf16[2,4,64,512]{3,2,1,0:T(8,128)(2,1)}, bf16[4,4,32,1024]{3,2,1,0:T(8,128)(2,1)}) custom-call(bf16[32,128,128]{2,1,0:T(8,128)(2,1)} %bitcast.170, f32[4,128,128]{2,1,0:T(8,128)} %get-tuple-element.61.refs_1_, ...), custom_call_target="tpu_custom_call" | custom-call | tf_op jit(solution)/shard_map/send_grad_qkv/pallas_call | solution.py:141
  418.3 2.2 fusion.58
  422.1 1.9 fusion.35
  425.4 2.1 convert_reduce_fusion
  430.2 2.0 bitcast_add_fusion.3
  435.0 144.0 %all-reduce.6.cloned.1.call-done = (f32[1024,33]{0,1:T(8,128)}, f32[1024,512]{1,0:T(8,128)}, f32[1024,256]{1,0:T(8,128)}, f32[1024,256]{1,0:T(8,128)}) async-done(((f32[1024,33]{0,1:T(8,128)}, f32[1024,512]{1,0:T(8,128)}, f32[1024,256]{1,0:T(8,128)}, f32[1024,256]{1,0:T(8,128)}), (f32[1024,33]{0,1:T(8,128)}, f32[1024,512]{1,0:T(8,128)}, f32[1024,256]{1,0:T(8,128)}, ...) | async-done | bytes 4329488 | tf_op jit(solution)/shard_map/psum | solution.py:761
  580.3 3.2 copy.169
  (194 shorter events, 42.9 us)
Async XLA Ops:
  7.2 4.6 copy-start.20
  7.2 372.3 %all-reduce.8.cloned.1.call-start = ((), (), s32[]{:S(2)}) async-start(), calls=%async_computation.1 | async-start | bytes 4521984 | tf_op jit(solution)/shard_map/psum | solution.py:730
  7.7 7.0 %copy-start.25 = (f32[128,64]{1,0:T(8,128)}, f32[128,64]{1,0:T(8,128)S(1)}, u32[]{:S(2)}) copy-start(f32[128,64]{1,0:T(8,128)S(1)} %get-tuple-element.103) | copy-start | bytes 98308
  7.7 7.0 %copy-start.31 = (f32[128,64]{1,0:T(8,128)}, f32[128,64]{1,0:T(8,128)S(1)}, u32[]{:S(2)}) copy-start(f32[128,64]{1,0:T(8,128)S(1)} %get-tuple-element.102) | copy-start | bytes 98308
  8.8 4.5 copy-start.51
  13.9 65.8 %copy-start.10 = (bf16[512,1024]{1,0:T(8,128)(2,1)S(1)}, bf16[512,1024]{1,0:T(8,128)(2,1)}, u32[]{:S(2)}) copy-start(bf16[512,1024]{1,0:T(8,128)(2,1)} %param.18) | copy-start | bytes 3145732
  15.6 64.6 %copy-start.57 = (s32[1,128,8]{1,2,0:T(8,128)S(1)}, s32[1,128,8]{1,2,0:T(8,128)}, u32[]{:S(2)}) copy-start(s32[1,128,8]{1,2,0:T(8,128)} %param.24) | copy-start | bytes 12292
  15.6 65.4 %copy-start.47 = (f32[1024]{0:T(1024)S(1)}, f32[1024]{0:T(1024)}, u32[]{:S(2)}) copy-start(f32[1024]{0:T(1024)} %param.19) | copy-start | bytes 12292
  39.1 42.1 %copy-start.42 = (bf16[1024,32]{0,1:T(8,128)(2,1)S(1)}, bf16[1024,32]{0,1:T(8,128)(2,1)}, u32[]{:S(2)}) copy-start(bf16[1024,32]{0,1:T(8,128)(2,1)} %param.20) | copy-start | bytes 196612
  79.8 44.3 %copy-start.23 = (bf16[128,4,128]{0,2,1:T(8,128)(2,1)}, bf16[128,4,128]{0,2,1:T(8,128)(2,1)S(1)}, u32[]{:S(2)}) copy-start(bf16[128,4,128]{0,2,1:T(8,128)(2,1)S(1)} %copy.122) | copy-start | bytes 393220
  81.4 42.7 %copy-start.33 = (f32[32,128]{1,0:T(8,128)}, f32[32,128]{1,0:T(8,128)S(1)}, u32[]{:S(2)}) copy-start(f32[32,128]{1,0:T(8,128)S(1)} %get-tuple-element.107) | copy-start | bytes 49156
  81.4 42.7 %copy-start.49 = (f32[128]{0:T(128)}, f32[128]{0:T(128)S(1)}, u32[]{:S(2)}) copy-start(f32[128]{0:T(128)S(1)} %get-tuple-element.106) | copy-start | bytes 1540
  81.4 42.7 %copy-start.53 = (f32[128]{0:T(128)}, f32[128]{0:T(128)S(1)}, u32[]{:S(2)}) copy-start(f32[128]{0:T(128)S(1)} %fusion.44) | copy-start | bytes 1540
  182.5 4.0 copy-start.7
  182.5 4.0 copy-start.43
  182.6 4.0 copy-start.48
  189.9 389.1 %all-reduce.6.cloned.1.call-start = ((), (), s32[]{:S(2)}) async-start(), calls=%async_computation | async-start | bytes 8716288 | tf_op jit(solution)/shard_map/psum | solution.py:761
  202.0 4.4 copy-start.16
  286.2 5.1 copy-start.1
  379.5 35.6 %copy-start.26 = (f32[128,64]{1,0:T(8,128)S(1)}, f32[128,64]{1,0:T(8,128)}, u32[]{:S(2)}) copy-start(f32[128,64]{1,0:T(8,128)} %copy-done.25) | copy-start | bytes 98308
  416.8 5.0 copy-start.41
  416.8 5.1 copy-start.40
  425.4 4.2 copy-start.27
  580.3 4.2 copy-start.28
  (36 other events, 90.6 us)
Sparse Core Ops, SparseCore 0:
  190.0 189.4 all-reduce.7
  425.5 153.4 all-reduce.5

commit v4 on v3

--- a/solution.py
+++ b/solution.py
@@ -19,7 +19,6 @@
 BF16 = jnp.bfloat16
 MESH_ID = pl.DeviceIdType.MESH
 SEQ_AXES = ("context", "expert")
-EVERY = ("dp", "context", "expert")
 
 
 def dot(left, right):
@@ -566,6 +565,97 @@
     )(moe_all, grad_all, table_all, gate_weight, up_weight, down_weight)
 
 
+CHIP_AXES = ("dp", "side", "expert")
+
+
+def sum_body(sizes, load_ref, out_ref, near, sums, got, *sems):
+    near_sems, send_sems, recv_sems, give_sems, take_sems, pass_sems, land_sems = sems
+    core = lax.rem(lax.axis_index("context"), 2)
+    partner = {"context": lax.axis_index("context") + 1 - 2 * core}
+    me, total = own_index(CHIP_AXES, sizes), group_size(CHIP_AXES, sizes)
+
+    def place(step):
+        target = lax.rem(me + step, total)
+        return target, coords_of(CHIP_AXES, sizes, target)
+
+    def remote(src, dst, send, recv, peer):
+        return pltpu.make_async_remote_copy(
+            src_ref=src, dst_ref=dst, send_sem=send, recv_sem=recv, device_id=peer, device_id_type=MESH_ID
+        )
+
+    def reduce_copy(step):
+        target, peer = place(step)
+        return remote(sums.at[target], got.at[me], send_sems.at[step], recv_sems.at[step], peer)
+
+    def gather_copy(step):
+        _, peer = place(step)
+        own = out_ref.at[core, me]
+        return remote(own, own, give_sems.at[step], take_sems.at[step], peer)
+
+    def pass_copy(step):
+        source = out_ref.at[core, lax.rem(me - step + total, total)]
+        return remote(source, source, pass_sems.at[step], land_sems.at[step], partner)
+
+    def each(start, body):
+        def run(step, carry):
+            body(step)
+            return carry
+
+        lax.fori_loop(start, total, run, 0)
+
+    barrier = pltpu.get_barrier_semaphore()
+    pl.semaphore_signal(barrier, inc=1, device_id=partner, device_id_type=MESH_ID)
+    each(
+        1,
+        lambda step: pl.semaphore_signal(
+            barrier, inc=1, device_id=place(step)[1], device_id_type=MESH_ID
+        ),
+    )
+    pl.semaphore_wait(barrier, total)
+
+    first = remote(load_ref.at[1 - core], near, near_sems.at[0], near_sems.at[1], partner)
+    first.start()
+    first.wait()
+
+    def add(chunk):
+        sums[chunk] = (load_ref[core, chunk].astype(F32) + near[chunk].astype(F32)).astype(BF16)
+
+    each(0, add)
+    got[me] = sums[me]
+    each(1, lambda step: reduce_copy(step).start())
+    each(1, lambda step: reduce_copy(step).wait())
+    whole = lax.fori_loop(
+        0, total, lambda i, held: held + got[i].astype(F32), jnp.zeros(got.shape[1:], F32)
+    )
+    out_ref[core, me] = whole.astype(BF16)
+    each(1, lambda step: gather_copy(step).start())
+    pass_copy(0).start()
+
+    def forward(step):
+        gather_copy(step).wait_recv()
+        pass_copy(step).start()
+
+    each(1, forward)
+    each(1, lambda step: gather_copy(step).wait_send())
+    each(0, lambda step: pass_copy(step).wait())
+
+
+def sum_everywhere(cid, sizes, payload):
+    total = payload.shape[1]
+    half = payload.shape[1:]
+    dma = pltpu.SemaphoreType.DMA
+    vmem = pl.BlockSpec(memory_space=pltpu.VMEM)
+    return pl.pallas_call(
+        functools.partial(sum_body, sizes),
+        out_shape=jax.ShapeDtypeStruct(payload.shape, payload.dtype),
+        in_specs=[vmem],
+        out_specs=vmem,
+        scratch_shapes=[pltpu.VMEM(half, BF16)] * 3 + [dma((2,))] + [dma((total,))] * 6,
+        name="sum_everywhere",
+        compiler_params=pltpu.CompilerParams(collective_id=cid, has_side_effects=True),
+    )(payload)
+
+
 def rope_tables(positions, head_size):
     half_dim = head_size // 2
     frequency = ROPE_BASE ** (-2.0 * jnp.arange(half_dim, dtype=F32) / head_size)
@@ -702,7 +792,7 @@
     midnorm_grad, grad_after = norm_backward(grad_moe_in, normed_second, inverse_second, midnorm_gain)
     grad_after = grad_out + grad_after
     grad_after_half = grad_after.astype(BF16)
-    output_grad = t_dot(mixture_flat, grad_after_half)
+    output_grad = t_dot(grad_after_half, mixture_flat)
     grad_mix = dot_t(grad_after_half, output_weight).astype(BF16)
     grad_mix = grad_mix.reshape(tokens, KV_HEADS, 2 * HEAD_DIM).transpose(1, 0, 2)
     (grad_mixtures,) = exchange(4, sizes, "send_grad_mixture", (grad_mix, ("context",), pick_target))
@@ -727,10 +817,6 @@
     half_u = sum_others(got_u, own_part(held_u, dp), dp).transpose(1, 0, 2, 3)
     half_d = sum_others(got_d, own_part(held_d, side), side).transpose(1, 0, 2, 3)
     kv_terms = kv_terms.reshape(-1, tokens, 2 * HEAD_DIM)
-    output_grad, narrow = lax.psum(
-        (output_grad, jnp.concatenate([router_grad, midnorm_grad[:, None]], axis=1)), EVERY
-    )
-    kv_terms, output_grad, narrow = lax.optimization_barrier((kv_terms, output_grad, narrow))
     kv_back, grad_query, got_g, got_u, got_d = exchange(
         5,
         sizes,
@@ -758,17 +844,34 @@
     )
     prenorm_grad, grad_inputs = norm_backward(grad_attn_in, normed_first, inverse_first, prenorm_gain)
     grad_inputs = grad_after + grad_inputs
-    query_grad, key_grad, value_grad, prenorm_grad = lax.psum(
-        (query_grad, key_grad, value_grad, jnp.pad(prenorm_grad[:, None], ((0, 0), (0, EXPERTS)))), EVERY
-    )
+    half, part = HEADS * HEAD_DIM // 2, EXPERTS // 2
+    blank = jnp.zeros((width, 128 - part - 1), F32)
+    payload = jnp.stack(
+        [
+            jnp.concatenate(
+                [query_grad, output_grad[:, :half], router_grad[:, :part], prenorm_grad[:, None], blank],
+                axis=1,
+            ),
+            jnp.concatenate(
+                [key_grad, value_grad, output_grad[:, half:], router_grad[:, part:], midnorm_grad[:, None], blank],
+                axis=1,
+            ),
+        ]
+    ).astype(BF16)
+    chips = group_size(CHIP_AXES, sizes)
+    summed = sum_everywhere(9, sizes, payload.reshape(2, chips, width // chips, -1))
+    first, second = summed.reshape(payload.shape).astype(F32)
+    columns = 2 * half
     dense = (
-        prenorm_grad[:, 0],
-        query_grad,
-        key_grad,
-        value_grad,
-        output_grad,
-        narrow[:, EXPERTS],
-        narrow[:, :EXPERTS],
+        first[:, columns + half + part],
+        first[:, :columns],
+        second[:, :half],
+        second[:, half:columns],
+        jnp.concatenate([first[:, columns : columns + half], second[:, columns : columns + half]], axis=1).T,
+        second[:, columns + half + part],
+        jnp.concatenate(
+            [table[:, columns + half : columns + half + part] for table in (first, second)], axis=1
+        ),
     )
     return (outputs[None], grad_inputs[None], *dense, gate_sum, up_sum, down_sum)
 

time: 594 us -> 471 us (0.79)
  waiting for transfers between devices: 230 us -> 0 us
  Pallas kernels: 269 us -> 353 us
  local copies, waits for them, and re-layouts: 27.1 us -> 50.4 us
  between operations: 15.1 us -> 1.61 us
  other arithmetic: 37.4 us -> 50.2 us
    psum x2 -> x0, waiting for transfers between devices: 230 us -> none  [the longest x1 144 us: local(): lax.psum((query_grad, key_grad, value_grad, jnp.pad(prenorm_grad[:, None]...]
    pallas_call x0 -> x1, Pallas kernels: none -> 80 us  [sum_everywhere(): pl.pallas_call(functools.partial(sum_body, sizes), out_shape=jax.ShapeDty...]
    slice x3 -> x11, local copies, waits for them, and re-layouts: 2.61 us -> 14.5 us  [the longest x1 3.39 us: local(): second[:, columns:columns + half]]
    concatenate x0 -> x4, local copies, waits for them, and re-layouts: none -> 8.09 us  [the longest x2 4.34 us: local(): jnp.concatenate([key_grad, value_grad, output_grad[:, half:], router_grad...]
    unnamed x123 -> x109, local copies, waits for them, and re-layouts: 14.4 us -> 10.4 us
  transfers between devices with their start and end apart: 2 -> 0, of which waited for: 2 -> 0; matrix products, arithmetic and copies ran while one was open for 6% -> 0% of each run, Pallas kernels for 12% -> 0%
where the time goes in v4:
time: 471 us; the launch traced here: 469 us
  Pallas kernels  353 us (75%)
  local copies, waits for them, and re-layouts  50.4 us (11%)
  other arithmetic  50.2 us (11%)
  matrix products  14.4 us (3%)
    pallas_call x7, Pallas kernels, exchange(): pl.pallas_call(functools.partial(exchange_body, items, sizes, compute, le...  214 us
    pallas_call x1, Pallas kernels, sum_everywhere(): pl.pallas_call(functools.partial(sum_body, sizes), out_shape=jax.ShapeDty...  80 us
    pallas_call x1, Pallas kernels, run_experts(): pl.pallas_call(functools.partial(moe_body, sizes), grid=(2 * mine + 1,),...  58.4 us
    unnamed x109, local copies, waits for them, and re-layouts  10.4 us

profile of v4, /device:TPU:1, one launch (start us, length us, event | category | flops | bytes accessed | tf_op | source)
XLA Modules:
  0.0 469.4 jit_solution(12915271790242378670)
XLA Ops:
  9.0 23.4 %send_qkv.1 = (bf16[32,128,128]{2,1,0:T(8,128)(2,1)}, bf16[4,128,128]{2,1,0:T(8,128)(2,1)}) custom-call(bf16[4,128,128]{2,1,0:T(8,128)(2,1)} %maximum_bitcast_fusion.1.refs_0_, bf16[4,128,128]{2,1,0:T(8,128)(2,1)} %bitcast.209), custom_call_target="tpu_custom_call" | custom-call | tf_op jit(solution)/shard_map/send_qkv/pallas_call | solution.py:140
  32.4 30.8 %attention_forward.1 = (bf16[8,128,1024]{2,1,0:T(8,128)(2,1)}, bf16[4,128,128]{2,1,0:T(8,128)(2,1)}, f32[4,1,256]{2,1,0:T(1,128)}) custom-call(bf16[128,1024]{1,0:T(8,128)(2,1)} %bitcast.202, bf16[4,128,128]{2,1,0:T(8,128)(2,1)} %get-tuple-element.39.refs_1_.refs_4_, bf16[4096,128]{1,0:T(8,128)(2,1)} %bitcast.184), custom_call_target="tpu_custom_call" | custom-call | tf_op jit(solution)/shard_map/attention_forward/pallas_call | solution.py:140
  63.2 8.8 %send_mixture.1 = bf16[4,128,128]{2,1,0:T(8,128)(2,1)} custom-call(bf16[4,128,128]{2,1,0:T(8,128)(2,1)} %get-tuple-element.41.refs_0_.refs_6_), custom_call_target="tpu_custom_call" | custom-call | tf_op jit(solution)/shard_map/send_mixture/pallas_call | solution.py:140
  75.8 42.0 %send_tokens.1 = (bf16[8,128,1024]{2,1,0:T(8,128)(2,1)}, f32[8,32,128]{2,1,0:T(8,128)}) custom-call(bf16[128,1024]{1,0:T(8,128)(2,1)} %copy-done.13, f32[32,128]{1,0:T(8,128)} %broadcast_select_fusion.refs_1_), custom_call_target="tpu_custom_call" | custom-call | tf_op jit(solution)/shard_map/send_tokens/pallas_call | solution.py:140
  117.8 58.4 %run_experts.1 = (f32[4,8,64,512]{3,2,1,0:T(8,128)}, f32[4,8,64,512]{3,2,1,0:T(8,128)}, f32[4,8,32,1024]{3,2,1,0:T(8,128)}, bf16[4,8,64,512]{3,2,1,0:T(8,128)(2,...) custom-call(bf16[8,128,1024]{2,1,0:T(8,128)(2,1)} %get-tuple-element, ...), custom_call_target="tpu_custom_call" | custom-call | tf_op jit(solution)/shard_map/run_experts/pallas_call | solution.py:511
  183.5 6.8 %send_grad_mixture.1.refs_7_ = bf16[4,128,128]{2,1,0:T(8,128)(2,1)} custom-call(bf16[4,128,128]{2,1,0:T(8,128)(2,1)} %bitcast.211), custom_call_target="tpu_custom_call" | custom-call | tf_op jit(solution)/shard_map/send_grad_mixture/pallas_call | solution.py:140
  190.3 2.9 convert_add_fusion
  197.7 5.0 %convert_add_fusion.1 = (f32[4,8,64,512]{3,2,1,0:T(8,128)S(1)}, f32[4,8,64,512]{3,2,1,0:T(8,128)S(1)}) fusion(f32[4,8,64,512]{3,2,1,0:T(8,128)} %get-tuple-element.47, bf16[4,8,64,512]{3,2,1,0:T(8,128)(2,1)S(1)} %copy-done.16, f32[4,8,64,512]{3,2,1,0:T(8,128)} %get-tuple-element.45, bf16[4,8,64,512]{3,2,1,0:T(8,128)(2,1)S(1)} %copy-done.15), kind=kLoop, calls=%fused_computation.9 | loop fusion | flops 4194304 | bytes 20971520 | tf_op jit(solution)/shard_map/add | solution.py:777
  204.5 2.2 copy.229
  207.1 64.2 %attention_backward.1 = (bf16[4,4,2,64,512]{4,3,2,1,0:T(8,128)(2,1)}, bf16[4,4,2,64,512]{4,3,2,1,0:T(8,128)(2,1)}, bf16[2,4,4,32,1024]{4,3,2,1,0:T(8,128)(2,1)},...) custom-call(bf16[4,4,2,64,512]{4,3,2,1,0:T(8,128)(2,1)} %bitcast.182, ...), custom_call_target="tpu_custom_call" | custom-call | tf_op jit(solution)/shard_map/attention_backward/pallas_call | solution.py:140
  271.4 2.5 select_reduce_fusion
  273.9 3.8 convert_bitcast_fusion
  277.7 3.4 select_reduce_fusion.1
  281.1 2.3 convert_bitcast_fusion.2
  283.4 2.3 convert_bitcast_fusion.3
  285.6 38.3 %send_grad_qkv.1 = (bf16[32,128,128]{2,1,0:T(8,128)(2,1)}, f32[4,128,128]{2,1,0:T(8,128)}, bf16[2,4,64,512]{3,2,1,0:T(8,128)(2,1)}, bf16[2,4,64,512]{3,2,1,0:T(8,128)(2,1)}, bf16[4,4,32,1024]{3,2,1,0:T(8,128)(2,1)}) custom-call(bf16[32,128,128]{2,1,0:T(8,128)(2,1)} %bitcast.201, f32[4,128,128]{2,1,0:T(8,128)} %get-tuple-element.57.refs_1_, ...), custom_call_target="tpu_custom_call" | custom-call | tf_op jit(solution)/shard_map/send_grad_qkv/pallas_call | solution.py:140
  345.0 2.2 fusion.18
  350.6 2.6 concatenate.68
  357.5 3.9 concatenate.72
  361.4 3.7 pad_maximum_fusion.load_ref
  365.0 80.0 %sum_everywhere.1 = bf16[2,64,16,896]{3,2,1,0:T(8,128)(2,1)} custom-call(bf16[2,64,16,896]{3,2,1,0:T(8,128)(2,1)} %pad_maximum_fusion.load_ref), custom_call_target="tpu_custom_call" | custom-call | tf_op jit(solution)/shard_map/sum_everywhere/pallas_call | solution.py:648
  445.1 4.3 fusion.48
  453.4 3.4 fusion.47
  459.7 2.9 maximum_bitcast_fusion
  (192 shorter events, 67.7 us)
Async XLA Ops:
  1.1 5.8 %copy-start.23 = (f32[128,64]{1,0:T(8,128)}, f32[128,64]{1,0:T(8,128)S(1)}, u32[]{:S(2)}) copy-start(f32[128,64]{1,0:T(8,128)S(1)} %get-tuple-element.100) | copy-start | bytes 98308
  1.1 5.8 %copy-start.26 = (f32[128,64]{1,0:T(8,128)}, f32[128,64]{1,0:T(8,128)S(1)}, u32[]{:S(2)}) copy-start(f32[128,64]{1,0:T(8,128)S(1)} %get-tuple-element.99) | copy-start | bytes 98308
  1.1 5.9 %copy-start.9 = (bf16[1024,512]{1,0:T(8,128)(2,1)S(1)}, bf16[1024,512]{1,0:T(8,128)(2,1)}, u32[]{:S(2)}) copy-start(bf16[1024,512]{1,0:T(8,128)(2,1)} %param.15) | copy-start | bytes 3145732
  6.9 66.2 %copy-start.32 = (f32[128,64]{0,1:T(8,128)}, f32[128,64]{0,1:T(8,128)S(1)}, u32[]{:S(2)}) copy-start(f32[128,64]{0,1:T(8,128)S(1)} %copy.165) | copy-start | bytes 98308
  7.0 66.1 %copy-start.34 = (f32[128,64]{0,1:T(8,128)}, f32[128,64]{0,1:T(8,128)S(1)}, u32[]{:S(2)}) copy-start(f32[128,64]{0,1:T(8,128)S(1)} %copy.166) | copy-start | bytes 98308
  7.0 66.1 %copy-start.11 = (bf16[512,1024]{1,0:T(8,128)(2,1)S(1)}, bf16[512,1024]{1,0:T(8,128)(2,1)}, u32[]{:S(2)}) copy-start(bf16[512,1024]{1,0:T(8,128)(2,1)} %param.18) | copy-start | bytes 3145732
  7.6 66.8 %copy-start.40 = (f32[1024]{0:T(1024)S(1)}, f32[1024]{0:T(1024)}, u32[]{:S(2)}) copy-start(f32[1024]{0:T(1024)} %param.19) | copy-start | bytes 12292
  7.6 67.3 %copy-start.50 = (s32[1,128,8]{1,2,0:T(8,128)S(1)}, s32[1,128,8]{1,2,0:T(8,128)}, u32[]{:S(2)}) copy-start(s32[1,128,8]{1,2,0:T(8,128)} %param.24) | copy-start | bytes 12292
  7.6 67.3 %copy-start.37 = (bf16[1024,32]{0,1:T(8,128)(2,1)S(1)}, bf16[1024,32]{0,1:T(8,128)(2,1)}, u32[]{:S(2)}) copy-start(bf16[1024,32]{0,1:T(8,128)(2,1)} %param.20) | copy-start | bytes 196612
  73.1 44.7 %copy-start.21 = (bf16[128,4,128]{0,2,1:T(8,128)(2,1)}, bf16[128,4,128]{0,2,1:T(8,128)(2,1)S(1)}, u32[]{:S(2)}) copy-start(bf16[128,4,128]{0,2,1:T(8,128)(2,1)S(1)} %copy.168) | copy-start | bytes 393220
  75.1 42.7 %copy-start.27 = (f32[32,128]{1,0:T(8,128)}, f32[32,128]{1,0:T(8,128)S(1)}, u32[]{:S(2)}) copy-start(f32[32,128]{1,0:T(8,128)S(1)} %get-tuple-element.104) | copy-start | bytes 49156
  75.1 42.7 %copy-start.42 = (f32[128]{0:T(128)}, f32[128]{0:T(128)S(1)}, u32[]{:S(2)}) copy-start(f32[128]{0:T(128)S(1)} %get-tuple-element.103) | copy-start | bytes 1540
  75.2 42.7 %copy-start.44 = (f32[128]{0:T(128)}, f32[128]{0:T(128)S(1)}, u32[]{:S(2)}) copy-start(f32[128]{0:T(128)S(1)} %fusion.40) | copy-start | bytes 1540
  176.2 5.6 %copy-start.6 = (f32[128,1024]{1,0:T(8,128)S(1)}, f32[128,1024]{1,0:T(8,128)}, u32[]{:S(2)}) copy-start(f32[128,1024]{1,0:T(8,128)} %copy-done.5) | copy-start | bytes 1572868
  176.2 5.6 %copy-start.25 = (bf16[1,128,1024]{2,1,0:T(8,128)(2,1)S(1)}, bf16[1,128,1024]{2,1,0:T(8,128)(2,1)}, u32[]{:S(2)}) copy-start(bf16[1,128,1024]{2,1,0:T(8,128)(2,1)} %param.25) | copy-start | bytes 786436
  176.3 5.8 %copy-start.12 = (bf16[512,1024]{1,0:T(8,128)(2,1)S(1)}, bf16[512,1024]{1,0:T(8,128)(2,1)}, u32[]{:S(2)}) copy-start(bf16[512,1024]{1,0:T(8,128)(2,1)} %param.18) | copy-start | bytes 3145732
  177.9 12.4 %copy-start.17 = (bf16[4,8,32,1024]{3,2,1,0:T(8,128)(2,1)S(1)}, bf16[4,8,32,1024]{3,2,1,0:T(8,128)(2,1)}, u32[]{:S(2)}) copy-start(bf16[4,8,32,1024]{3,2,1,0:T(8,128)(2,1)} %get-tuple-element.50) | copy-start | bytes 6291460
  325.6 7.1 %copy-start.36 = (f32[4,128,128]{2,1,0:T(8,128)S(1)}, f32[4,128,128]{2,1,0:T(8,128)}, u32[]{:S(2)}) copy-start(f32[4,128,128]{2,1,0:T(8,128)} %get-tuple-element.61) | copy-start | bytes 786436
  331.9 6.7 %copy-start.24 = (f32[128,64]{1,0:T(8,128)S(1)}, f32[128,64]{1,0:T(8,128)}, u32[]{:S(2)}) copy-start(f32[128,64]{1,0:T(8,128)} %copy-done.23) | copy-start | bytes 98308
  335.4 9.6 %copy-start.10 = (bf16[1024,512]{1,0:T(8,128)(2,1)S(1)}, bf16[1024,512]{1,0:T(8,128)(2,1)}, u32[]{:S(2)}) copy-start(bf16[1024,512]{1,0:T(8,128)(2,1)} %param.15) | copy-start | bytes 3145732
  338.7 9.7 %copy-start.22 = (bf16[128,4,128]{0,2,1:T(8,128)(2,1)S(1)}, bf16[128,4,128]{0,2,1:T(8,128)(2,1)}, u32[]{:S(2)}) copy-start(bf16[128,4,128]{0,2,1:T(8,128)(2,1)} %copy-done.21) | copy-start | bytes 393220
  343.6 6.3 %copy-start.30 = (bf16[128,4,64]{0,2,1:T(8,128)(2,1)}, bf16[128,4,64]{0,2,1:T(8,128)(2,1)S(1)}, u32[]{:S(2)}) copy-start(bf16[128,4,64]{0,2,1:T(8,128)(2,1)S(1)} %copy.183) | copy-start | bytes 196612
  348.8 6.0 %copy-start.29 = (bf16[128,4,64]{0,2,1:T(8,128)(2,1)S(1)}, bf16[128,4,64]{0,2,1:T(8,128)(2,1)}, u32[]{:S(2)}) copy-start(bf16[128,4,64]{0,2,1:T(8,128)(2,1)} %copy.182) | copy-start | bytes 196612
  349.9 6.1 %copy-start.31 = (bf16[128,4,64]{0,2,1:T(8,128)(2,1)S(1)}, bf16[128,4,64]{0,2,1:T(8,128)(2,1)}, u32[]{:S(2)}) copy-start(bf16[128,4,64]{0,2,1:T(8,128)(2,1)} %copy-done.30) | copy-start | bytes 196612
  (27 other events, 112.9 us)

commit v5 on v3

--- a/solution.py
+++ b/solution.py
@@ -19,7 +19,6 @@
 BF16 = jnp.bfloat16
 MESH_ID = pl.DeviceIdType.MESH
 SEQ_AXES = ("context", "expert")
-EVERY = ("dp", "context", "expert")
 
 
 def dot(left, right):
@@ -77,17 +76,10 @@
     return ref.at[peer["context"]]
 
 
-def exchange_body(items, sizes, compute, more_ins, more_outs, *refs):
-    count = len(items)
-    ins, refs = refs[:count], refs[count:]
-    data_ins, refs = refs[:more_ins], refs[more_ins:]
-    outs, refs = refs[:count], refs[count:]
-    data_outs, refs = refs[:more_outs], refs[more_outs:]
-    sems, scratch = refs[: 2 * count], refs[2 * count :]
-
+def greet(all_axes, sizes):
     barrier = pltpu.get_barrier_semaphore()
     groups = []
-    for axes, _, _ in items:
+    for axes in all_axes:
         if not any(set(axes) <= set(other) for other in groups):
             groups = [other for other in groups if not set(other) <= set(axes)] + [axes]
     signals = 0
@@ -99,29 +91,45 @@
         signals += total - 1
     pl.semaphore_wait(barrier, signals)
 
+
+def launch(sizes, axes, pick, keep, source, landing, send, recv):
+    started = []
+    me, total = own_index(axes, sizes), group_size(axes, sizes)
+    for step in range(1, total):
+        target = lax.rem(me + step, total)
+        peer = coords_of(axes, sizes, target)
+        copy = pltpu.make_async_remote_copy(
+            src_ref=pick(source, target, peer),
+            dst_ref=landing.at[me],
+            send_sem=send.at[step],
+            recv_sem=recv.at[step],
+            device_id=peer,
+            device_id_type=MESH_ID,
+        )
+        copy.start()
+        started.append(copy)
+    if keep:
+        own = pltpu.make_async_copy(
+            pick(source, me, coords_of(axes, sizes, me)), landing.at[me], send.at[0]
+        )
+        own.start()
+        started.append(own)
+    return started
+
+
+def exchange_body(items, sizes, compute, more_ins, more_outs, *refs):
+    count = len(items)
+    ins, refs = refs[:count], refs[count:]
+    data_ins, refs = refs[:more_ins], refs[more_ins:]
+    outs, refs = refs[:count], refs[count:]
+    data_outs, refs = refs[:more_outs], refs[more_outs:]
+    sems, scratch = refs[: 2 * count], refs[2 * count :]
+
+    greet([item[0] for item in items], sizes)
     waits = []
-    for number, (axes, pick, keep) in enumerate(items):
-        me, total = own_index(axes, sizes), group_size(axes, sizes)
-        send, recv = sems[2 * number], sems[2 * number + 1]
-        for step in range(1, total):
-            target = lax.rem(me + step, total)
-            peer = coords_of(axes, sizes, target)
-            copy = pltpu.make_async_remote_copy(
-                src_ref=pick(ins[number], target, peer),
-                dst_ref=outs[number].at[me],
-                send_sem=send.at[step],
-                recv_sem=recv.at[step],
-                device_id=peer,
-                device_id_type=MESH_ID,
-            )
-            copy.start()
-            waits.append(copy)
-        if keep:
-            own = pltpu.make_async_copy(
-                pick(ins[number], me, coords_of(axes, sizes, me)), outs[number].at[me], send.at[0]
-            )
-            own.start()
-            waits.append(own)
+    for number, item in enumerate(items):
+        pair = sems[2 * number : 2 * number + 2]
+        waits += launch(sizes, *item, ins[number], outs[number], *pair)
     if compute is not None:
         compute(data_ins, data_outs, scratch)
     for copy in waits:
@@ -249,7 +257,118 @@
         return carry
 
     lax.fori_loop(0, blocks, block, 0)
-    terms_ref[...] = sum_kv[...].astype(BF16)
+    terms_ref[...] = sum_kv[...].astype(BF16).reshape(terms_ref.shape)
+
+
+def backward_body(sizes, *refs):
+    owns, others, y_ref, data, refs = refs[:3], refs[3:6], refs[6], refs[7:12], refs[12:]
+    y_back, kv_back, query_back, *totals = refs[:6]
+    sends, gots, sends_2, gots_2 = refs[6:9], refs[9:12], refs[12:15], refs[15:18]
+    grad_query, terms, sum_kv = refs[18:21]
+    sems = refs[21:]
+    dp, side = lax.axis_index("dp"), lax.axis_index("context") // 2
+    experts = owns[0].shape[0]
+    firsts = (("dp",), ("dp",), ("side",))
+    seconds = (("side",), ("side",), ("dp",))
+
+    def chip_sum(i, expert, place):
+        return owns[i][expert, place] + others[i][expert, place].astype(F32)
+
+    for i, axes in enumerate(firsts):
+
+        def fill(expert, carry, i=i, axes=axes):
+            for d in range(4):
+                for v in range(2):
+                    terms_now = chip_sum(i, expert, 2 * d + v).astype(BF16)
+                    if axes == ("dp",):
+                        sends[i][d, expert, v] = terms_now
+                    else:
+                        sends[i][v, expert, d] = terms_now
+            return carry
+
+        lax.fori_loop(0, experts, fill, 0)
+    greet([SEQ_AXES, ("dp",)], sizes)
+    stage_1 = []
+    for i, axes in enumerate(firsts):
+        stage_1 += launch(sizes, axes, pick_target, False, sends[i], gots[i], *sems[2 * i : 2 * i + 2])
+    rest = launch(sizes, ("expert",), pick_target, True, y_ref, y_back, *sems[6:8])
+
+    attention_backward(data, (grad_query, terms), (sum_kv,))
+    rest += launch(sizes, SEQ_AXES, pick_target, True, terms, kv_back, *sems[8:10])
+    rest += launch(sizes, ("context",), pick_target, True, grad_query, query_back, *sems[10:12])
+    for copy in stage_1:
+        copy.wait()
+
+    def part(i, expert, place):
+        if firsts[i] == ("dp",):
+            total = chip_sum(i, expert, 2 * dp + place)
+            for step in range(1, 4):
+                total = total + gots[i][lax.rem(dp + step, 4), expert, place].astype(F32)
+            return total
+        return chip_sum(i, expert, 2 * place + side) + gots[i][1 - side, expert, place].astype(F32)
+
+    for i, axes in enumerate(seconds):
+
+        def refill(expert, carry, i=i, axes=axes):
+            for place in range(group_size(axes, sizes)):
+                sends_2[i][place, expert] = part(i, expert, place).astype(BF16)
+            return carry
+
+        lax.fori_loop(0, experts, refill, 0)
+    stage_2 = []
+    for i, axes in enumerate(seconds):
+        stage_2 += launch(
+            sizes, axes, pick_target, False, sends_2[i], gots_2[i], *sems[12 + 2 * i : 14 + 2 * i]
+        )
+    for copy in stage_2:
+        copy.wait()
+    for i, axes in enumerate(seconds):
+        me, total = own_index(axes, sizes), group_size(axes, sizes)
+
+        def close(expert, carry, i=i, me=me, total=total):
+            held = part(i, expert, me)
+            for step in range(1, total):
+                held = held + gots_2[i][lax.rem(me + step, total), expert].astype(F32)
+            totals[i][expert] = held
+            return carry
+
+        lax.fori_loop(0, experts, close, 0)
+    for copy in rest:
+        copy.wait()
+
+
+def run_backward(cid, sizes, owns, others, y_terms, data):
+    queries, kv_all = data[:2]
+    tokens = queries.shape[1]
+    experts = owns[0].shape[0]
+    vmem = pl.BlockSpec(memory_space=pltpu.VMEM)
+    tiles = [own.shape[2:] for own in owns]
+    stage_1 = [(4, experts, 2, *tiles[0]), (4, experts, 2, *tiles[1]), (2, experts, 4, *tiles[2])]
+    stage_2 = [(2, experts, *tiles[0]), (2, experts, *tiles[1]), (4, experts, *tiles[2])]
+    sizes_of = [4, 4, 2, sizes["expert"], group_size(SEQ_AXES, sizes), sizes["context"], 2, 2, 4]
+    dma = pltpu.SemaphoreType.DMA
+    return pl.pallas_call(
+        functools.partial(backward_body, sizes),
+        out_shape=[
+            jax.ShapeDtypeStruct(y_terms.shape, BF16),
+            jax.ShapeDtypeStruct((kv_all.shape[0] // tokens, tokens, 2 * HEAD_DIM), BF16),
+            jax.ShapeDtypeStruct(queries.shape, F32),
+            *[jax.ShapeDtypeStruct((experts, *tile), F32) for tile in tiles],
+        ],
+        in_specs=[vmem] * 12,
+        out_specs=[vmem] * 6,
+        scratch_shapes=[
+            *[pltpu.VMEM(shape, BF16) for shape in stage_1 * 2 + stage_2 * 2],
+            pltpu.VMEM(queries.shape, F32),
+            pltpu.VMEM((kv_all.shape[0] // tokens, tokens, 2 * HEAD_DIM), BF16),
+            pltpu.VMEM(kv_all.shape, F32),
+            *[dma((n,)) for n in sizes_of for _ in range(2)],
+        ],
+        name="attention_backward",
+        compiler_params=pltpu.CompilerParams(
+            collective_id=cid, has_side_effects=True, vmem_limit_bytes=67_043_328
+        ),
+    )(*owns, *others, y_terms, *data)
 
 
 def moe_copies(sizes, refs):
@@ -566,6 +685,167 @@
     )(moe_all, grad_all, table_all, gate_weight, up_weight, down_weight)
 
 
+CHIP_AXES = ("dp", "side", "expert")
+
+
+def sum_body(sizes, *refs):
+    query_in, key_in, value_in, output_in, narrow_in = refs[:5]
+    query_out, key_out, value_out, output_out, narrow_out = refs[5:10]
+    load, near, sums, got, whole = refs[10:15]
+    near_send, near_recv, send_sems, recv_sems, give_sems, take_sems, pass_sems, land_sems = refs[15:]
+    core = lax.rem(lax.axis_index("context"), 2)
+    partner = {"context": lax.axis_index("context") + 1 - 2 * core}
+    me, total = own_index(CHIP_AXES, sizes), group_size(CHIP_AXES, sizes)
+    plane = total // sizes["dp"]
+    rows = load.shape[1]
+    some, wide = rows // 2, query_in.shape[1]
+    half = wide // 2
+
+    def place(step):
+        target = lax.rem(me + step, total)
+        return target, coords_of(CHIP_AXES, sizes, target)
+
+    def remote(src, dst, send, recv, peer):
+        return pltpu.make_async_remote_copy(
+            src_ref=src, dst_ref=dst, send_sem=send, recv_sem=recv, device_id=peer, device_id_type=MESH_ID
+        )
+
+    def reduce_copy(step):
+        target, peer = place(step)
+        return remote(sums.at[target], got.at[me], send_sems.at[step], recv_sems.at[step], peer)
+
+    def gather_copy(step):
+        _, peer = place(step)
+        own = whole.at[core, me]
+        return remote(own, own, give_sems.at[step], take_sems.at[step], peer)
+
+    def pass_copy(step):
+        source = whole.at[core, lax.rem(me - step + total, total)]
+        return remote(source, source, pass_sems.at[step], land_sems.at[step], partner)
+
+    def near_copy(turn):
+        chunks = pl.ds(lax.rem(lax.axis_index("dp") + turn, sizes["dp"]) * plane, plane)
+        return remote(load.at[chunks], near.at[chunks], near_send.at[turn], near_recv.at[turn], partner)
+
+    def each(start, stop, body):
+        def run(step, carry):
+            body(step)
+            return carry
+
+        lax.fori_loop(start, stop, run, 0)
+
+    def pack(number, chunk):
+        here = pl.ds(pl.multiple_of(chunk * rows, rows), rows)
+        there = pl.ds(pl.multiple_of(chunk * some, some), some)
+        if number == 0:
+            parts = [query_in[here, :]]
+        else:
+            parts = [key_in[here, :], value_in[here, :]]
+        start = number * wide
+        output = jnp.concatenate(
+            [output_in[there, start : start + half], output_in[there, start + half : start + wide]], axis=0
+        )
+        return jnp.concatenate([*parts, output, narrow_in[here, :]], axis=1)
+
+    def unpack(number, chunk):
+        here = pl.ds(pl.multiple_of(chunk * rows, rows), rows)
+        there = pl.ds(pl.multiple_of(chunk * some, some), some)
+        block = whole[number, chunk].astype(F32)
+        if number == 0:
+            query_out[here, :] = block[:, :wide]
+            narrow_out[here, :] = block[:, wide + half :]
+        else:
+            key_out[here, :] = block[:, :half]
+            value_out[here, :] = block[:, half:wide]
+        start = number * wide
+        output_out[there, start : start + half] = block[:some, wide : wide + half]
+        output_out[there, start + half : start + wide] = block[some:, wide : wide + half]
+
+    barrier = pltpu.get_barrier_semaphore()
+    pl.semaphore_signal(barrier, inc=1, device_id=partner, device_id_type=MESH_ID)
+    each(
+        1,
+        total,
+        lambda step: pl.semaphore_signal(
+            barrier, inc=1, device_id=place(step)[1], device_id_type=MESH_ID
+        ),
+    )
+    for number in range(2):
+
+        @pl.when(core == 1 - number)
+        def _(number=number):
+            def fill(chunk):
+                load[chunk] = pack(number, chunk).astype(BF16)
+
+            each(0, total, fill)
+
+    pl.semaphore_wait(barrier, total)
+    for turn in range(sizes["dp"]):
+        near_copy(turn).start()
+
+    for turn in range(sizes["dp"]):
+        near_copy(turn).wait()
+        base = lax.rem(lax.axis_index("dp") + turn, sizes["dp"]) * plane
+        for number in range(2):
+
+            @pl.when(core == number)
+            def _(number=number, base=base):
+                def add(chunk):
+                    sums[chunk] = (pack(number, chunk) + near[chunk].astype(F32)).astype(BF16)
+
+                each(base, base + plane, add)
+
+        def send(i, base=base):
+            target = base + lax.rem(me + i, plane)
+
+            @pl.when(target != me)
+            def _():
+                reduce_copy(lax.rem(target - me + total, total)).start()
+
+        each(0, plane, send)
+
+    got[me] = sums[me]
+    each(1, total, lambda step: reduce_copy(step).wait())
+    result = lax.fori_loop(
+        0, total, lambda i, held: held + got[i].astype(F32), jnp.zeros(got.shape[1:], F32)
+    )
+    whole[core, me] = result.astype(BF16)
+    each(1, total, lambda step: gather_copy(step).start())
+    pass_copy(0).start()
+
+    def forward(step):
+        gather_copy(step).wait_recv()
+        pass_copy(step).start()
+
+    each(1, total, forward)
+    each(1, total, lambda step: gather_copy(step).wait_send())
+    each(0, total, lambda step: pass_copy(step).wait())
+    for number in range(2):
+        each(0, total, functools.partial(unpack, number))
+
+
+def sum_everywhere(cid, sizes, *arrays):
+    total = group_size(CHIP_AXES, sizes)
+    depth, wide = arrays[0].shape
+    half = (total, depth // total, wide + wide // 2 + arrays[4].shape[1])
+    dma = pltpu.SemaphoreType.DMA
+    vmem = pl.BlockSpec(memory_space=pltpu.VMEM)
+    return pl.pallas_call(
+        functools.partial(sum_body, sizes),
+        out_shape=[jax.ShapeDtypeStruct(array.shape, F32) for array in arrays],
+        in_specs=[vmem] * 5,
+        out_specs=[vmem] * 5,
+        scratch_shapes=[pltpu.VMEM(half, BF16)] * 4
+        + [pltpu.VMEM((2, *half), BF16)]
+        + [dma((sizes["dp"],))] * 2
+        + [dma((total,))] * 6,
+        name="sum_everywhere",
+        compiler_params=pltpu.CompilerParams(
+            collective_id=cid, has_side_effects=True, vmem_limit_bytes=60_000_000
+        ),
+    )(*arrays)
+
+
 def rope_tables(positions, head_size):
     half_dim = head_size // 2
     frequency = ROPE_BASE ** (-2.0 * jnp.arange(half_dim, dtype=F32) / head_size)
@@ -598,15 +878,6 @@
     scaled = grad_out * gain_vec
     inner = jnp.mean(scaled * normed, axis=-1, keepdims=True)
     return (gain_grad, inverse * (scaled - normed * inner))
-
-
-def sum_others(received, own, index):
-    numbers = jnp.arange(received.shape[0]).reshape(-1, *([1] * own.ndim))
-    return own + jnp.sum(jnp.where(numbers == index, 0.0, received.astype(F32)), axis=0)
-
-
-def own_part(array, index):
-    return lax.dynamic_index_in_dim(array, index, 0, keepdims=False)
 
 
 def local(
@@ -681,15 +952,6 @@
     own_g, own_u, own_d, other_g, other_u, other_d, moe_terms, grad_back, dot_back = run_experts(
         3, sizes, moe_all, grad_all, table_all, gate_weight, up_weight, down_weight
     )
-    dp, side = lax.axis_index("dp"), context // 2
-
-    def chip_sum(own, other):
-        held = own + other.astype(F32)
-        return held.reshape(mine, sizes["dp"], 2, *held.shape[2:])
-
-    held_g = chip_sum(own_g, other_g).transpose(1, 0, 2, 3, 4)
-    held_u = chip_sum(own_u, other_u).transpose(1, 0, 2, 3, 4)
-    held_d = chip_sum(own_d, other_d).transpose(2, 0, 1, 3, 4)
     grad_gates = dot_back[:, :mine].reshape(EXPERTS, tokens)
     grad_logits = gates * (grad_gates - jnp.sum(gates * grad_gates, axis=0, keepdims=True))
     router_grad = jnp.einsum(
@@ -706,44 +968,15 @@
     grad_mix = dot_t(grad_after_half, output_weight).astype(BF16)
     grad_mix = grad_mix.reshape(tokens, KV_HEADS, 2 * HEAD_DIM).transpose(1, 0, 2)
     (grad_mixtures,) = exchange(4, sizes, "send_grad_mixture", (grad_mix, ("context",), pick_target))
-    got_g, got_u, got_d, moe_back, grad_queries, kv_terms = exchange(
+    moe_back, kv_back, grad_query, gate_sum, up_sum, down_sum = run_backward(
         8,
         sizes,
-        "attention_backward",
-        (held_g.astype(BF16), ("dp",), pick_target, True),
-        (held_u.astype(BF16), ("dp",), pick_target, True),
-        (held_d.astype(BF16), ("side",), pick_target, True),
-        (moe_terms, ("expert",), pick_target),
-        compute=attention_backward,
-        data=(queries, kv_all, mixtures, grad_mixtures, sums),
-        results=(
-            jax.ShapeDtypeStruct(queries.shape, F32),
-            jax.ShapeDtypeStruct(kv_all.shape, BF16),
-        ),
-        scratch=(pltpu.VMEM(kv_all.shape, F32),),
+        (own_g, own_u, own_d),
+        (other_g, other_u, other_d),
+        moe_terms,
+        (queries, kv_all, mixtures, grad_mixtures, sums),
     )
     outputs = (after_attn + jnp.sum(moe_back.astype(F32), axis=0)).astype(BF16)
-    half_g = sum_others(got_g, own_part(held_g, dp), dp).transpose(1, 0, 2, 3)
-    half_u = sum_others(got_u, own_part(held_u, dp), dp).transpose(1, 0, 2, 3)
-    half_d = sum_others(got_d, own_part(held_d, side), side).transpose(1, 0, 2, 3)
-    kv_terms = kv_terms.reshape(-1, tokens, 2 * HEAD_DIM)
-    output_grad, narrow = lax.psum(
-        (output_grad, jnp.concatenate([router_grad, midnorm_grad[:, None]], axis=1)), EVERY
-    )
-    kv_terms, output_grad, narrow = lax.optimization_barrier((kv_terms, output_grad, narrow))
-    kv_back, grad_query, got_g, got_u, got_d = exchange(
-        5,
-        sizes,
-        "send_grad_qkv",
-        (kv_terms, SEQ_AXES, pick_target),
-        (grad_queries, ("context",), pick_target),
-        (half_g.astype(BF16), ("side",), pick_target, True),
-        (half_u.astype(BF16), ("side",), pick_target, True),
-        (half_d.astype(BF16), ("dp",), pick_target, True),
-    )
-    gate_sum = sum_others(got_g, own_part(half_g, side), side)
-    up_sum = sum_others(got_u, own_part(half_u, side), side)
-    down_sum = sum_others(got_d, own_part(half_d, dp), dp)
     grad_kv = jnp.sum(kv_back.astype(F32).reshape(KV_HEADS, owners, tokens, 2 * HEAD_DIM), axis=1)
     grad_kv = grad_kv.transpose(1, 0, 2)
     grad_query = grad_query.transpose(1, 0, 2).reshape(tokens, HEADS, HEAD_DIM)
@@ -758,16 +991,18 @@
     )
     prenorm_grad, grad_inputs = norm_backward(grad_attn_in, normed_first, inverse_first, prenorm_gain)
     grad_inputs = grad_after + grad_inputs
-    query_grad, key_grad, value_grad, prenorm_grad = lax.psum(
-        (query_grad, key_grad, value_grad, jnp.pad(prenorm_grad[:, None], ((0, 0), (0, EXPERTS)))), EVERY
+    narrow = jnp.concatenate([router_grad, prenorm_grad[:, None], midnorm_grad[:, None]], axis=1)
+    narrow = jnp.pad(narrow, ((0, 0), (0, 128 - EXPERTS - 2)))
+    query_grad, key_grad, value_grad, output_grad, narrow = sum_everywhere(
+        9, sizes, query_grad, key_grad, value_grad, output_grad, narrow
     )
     dense = (
-        prenorm_grad[:, 0],
+        narrow[:, EXPERTS],
         query_grad,
         key_grad,
         value_grad,
         output_grad,
-        narrow[:, EXPERTS],
+        narrow[:, EXPERTS + 1],
         narrow[:, :EXPERTS],
     )
     return (outputs[None], grad_inputs[None], *dense, gate_sum, up_sum, down_sum)

time: 594 us -> 404 us (0.68)
  waiting for transfers between devices: 230 us -> 0 us
  Pallas kernels: 269 us -> 354 us
  other arithmetic: 37.4 us -> 11.6 us
  between operations: 15.1 us -> 1.52 us
    psum x2 -> x0, waiting for transfers between devices: 230 us -> none  [the longest x1 144 us: local(): lax.psum((query_grad, key_grad, value_grad, jnp.pad(prenorm_grad[:, None]...]
    pallas_call x0 -> x2, Pallas kernels: none -> 183 us  [the longest x1 99.7 us: run_backward(): pl.pallas_call(functools.partial(backward_body, sizes), out_shape=[jax.Sh...]
    pallas_call x7 -> x5, Pallas kernels: 211 us -> 112 us  [exchange(): pl.pallas_call(functools.partial(exchange_body, items, sizes, compute, le...]
    add x5 -> x0, other arithmetic: 12.3 us -> none  [the longest x2 8.58 us: chip_sum(): held = own + other.astype(F32)]
    convert_element_type x3 -> x0, other arithmetic: 7.24 us -> none  [the longest x1 2.62 us: local(): half_g.astype(BF16)]
    unnamed x123 -> x117, local copies, waits for them, and re-layouts: 14.4 us -> 15.5 us
  transfers between devices with their start and end apart: 2 -> 0, of which waited for: 2 -> 0; matrix products, arithmetic and copies ran while one was open for 6% -> 0% of each run, Pallas kernels for 12% -> 0%
where the time goes in v5:
time: 404 us
  Pallas kernels  354 us (88%)
  local copies, waits for them, and re-layouts  23.2 us (6%)
  matrix products  14 us (3%)
  other arithmetic  11.6 us (3%)
    pallas_call x5, Pallas kernels, exchange(): pl.pallas_call(functools.partial(exchange_body, items, sizes, compute, le...  112 us
    pallas_call x1, Pallas kernels, run_backward(): pl.pallas_call(functools.partial(backward_body, sizes), out_shape=[jax.Sh...  99.7 us
    pallas_call x1, Pallas kernels, sum_everywhere(): pl.pallas_call(functools.partial(sum_body, sizes), out_shape=[jax.ShapeDt...  83.6 us
    pallas_call x1, Pallas kernels, run_experts(): pl.pallas_call(functools.partial(moe_body, sizes), grid=(2 * mine + 1,),...  58.4 us
    unnamed x117, local copies, waits for them, and re-layouts  15.5 us

profile of v5, /device:TPU:1, one launch (start us, length us, event | category | flops | bytes accessed | tf_op | source)
XLA Modules:
  0.0 403.8 jit_solution(7420314363593299957)
XLA Ops:
  0.7 1.1 fusion.13
  3.2 1.3 copy.95
  4.5 1.4 fusion.26
  9.7 23.3 %send_qkv.1 = (bf16[32,128,128]{2,1,0:T(8,128)(2,1)}, bf16[4,128,128]{2,1,0:T(8,128)(2,1)}) custom-call(bf16[4,128,128]{2,1,0:T(8,128)(2,1)} %maximum_bitcast_fusion.refs_0_, bf16[4,128,128]{2,1,0:T(8,128)(2,1)} %bitcast.134), custom_call_target="tpu_custom_call" | custom-call | tf_op jit(solution)/shard_map/send_qkv/pallas_call | solution.py:149
  33.1 30.8 %attention_forward.1 = (bf16[8,128,1024]{2,1,0:T(8,128)(2,1)}, bf16[4,128,128]{2,1,0:T(8,128)(2,1)}, f32[4,1,256]{2,1,0:T(1,128)}) custom-call(bf16[128,1024]{1,0:T(8,128)(2,1)} %bitcast.127, bf16[4,128,128]{2,1,0:T(8,128)(2,1)} %get-tuple-element.39.refs_1_.refs_7_, bf16[4096,128]{1,0:T(8,128)(2,1)} %bitcast.117), custom_call_target="tpu_custom_call" | custom-call | tf_op jit(solution)/shard_map/attention_forward/pallas_call | solution.py:149
  63.9 8.8 %send_mixture.1 = bf16[4,128,128]{2,1,0:T(8,128)(2,1)} custom-call(bf16[4,128,128]{2,1,0:T(8,128)(2,1)} %get-tuple-element.41.refs_0_.refs_9_), custom_call_target="tpu_custom_call" | custom-call | tf_op jit(solution)/shard_map/send_mixture/pallas_call | solution.py:149
  76.0 42.1 %send_tokens.1 = (bf16[8,128,1024]{2,1,0:T(8,128)(2,1)}, f32[8,32,128]{2,1,0:T(8,128)}) custom-call(bf16[128,1024]{1,0:T(8,128)(2,1)} %copy-done.11, f32[32,128]{1,0:T(8,128)} %broadcast_select_fusion.refs_1_), custom_call_target="tpu_custom_call" | custom-call | tf_op jit(solution)/shard_map/send_tokens/pallas_call | solution.py:149
  118.2 58.4 %run_experts.1 = (f32[4,8,64,512]{3,2,1,0:T(8,128)}, f32[4,8,64,512]{3,2,1,0:T(8,128)}, f32[4,8,32,1024]{3,2,1,0:T(8,128)}, bf16[4,8,64,512]{3,2,1,0:T(8,128)(2,...) custom-call(bf16[8,128,1024]{2,1,0:T(8,128)(2,1)} %get-tuple-element, ...), custom_call_target="tpu_custom_call" | custom-call | tf_op jit(solution)/shard_map/run_experts/pallas_call | solution.py:631
  178.2 1.9 fusion.42
  180.1 2.1 convert_reduce_fusion.1
  182.2 1.2 multiply_reduce_fusion
  185.8 6.8 %send_grad_mixture.1.refs_10_ = bf16[4,128,128]{2,1,0:T(8,128)(2,1)} custom-call(bf16[4,128,128]{2,1,0:T(8,128)(2,1)} %bitcast.136), custom_call_target="tpu_custom_call" | custom-call | tf_op jit(solution)/shard_map/send_grad_mixture/pallas_call | solution.py:149
  192.6 99.7 %attention_backward.1 = (bf16[8,128,1024]{2,1,0:T(8,128)(2,1)}, bf16[32,128,128]{2,1,0:T(8,128)(2,1)}, f32[4,128,128]{2,1,0:T(8,128)}, f32[4,64,512]{2,1,0:T(8,1...) custom-call(f32[4,8,64,512]{3,2,1,0:T(8,128)} %get-tuple-element.45.refs_0_, ...), custom_call_target="tpu_custom_call" | custom-call | tf_op jit(solution)/shard_map/attention_backward/pallas_call | solution.py:350
  292.3 2.0 convert_reduce_fusion
  298.3 1.1 fusion.11
  300.5 1.4 fusion.30.refs_2_
  301.9 1.4 fusion.28.refs_1_
  303.2 1.7 fusion.34.refs_3_
  305.0 1.9 fusion.32.refs_0_
  306.8 83.6 %sum_everywhere.1 = (f32[1024,512]{1,0:T(8,128)}, f32[1024,256]{1,0:T(8,128)}, f32[1024,256]{1,0:T(8,128)}, f32[512,1024]{1,0:T(8,128)}, f32[1024,128]{1,0:T(8,128)}) custom-call(f32[1024,512]{1,0:T(8,128)} %fusion.32.refs_0_, f32[1024,256]{1,0:T(8,128)} %fusion.28.refs_1_, f32[1024,256]{1,0:T(8,128)} %fusion.30.refs_2_, f32[512,1024]{1,0:T(8,128)} %fusion.34.refs_3_, ...), custom_call_target="tpu_custom_call" | custom-call | tf_op jit(solution)/shard_map/sum_everywhere/pallas_call | solution.py:833
  390.4 2.5 slice_reduce_fusion
  392.9 1.9 copy.113
  394.8 3.2 copy.122
  400.0 1.3 copy.125
  (163 shorter events, 21.5 us)
Async XLA Ops:
  0.6 5.5 %copy-start = (bf16[1,128,1024]{2,1,0:T(8,128)(2,1)S(1)}, bf16[1,128,1024]{2,1,0:T(8,128)(2,1)}, u32[]{:S(2)}) copy-start(bf16[1,128,1024]{2,1,0:T(8,128)(2,1)} %param.13) | copy-start | bytes 786436
  0.7 5.5 %copy-start.40 = (f32[1024]{0:T(1024)S(1)}, f32[1024]{0:T(1024)}, u32[]{:S(2)}) copy-start(f32[1024]{0:T(1024)} %param.14) | copy-start | bytes 12292
  0.7 5.2 %copy-start.14 = (bf16[1024,256]{1,0:T(8,128)(2,1)S(1)}, bf16[1024,256]{1,0:T(8,128)(2,1)}, u32[]{:S(2)}) copy-start(bf16[1024,256]{1,0:T(8,128)(2,1)} %param.17) | copy-start | bytes 1572868
  1.9 6.4 %copy-start.46 = (f32[128]{0:T(128)}, f32[128]{0:T(128)S(1)}, u32[]{:S(2)}) copy-start(f32[128]{0:T(128)S(1)} %add_rsqrt_fusion.1) | copy-start | bytes 1540
  3.0 3.8 copy-start.18
  3.0 3.8 copy-start.24
  3.1 5.8 %copy-start.33 = (f32[128,64]{0,1:T(8,128)}, f32[128,64]{0,1:T(8,128)S(1)}, u32[]{:S(2)}) copy-start(f32[128,64]{0,1:T(8,128)S(1)} %copy.102) | copy-start | bytes 98308
  3.2 5.7 %copy-start.35 = (f32[128,64]{0,1:T(8,128)}, f32[128,64]{0,1:T(8,128)S(1)}, u32[]{:S(2)}) copy-start(f32[128,64]{0,1:T(8,128)S(1)} %copy.103) | copy-start | bytes 98308
  8.8 64.9 %copy-start.9 = (bf16[512,1024]{1,0:T(8,128)(2,1)S(1)}, bf16[512,1024]{1,0:T(8,128)(2,1)}, u32[]{:S(2)}) copy-start(bf16[512,1024]{1,0:T(8,128)(2,1)} %param.18) | copy-start | bytes 3145732
  9.7 65.3 %copy-start.42 = (f32[1024]{0:T(1024)S(1)}, f32[1024]{0:T(1024)}, u32[]{:S(2)}) copy-start(f32[1024]{0:T(1024)} %param.19) | copy-start | bytes 12292
  33.1 42.1 %copy-start.38 = (bf16[1024,32]{0,1:T(8,128)(2,1)S(1)}, bf16[1024,32]{0,1:T(8,128)(2,1)}, u32[]{:S(2)}) copy-start(bf16[1024,32]{0,1:T(8,128)(2,1)} %param.20) | copy-start | bytes 196612
  73.8 44.4 %copy-start.16 = (bf16[128,4,128]{0,2,1:T(8,128)(2,1)}, bf16[128,4,128]{0,2,1:T(8,128)(2,1)S(1)}, u32[]{:S(2)}) copy-start(bf16[128,4,128]{0,2,1:T(8,128)(2,1)S(1)} %copy.105) | copy-start | bytes 393220
  75.0 43.2 %copy-start.51 = (f32[128]{0:T(128)}, f32[128]{0:T(128)S(1)}, u32[]{:S(2)}) copy-start(f32[128]{0:T(128)S(1)} %add_rsqrt_fusion) | copy-start | bytes 1540
  75.3 42.8 %copy-start.26 = (f32[32,128]{1,0:T(8,128)}, f32[32,128]{1,0:T(8,128)S(1)}, u32[]{:S(2)}) copy-start(f32[32,128]{1,0:T(8,128)S(1)} %get-tuple-element.147) | copy-start | bytes 49156
  75.4 42.8 %copy-start.44 = (f32[128]{0:T(128)}, f32[128]{0:T(128)S(1)}, u32[]{:S(2)}) copy-start(f32[128]{0:T(128)S(1)} %get-tuple-element.146) | copy-start | bytes 1540
  75.4 42.8 %copy-start.49 = (f32[128]{0:T(128)}, f32[128]{0:T(128)S(1)}, u32[]{:S(2)}) copy-start(f32[128]{0:T(128)S(1)} %fusion.41) | copy-start | bytes 1540
  176.6 5.6 %copy-start.3 = (f32[128,1024]{1,0:T(8,128)S(1)}, f32[128,1024]{1,0:T(8,128)}, u32[]{:S(2)}) copy-start(f32[128,1024]{1,0:T(8,128)} %copy-done.2) | copy-start | bytes 1572868
  176.6 5.6 %copy-start.27 = (f32[32,128]{1,0:T(8,128)S(1)}, f32[32,128]{1,0:T(8,128)}, u32[]{:S(2)}) copy-start(f32[32,128]{1,0:T(8,128)} %copy-done.26) | copy-start | bytes 49156
  176.6 5.6 %copy-start.39 = (bf16[1024,32]{0,1:T(8,128)(2,1)S(1)}, bf16[1024,32]{0,1:T(8,128)(2,1)}, u32[]{:S(2)}) copy-start(bf16[1024,32]{0,1:T(8,128)(2,1)} %param.20) | copy-start | bytes 196612
  176.6 5.6 %copy-start.43 = (f32[1024]{0:T(1024)S(1)}, f32[1024]{0:T(1024)}, u32[]{:S(2)}) copy-start(f32[1024]{0:T(1024)} %param.19) | copy-start | bytes 12292
  176.6 5.6 %copy-start.45 = (f32[128]{0:T(128)S(1)}, f32[128]{0:T(128)}, u32[]{:S(2)}) copy-start(f32[128]{0:T(128)} %copy-done.44) | copy-start | bytes 1540
  176.6 5.6 %copy-start.50 = (f32[128]{0:T(128)S(1)}, f32[128]{0:T(128)}, u32[]{:S(2)}) copy-start(f32[128]{0:T(128)} %copy-done.49) | copy-start | bytes 1540
  176.6 5.6 %copy-start.52 = (f32[128]{0:T(128)S(1)}, f32[128]{0:T(128)}, u32[]{:S(2)}) copy-start(f32[128]{0:T(128)} %copy-done.51) | copy-start | bytes 1540
  394.8 4.2 %copy-start.21 = (f32[1024,256]{1,0:T(8,128)S(1)}, f32[1024,256]{1,0:T(8,128)}, u32[]{:S(2)}) copy-start(f32[1024,256]{1,0:T(8,128)} %get-tuple-element.169) | copy-start | bytes 3145732
  (29 other events, 50.0 us)

commit v6 on v5

--- a/solution.py
+++ b/solution.py
@@ -193,13 +193,16 @@
         def keys_of(j):
             return pl.ds(pl.multiple_of(j * chunk, chunk), chunk)
 
+        def kv_of(j):
+            return kv_ref[pl.ds(j * 8, 8)].reshape(chunk, 2 * HEAD_DIM)
+
         def first(j, top):
-            scores = dot_t(kv_ref[keys_of(j), :], rows)
+            scores = dot_t(kv_of(j), rows)
             score_ref[keys_of(j), :] = scores
             return jnp.maximum(top, jnp.max(scores, axis=0, keepdims=True))
 
         top = lax.fori_loop(0, number, first, jnp.full((1, columns), -jnp.inf, F32))
-        scores = dot_t(kv_ref[keys_of(number), :], rows)
+        scores = dot_t(kv_of(number), rows)
         scores = jnp.where(causal(scores.shape, tokens), scores, -jnp.inf)
         score_ref[keys_of(number), :] = scores
         top = jnp.maximum(top, jnp.max(scores, axis=0, keepdims=True))
@@ -208,7 +211,7 @@
             total, mixed = held
             powers = jnp.exp(score_ref[keys_of(j), :] - top)
             total = total + jnp.sum(powers, axis=0, keepdims=True)
-            return total, mixed + t_dot(powers.astype(BF16), kv_ref[keys_of(j), :])
+            return total, mixed + t_dot(powers.astype(BF16), kv_of(j))
 
         start = (jnp.zeros((1, columns), F32), jnp.zeros((columns, 2 * HEAD_DIM), F32))
         total, mixed = lax.fori_loop(0, number + 1, second, start)
@@ -240,7 +243,7 @@
 
         def unit(j, total, masked):
             keys = pl.ds(pl.multiple_of(j * chunk, chunk), chunk)
-            kv = kv_ref[keys, :]
+            kv = kv_ref[pl.ds(j * 8, 8)].reshape(chunk, 2 * HEAD_DIM)
             products = dot_t(kv, both)
             soft = jnp.exp(products[:, :columns] - logsum)
             if masked:
@@ -258,6 +261,50 @@
 
     lax.fori_loop(0, blocks, block, 0)
     terms_ref[...] = sum_kv[...].astype(BF16).reshape(terms_ref.shape)
+
+
+def forward_body(sizes, *refs):
+    kv_send, query_send, grad_ref = refs[:3]
+    kv_all, queries, grad_all, mixtures, sums, mixture_back = refs[3:9]
+    sems, scores = refs[9:17], refs[17]
+    greet([SEQ_AXES], sizes)
+    early = launch(sizes, ("context",), pick_target, True, query_send, queries, *sems[0:2])
+    early += launch(sizes, SEQ_AXES, pick_context, True, kv_send, kv_all, *sems[2:4])
+    late = launch(sizes, ("expert",), pick_whole, True, grad_ref, grad_all, *sems[4:6])
+    for copy in early:
+        copy.wait()
+    attention_forward((queries, kv_all), (mixtures, sums), (scores,))
+    late += launch(sizes, ("context",), pick_target, True, mixtures, mixture_back, *sems[6:8])
+    for copy in late:
+        copy.wait()
+
+
+def run_forward(cid, sizes, kv_send, query_send, cotangent):
+    heads, tokens, columns = query_send.shape
+    total, owners = group_size(SEQ_AXES, sizes), sizes["expert"]
+    vmem = pl.BlockSpec(memory_space=pltpu.VMEM)
+    dma = pltpu.SemaphoreType.DMA
+    return pl.pallas_call(
+        functools.partial(forward_body, sizes),
+        out_shape=[
+            jax.ShapeDtypeStruct((total, tokens, columns), BF16),
+            jax.ShapeDtypeStruct(query_send.shape, BF16),
+            jax.ShapeDtypeStruct((owners, *cotangent.shape), BF16),
+            jax.ShapeDtypeStruct(query_send.shape, BF16),
+            jax.ShapeDtypeStruct((heads, 1, 2 * tokens), F32),
+            jax.ShapeDtypeStruct(query_send.shape, BF16),
+        ],
+        in_specs=[vmem] * 3,
+        out_specs=[vmem] * 6,
+        scratch_shapes=[
+            *[dma((n,)) for n in (heads, total, owners, heads) for _ in range(2)],
+            pltpu.VMEM((total * tokens, 2 * tokens), F32),
+        ],
+        name="attention_forward",
+        compiler_params=pltpu.CompilerParams(
+            collective_id=cid, has_side_effects=True, vmem_limit_bytes=60_000_000
+        ),
+    )(kv_send, query_send, cotangent)
 
 
 def backward_body(sizes, *refs):
@@ -351,7 +398,7 @@
         functools.partial(backward_body, sizes),
         out_shape=[
             jax.ShapeDtypeStruct(y_terms.shape, BF16),
-            jax.ShapeDtypeStruct((kv_all.shape[0] // tokens, tokens, 2 * HEAD_DIM), BF16),
+            jax.ShapeDtypeStruct(kv_all.shape, BF16),
             jax.ShapeDtypeStruct(queries.shape, F32),
             *[jax.ShapeDtypeStruct((experts, *tile), F32) for tile in tiles],
         ],
@@ -360,8 +407,8 @@
         scratch_shapes=[
             *[pltpu.VMEM(shape, BF16) for shape in stage_1 * 2 + stage_2 * 2],
             pltpu.VMEM(queries.shape, F32),
-            pltpu.VMEM((kv_all.shape[0] // tokens, tokens, 2 * HEAD_DIM), BF16),
-            pltpu.VMEM(kv_all.shape, F32),
+            pltpu.VMEM(kv_all.shape, BF16),
+            pltpu.VMEM((kv_all.shape[0] * tokens, 2 * HEAD_DIM), F32),
             *[dma((n,)) for n in sizes_of for _ in range(2)],
         ],
         name="attention_backward",
@@ -372,24 +419,37 @@
 
 
 def moe_copies(sizes, refs):
-    d_send, d_back, dots, dot_back, g_sends, g_backs, sems = refs
+    moe_ref, table_ref, moe_land, table_land, d_send, d_back, dots, dot_back, g_sends, g_backs, sems = refs
     owners = sizes["expert"]
     owner, context = lax.axis_index("expert"), lax.axis_index("context")
 
-    def results(step):
-        target = lax.rem(owner + step, owners)
-        pairs = ((d_send, d_back, sems[0], sems[1]), (dots, dot_back, sems[2], sems[3]))
+    def pair_of(copies, target, number):
         return [
             pltpu.make_async_remote_copy(
-                src_ref=src.at[target],
-                dst_ref=dst.at[owner],
-                send_sem=send.at[step],
-                recv_sem=recv.at[step],
+                src_ref=src,
+                dst_ref=dst,
+                send_sem=send.at[number],
+                recv_sem=recv.at[number],
                 device_id={"expert": target},
                 device_id_type=MESH_ID,
             )
-            for src, dst, send, recv in pairs
+            for src, dst, send, recv in copies
         ]
+
+    def tokens_to(number):
+        pairs = (
+            (table_ref, table_land.at[number], sems[7], sems[8]),
+            (moe_ref, moe_land.at[number], sems[9], sems[10]),
+        )
+        return pair_of(pairs, lax.rem(owner + number, owners), number)
+
+    def results_of(number):
+        target = lax.rem(owner + owners - number, owners)
+        pairs = (
+            (d_send.at[target], d_back.at[owner], sems[0], sems[1]),
+            (dots.at[target], dot_back.at[owner], sems[2], sems[3]),
+        )
+        return pair_of(pairs, target, number)
 
     def own_results():
         return [
@@ -411,14 +471,14 @@
             for i in range(3)
         ]
 
-    return results, own_results, halves
+    return tokens_to, results_of, own_results, halves
 
 
 def moe_body(
     sizes,
     moe_ref,
+    table_ref,
     grad_ref,
-    table_ref,
     wg_ref,
     wu_ref,
     wd_ref,
@@ -431,6 +491,8 @@
     y_out,
     d_back,
     dot_back,
+    moe_land,
+    table_land,
     x_all,
     g_now,
     deo_all,
@@ -456,52 +518,87 @@
     owner, context = lax.axis_index("expert"), lax.axis_index("context")
     core = lax.rem(context, 2)
     mine = 4
-    tokens, width = moe_ref.shape[1:]
+    group = owners // 2
+    tokens, width = moe_ref.shape
     hidden_width = wg_ref.shape[2]
-    rows = owners * CAP
-    tile = rows // 2
+    rows = group * CAP
     barrier = pltpu.get_barrier_semaphore()
-    results, own_results, halves = moe_copies(
-        sizes, (d_send, d_back, dots, dot_back, (send_g, send_u, send_d), (back_g, back_u, back_d), sems)
+    tokens_to, results_of, own_results, halves = moe_copies(
+        sizes,
+        (
+            moe_ref,
+            table_ref,
+            moe_land,
+            table_land,
+            d_send,
+            d_back,
+            dots,
+            dot_back,
+            (send_g, send_u, send_d),
+            (back_g, back_u, back_d),
+            sems,
+        ),
     )
 
     @pl.when(step == 0)
     def _():
-        for shift_by in range(1, owners):
+        for number in range(1, owners):
             pl.semaphore_signal(
                 barrier,
                 inc=1,
-                device_id={"expert": lax.rem(owner + shift_by, owners)},
+                device_id={"expert": lax.rem(owner + number, owners)},
                 device_id_type=MESH_ID,
             )
         pl.semaphore_signal(
             barrier, inc=1, device_id={"context": context + 1 - 2 * core}, device_id_type=MESH_ID
         )
+        pl.semaphore_wait(barrier, owners)
+        for number in range(1, owners):
+            for copy in tokens_to(number):
+                copy.start()
         dots[...] = jnp.zeros_like(dots)
-
-    @pl.when(step == 4)
+        moe_land[0] = moe_ref[...]
+        table_land[0] = table_ref[...]
+        for number in range(1, group):
+            for copy in tokens_to(number):
+                copy.wait_recv()
+
+    @pl.when(step == mine)
     def _():
-        pl.semaphore_wait(barrier, owners)
-        for shift_by in range(1, owners):
-            for copy in results(shift_by):
-                copy.start()
         for copy in own_results():
             copy.start()
+        for number in range(1, group):
+            for copy in results_of(number):
+                copy.start()
+        for number in range(group, owners):
+            for copy in tokens_to(number):
+                copy.wait_recv()
+
+    @pl.when(step == 2 * mine)
+    def _():
+        for number in range(group, owners):
+            for copy in results_of(number):
+                copy.start()
         pltpu.make_async_copy(y_send, y_out, sems[6].at[0]).start()
 
     for number in range(mine):
 
-        @pl.when(step == 5 + number)
+        @pl.when(step == 2 * mine + 1 + number)
         def _(number=number):
             for copy in halves(number):
                 copy.start()
 
-    @pl.when(step < mine)
+    @pl.when(step < 2 * mine)
     def _():
-        place = pl.multiple_of(step * CAP, CAP)
+        expert, tile = lax.rem(step, mine), step // mine
+        place = pl.multiple_of(expert * CAP, CAP)
+        spot = pl.ds(place, CAP)
+        here = pl.ds(pl.multiple_of(tile * rows, rows), rows)
+        part = pl.ds(tile * group, group)
         table = jnp.concatenate(
-            [table_ref[s, pl.ds(owner * mine + step, 1), :] for s in range(owners)], axis=0
+            [table_land[tile * group + j, pl.ds(owner * mine + expert, 1), :] for j in range(group)], axis=0
         )
+        table = jnp.concatenate([table, table], axis=0)
         named = table >= 0.0
         above = lax.broadcasted_iota(jnp.int32, (tokens, tokens), 0)
         beside = lax.broadcasted_iota(jnp.int32, (tokens, tokens), 1)
@@ -509,64 +606,65 @@
         slots = dot(named.astype(F32).astype(BF16), before)
         slots = jnp.where(named, slots, -1.0)
         counts = lax.broadcasted_iota(jnp.int32, (CAP, tokens), 0).astype(F32)
-        for s in range(owners):
-            chosen = counts == slots[s : s + 1]
+        for j in range(group):
+            position = tile * group + j
+            source = lax.rem(owner + owners - position, owners)
+            chosen = counts == slots[j : j + 1]
             onehot = jnp.where(chosen, 1.0, 0.0).astype(BF16)
-            weight = jnp.where(chosen, table[s : s + 1], 0.0)
+            weight = jnp.where(chosen, table[j : j + 1], 0.0)
             high = weight.astype(BF16)
-            picks[s, pl.ds(place, CAP), :] = onehot
-            highs[s, pl.ds(place, CAP), :] = high
-            lows[s, pl.ds(place, CAP), :] = (weight - high.astype(F32)).astype(BF16)
-            gate_col[s * CAP : (s + 1) * CAP, :] = jnp.sum(weight, axis=1, keepdims=True)
-            x_all[step, s * CAP : (s + 1) * CAP, :] = dot(onehot, moe_ref[s]).astype(BF16)
-            g_now[s * CAP : (s + 1) * CAP, :] = dot(onehot, grad_ref[s]).astype(BF16)
-
-        def run_tile(r, carry):
-            here = pl.ds(pl.multiple_of(r * tile, tile), tile)
-            part = pl.ds(r * (owners // 2), owners // 2)
-            spot = pl.ds(place, CAP)
-            rows_in = x_all[step, here, :]
-            gate_act = dot(rows_in, wg_ref[0])
-            up_act = dot(rows_in, wu_ref[0])
-            sigma = jax.nn.sigmoid(gate_act)
-            silu = gate_act * sigma
-            hidden = (silu * up_act).astype(BF16)
-            eh_all[step, here, :] = hidden
-            expert_out = dot(hidden, wd_ref[0]).astype(BF16)
-            eo_all[part, spot, :] = expert_out.reshape(owners // 2, CAP, width)
-            grads = g_now[here, :].astype(F32)
-            dot_col[here, :] = jnp.sum(grads * expert_out.astype(F32), axis=1, keepdims=True)
-            grad_expert = (gate_col[here, :] * grads).astype(BF16)
-            deo_all[step, here, :] = grad_expert
-            grad_hidden = dot_t(grad_expert, wd_ref[0])
-            slope = sigma * (1.0 + gate_act * (1.0 - sigma))
-            grad_gate = (grad_hidden * up_act * slope).astype(BF16)
-            grad_up = (grad_hidden * silu).astype(BF16)
-            dgu_all[step, here, :hidden_width] = grad_gate
-            dgu_all[step, here, hidden_width:] = grad_up
-            grad_buffer = (dot_t(grad_gate, wg_ref[0]) + dot_t(grad_up, wu_ref[0])).astype(BF16)
-            dbuf_all[part, spot, :] = grad_buffer.reshape(owners // 2, CAP, width)
-            return carry
-
-        lax.fori_loop(0, 2, run_tile, 0)
-        for s in range(owners):
-            onehot = picks[s, pl.ds(place, CAP), :].astype(F32)
-            line = jnp.sum(onehot * dot_col[s * CAP : (s + 1) * CAP, :], axis=0, keepdims=True)
-            dots[s, pl.ds(step, 1), :] = line
-
-    @pl.when(step == mine - 1)
+            picks[position, spot, :] = onehot
+            highs[position, spot, :] = high
+            lows[position, spot, :] = (weight - high.astype(F32)).astype(BF16)
+            gate_col[j * CAP : (j + 1) * CAP, :] = jnp.sum(weight, axis=1, keepdims=True)
+            line = pl.ds(pl.multiple_of(tile * rows + j * CAP, CAP), CAP)
+            x_all[expert, line, :] = dot(onehot, moe_land[position]).astype(BF16)
+            g_now[j * CAP : (j + 1) * CAP, :] = dot(onehot, grad_ref[source]).astype(BF16)
+
+        rows_in = x_all[expert, here, :]
+        gate_act = dot(rows_in, wg_ref[0])
+        up_act = dot(rows_in, wu_ref[0])
+        sigma = jax.nn.sigmoid(gate_act)
+        silu = gate_act * sigma
+        hidden = (silu * up_act).astype(BF16)
+        eh_all[expert, here, :] = hidden
+        expert_out = dot(hidden, wd_ref[0]).astype(BF16)
+        eo_all[part, spot, :] = expert_out.reshape(group, CAP, width)
+        grads = g_now[...].astype(F32)
+        dot_col[...] = jnp.sum(grads * expert_out.astype(F32), axis=1, keepdims=True)
+        grad_expert = (gate_col[...] * grads).astype(BF16)
+        deo_all[expert, here, :] = grad_expert
+        grad_hidden = dot_t(grad_expert, wd_ref[0])
+        slope = sigma * (1.0 + gate_act * (1.0 - sigma))
+        grad_gate = (grad_hidden * up_act * slope).astype(BF16)
+        grad_up = (grad_hidden * silu).astype(BF16)
+        dgu_all[expert, here, :hidden_width] = grad_gate
+        dgu_all[expert, here, hidden_width:] = grad_up
+        grad_buffer = (dot_t(grad_gate, wg_ref[0]) + dot_t(grad_up, wu_ref[0])).astype(BF16)
+        dbuf_all[part, spot, :] = grad_buffer.reshape(group, CAP, width)
+        for j in range(group):
+            position = tile * group + j
+            source = lax.rem(owner + owners - position, owners)
+            onehot = picks[position, spot, :].astype(F32)
+            dots[source, pl.ds(expert, 1), :] = jnp.sum(
+                onehot * dot_col[j * CAP : (j + 1) * CAP, :], axis=0, keepdims=True
+            )
+
+        @pl.when(expert == mine - 1)
+        def _():
+            def combine(j, carry):
+                position = tile * group + j
+                source = lax.rem(owner + owners - position, owners)
+                d_send[source] = t_dot(picks[position], dbuf_all[position]).astype(BF16)
+                moved = t_dot(highs[position], eo_all[position]) + t_dot(lows[position], eo_all[position])
+                y_send[source] = moved.astype(BF16)
+                return carry
+
+            lax.fori_loop(0, group, combine, 0)
+
+    @pl.when((step >= 2 * mine) & (step < 3 * mine))
     def _():
-        def combine(s, carry):
-            moved = t_dot(highs[s], eo_all[s]) + t_dot(lows[s], eo_all[s])
-            y_send[s] = moved.astype(BF16)
-            d_send[s] = t_dot(picks[s], dbuf_all[s]).astype(BF16)
-            return carry
-
-        lax.fori_loop(0, owners, combine, 0)
-
-    @pl.when((step >= mine) & (step < 2 * mine))
-    def _():
-        number = step - mine
+        number = step - 2 * mine
         blocks = width // 256
         per = width // 16
 
@@ -577,9 +675,9 @@
                 grads = dgu_all[number, :, half * hidden_width : (half + 1) * hidden_width]
                 terms = t_dot(rows_in, grads).reshape(128 // per, 2, per, hidden_width)
                 first, second = terms[:, 0], terms[:, 1]
-                group = pl.ds(j * (128 // per), 128 // per)
-                own[0, group] = jnp.where(core == 0, first, second)
-                send[number, group] = jnp.where(core == 0, second, first).astype(BF16)
+                places = pl.ds(j * (128 // per), 128 // per)
+                own[0, places] = jnp.where(core == 0, first, second)
+                send[number, places] = jnp.where(core == 0, second, first).astype(BF16)
             return carry
 
         lax.fori_loop(0, blocks, gate_rows, 0)
@@ -590,17 +688,19 @@
             terms = t_dot(eh_all[number, :, columns], deo_all[number])
             terms = terms.reshape(128 // less, 2, less, width)
             first, second = terms[:, 0], terms[:, 1]
-            group = pl.ds(j * (128 // less), 128 // less)
-            own_d[0, group] = jnp.where(core == 0, first, second)
-            send_d[number, group] = jnp.where(core == 0, second, first).astype(BF16)
+            places = pl.ds(j * (128 // less), 128 // less)
+            own_d[0, places] = jnp.where(core == 0, first, second)
+            send_d[number, places] = jnp.where(core == 0, second, first).astype(BF16)
             return carry
 
         lax.fori_loop(0, hidden_width // 256, down_rows, 0)
 
-    @pl.when(step == 2 * mine)
+    @pl.when(step == 3 * mine)
     def _():
-        for shift_by in range(1, owners):
-            for copy in results(shift_by):
+        for number in range(1, owners):
+            for copy in tokens_to(number):
+                copy.wait_send()
+            for copy in results_of(number):
                 copy.wait()
         for copy in own_results():
             copy.wait()
@@ -610,27 +710,27 @@
                 copy.wait()
 
 
-def run_experts(cid, sizes, moe_all, grad_all, table_all, gate_weight, up_weight, down_weight):
-    owners, tokens, width = moe_all.shape
+def run_experts(cid, sizes, moe_input, table, grad_all, gate_weight, up_weight, down_weight):
+    owners, tokens, width = grad_all.shape
     mine, _, inner = gate_weight.shape
     rows = owners * CAP
     part, less = width // 16, inner // 16
 
     def fixed(array):
-        return pl.BlockSpec(array.shape, lambda i: (0, 0, 0), pipeline_mode=pl.Buffered(1))
+        return pl.BlockSpec(array.shape, lambda i: (0,) * array.ndim, pipeline_mode=pl.Buffered(1))
 
     def expert_block(array):
-        return pl.BlockSpec((1, *array.shape[1:]), lambda i: (jnp.minimum(i, mine - 1), 0, 0))
+        return pl.BlockSpec((1, *array.shape[1:]), lambda i: (lax.rem(jnp.minimum(i, 2 * mine - 1), mine), 0, 0))
 
     def own_block(*shape):
-        return pl.BlockSpec((1, *shape), lambda i: (jnp.clip(i - mine, 0, mine - 1), 0, 0, 0))
+        return pl.BlockSpec((1, *shape), lambda i: (jnp.clip(i - 2 * mine, 0, mine - 1), 0, 0, 0))
 
     anywhere = pl.BlockSpec(memory_space=pl.ANY)
     wide, tall = (8, part, inner), (8, less, width)
     dma = pltpu.SemaphoreType.DMA
     return pl.pallas_call(
         functools.partial(moe_body, sizes),
-        grid=(2 * mine + 1,),
+        grid=(3 * mine + 1,),
         out_shape=[
             jax.ShapeDtypeStruct((mine, *wide), F32),
             jax.ShapeDtypeStruct((mine, *wide), F32),
@@ -643,17 +743,19 @@
             jax.ShapeDtypeStruct((owners, 8, tokens), F32),
         ],
         in_specs=[
-            fixed(moe_all),
+            fixed(moe_input),
+            fixed(table),
             fixed(grad_all),
-            fixed(table_all),
             expert_block(gate_weight),
             expert_block(up_weight),
             expert_block(down_weight),
         ],
         out_specs=[own_block(*wide), own_block(*wide), own_block(*tall), *([anywhere] * 6)],
         scratch_shapes=[
+            pltpu.VMEM(grad_all.shape, BF16),
+            pltpu.VMEM((owners, *table.shape), F32),
             pltpu.VMEM((mine, rows, width), BF16),
-            pltpu.VMEM((rows, width), BF16),
+            pltpu.VMEM((rows // 2, width), BF16),
             pltpu.VMEM((mine, rows, width), BF16),
             pltpu.VMEM((mine, rows, 2 * inner), BF16),
             pltpu.VMEM((mine, rows, inner), BF16),
@@ -662,8 +764,8 @@
             pltpu.VMEM((owners, mine * CAP, tokens), BF16),
             pltpu.VMEM((owners, mine * CAP, tokens), BF16),
             pltpu.VMEM((owners, mine * CAP, tokens), BF16),
-            pltpu.VMEM((rows, 1), F32),
-            pltpu.VMEM((rows, 1), F32),
+            pltpu.VMEM((rows // 2, 1), F32),
+            pltpu.VMEM((rows // 2, 1), F32),
             pltpu.VMEM((owners, 8, tokens), F32),
             pltpu.VMEM((owners, tokens, width), BF16),
             pltpu.VMEM((owners, tokens, width), BF16),
@@ -677,12 +779,13 @@
             dma((3 * mine,)),
             dma((3 * mine,)),
             dma((1,)),
+            *[dma((owners,))] * 4,
         ],
         name="run_experts",
         compiler_params=pltpu.CompilerParams(
             collective_id=cid, has_side_effects=True, vmem_limit_bytes=67_043_328
         ),
-    )(moe_all, grad_all, table_all, gate_weight, up_weight, down_weight)
+    )(moe_input, table, grad_all, gate_weight, up_weight, down_weight)
 
 
 CHIP_AXES = ("dp", "side", "expert")
@@ -690,9 +793,8 @@
 
 def sum_body(sizes, *refs):
     query_in, key_in, value_in, output_in, narrow_in = refs[:5]
-    query_out, key_out, value_out, output_out, narrow_out = refs[5:10]
-    load, near, sums, got, whole = refs[10:15]
-    near_send, near_recv, send_sems, recv_sems, give_sems, take_sems, pass_sems, land_sems = refs[15:]
+    whole, load, near, sums, got = refs[5:10]
+    near_send, near_recv, send_sems, recv_sems, give_sems, take_sems, pass_sems, land_sems = refs[10:]
     core = lax.rem(lax.axis_index("context"), 2)
     partner = {"context": lax.axis_index("context") + 1 - 2 * core}
     me, total = own_index(CHIP_AXES, sizes), group_size(CHIP_AXES, sizes)
@@ -747,20 +849,6 @@
         )
         return jnp.concatenate([*parts, output, narrow_in[here, :]], axis=1)
 
-    def unpack(number, chunk):
-        here = pl.ds(pl.multiple_of(chunk * rows, rows), rows)
-        there = pl.ds(pl.multiple_of(chunk * some, some), some)
-        block = whole[number, chunk].astype(F32)
-        if number == 0:
-            query_out[here, :] = block[:, :wide]
-            narrow_out[here, :] = block[:, wide + half :]
-        else:
-            key_out[here, :] = block[:, :half]
-            value_out[here, :] = block[:, half:wide]
-        start = number * wide
-        output_out[there, start : start + half] = block[:some, wide : wide + half]
-        output_out[there, start + half : start + wide] = block[some:, wide : wide + half]
-
     barrier = pltpu.get_barrier_semaphore()
     pl.semaphore_signal(barrier, inc=1, device_id=partner, device_id_type=MESH_ID)
     each(
@@ -820,8 +908,26 @@
     each(1, total, forward)
     each(1, total, lambda step: gather_copy(step).wait_send())
     each(0, total, lambda step: pass_copy(step).wait())
-    for number in range(2):
-        each(0, total, functools.partial(unpack, number))
+
+
+def unpack_body(whole, query_out, key_out, value_out, output_out, narrow_out):
+    chunks, rows = whole.shape[1:3]
+    some, wide = rows // 2, query_out.shape[1]
+    half = wide // 2
+    for chunk in range(chunks):
+        here = slice(chunk * rows, (chunk + 1) * rows)
+        there = slice(chunk * some, (chunk + 1) * some)
+        for number in range(2):
+            block = whole[number, chunk].astype(F32)
+            if number == 0:
+                query_out[here, :] = block[:, :wide]
+                narrow_out[here, :] = block[:, wide + half :]
+            else:
+                key_out[here, :] = block[:, :half]
+                value_out[here, :] = block[:, half:wide]
+            start = number * wide
+            output_out[there, start : start + half] = block[:some, wide : wide + half]
+            output_out[there, start + half : start + wide] = block[some:, wide : wide + half]
 
 
 def sum_everywhere(cid, sizes, *arrays):
@@ -830,13 +936,12 @@
     half = (total, depth // total, wide + wide // 2 + arrays[4].shape[1])
     dma = pltpu.SemaphoreType.DMA
     vmem = pl.BlockSpec(memory_space=pltpu.VMEM)
-    return pl.pallas_call(
+    whole = pl.pallas_call(
         functools.partial(sum_body, sizes),
-        out_shape=[jax.ShapeDtypeStruct(array.shape, F32) for array in arrays],
+        out_shape=jax.ShapeDtypeStruct((2, *half), BF16),
         in_specs=[vmem] * 5,
-        out_specs=[vmem] * 5,
+        out_specs=vmem,
         scratch_shapes=[pltpu.VMEM(half, BF16)] * 4
-        + [pltpu.VMEM((2, *half), BF16)]
         + [dma((sizes["dp"],))] * 2
         + [dma((total,))] * 6,
         name="sum_everywhere",
@@ -844,6 +949,17 @@
             collective_id=cid, has_side_effects=True, vmem_limit_bytes=60_000_000
         ),
     )(*arrays)
+    parts = 4
+    return pl.pallas_call(
+        unpack_body,
+        grid=(parts,),
+        out_shape=[jax.ShapeDtypeStruct(array.shape, F32) for array in arrays],
+        in_specs=[pl.BlockSpec((2, total // parts, *half[1:]), lambda i: (0, i, 0, 0))],
+        out_specs=[
+            pl.BlockSpec((array.shape[0] // parts, array.shape[1]), lambda i: (i, 0)) for array in arrays
+        ],
+        name="unpack_sums",
+    )(whole)
 
 
 def rope_tables(positions, head_size):
@@ -913,25 +1029,9 @@
     key_rot = rotate(key_raw, cosine, sine_table).astype(BF16)
     query_send = query_rot.reshape(tokens, KV_HEADS, 2 * HEAD_DIM).transpose(1, 0, 2)
     kv_send = jnp.concatenate([key_rot, value_raw.astype(BF16)], axis=2).transpose(1, 0, 2)
-    kv_all, queries = exchange(
-        0, sizes, "send_qkv", (kv_send, SEQ_AXES, pick_context), (query_send, ("context",), pick_target)
-    )
-    kv_all = kv_all.reshape(-1, 2 * HEAD_DIM)
-    columns = 2 * tokens
-    grad_all, mixtures, sums = exchange(
-        7,
-        sizes,
-        "attention_forward",
-        (cotangent[0], ("expert",), pick_whole),
-        compute=attention_forward,
-        data=(queries, kv_all),
-        results=(
-            jax.ShapeDtypeStruct(queries.shape, BF16),
-            jax.ShapeDtypeStruct((KV_HEADS, 1, columns), F32),
-        ),
-        scratch=(pltpu.VMEM((kv_all.shape[0], columns), F32),),
-    )
-    (mixture,) = exchange(1, sizes, "send_mixture", (mixtures, ("context",), pick_target))
+    kv_all, queries, grad_all, mixtures, sums, mixture = run_forward(
+        0, sizes, kv_send, query_send, cotangent[0]
+    )
     mixture_flat = mixture.transpose(1, 0, 2).reshape(tokens, HEADS * HEAD_DIM)
 
     after_attn = input_float + dot(mixture_flat, output_weight)
@@ -946,11 +1046,8 @@
     gates = powers / jnp.sum(powers, axis=0, keepdims=True)
     gate_table = jnp.where(chosen, gates, -1.0)
 
-    moe_all, table_all = exchange(
-        2, sizes, "send_tokens", (moe_input, ("expert",), pick_whole), (gate_table, ("expert",), pick_whole)
-    )
     own_g, own_u, own_d, other_g, other_u, other_d, moe_terms, grad_back, dot_back = run_experts(
-        3, sizes, moe_all, grad_all, table_all, gate_weight, up_weight, down_weight
+        3, sizes, moe_input, gate_table, grad_all, gate_weight, up_weight, down_weight
     )
     grad_gates = dot_back[:, :mine].reshape(EXPERTS, tokens)
     grad_logits = gates * (grad_gates - jnp.sum(gates * grad_gates, axis=0, keepdims=True))

time: 404 us -> 376 us (0.931)
  Pallas kernels: 354 us -> 327 us
  local copies, waits for them, and re-layouts: 23.2 us -> 17.1 us
    pallas_call x5 -> x1, Pallas kernels: 112 us -> 10.5 us  [exchange(): pl.pallas_call(functools.partial(exchange_body, items, sizes, compute, le...]
    pallas_call x2 -> x4, Pallas kernels: 142 us -> 223 us  [the longest x1 85.1 us: run_experts(): pl.pallas_call(functools.partial(moe_body, sizes), grid=(3 * mine + 1,),...]
    pallas_call x1, Pallas kernels: 99.7 us -> 93.5 us  [run_backward(): pl.pallas_call(functools.partial(backward_body, sizes), out_shape=[jax.Sh...]
    unnamed x117 -> x103, local copies, waits for them, and re-layouts: 15.5 us -> 9.39 us
where the time goes in v6:
time: 376 us; the launch traced here: 375 us
  Pallas kernels  327 us (87%)
  local copies, waits for them, and re-layouts  17.1 us (5%)
  matrix products  15.8 us (4%)
  other arithmetic  14.2 us (4%)
    pallas_call x1, Pallas kernels, run_backward(): pl.pallas_call(functools.partial(backward_body, sizes), out_shape=[jax.Sh...  93.5 us
    pallas_call x1, Pallas kernels, run_experts(): pl.pallas_call(functools.partial(moe_body, sizes), grid=(3 * mine + 1,),...  85.1 us
    pallas_call x1, Pallas kernels, sum_everywhere(): pl.pallas_call(functools.partial(sum_body, sizes), out_shape=jax.ShapeDty...  80.7 us
    pallas_call x1, Pallas kernels, run_forward(): pl.pallas_call(functools.partial(forward_body, sizes), out_shape=[jax.Sha...  51.4 us
    pallas_call x1, Pallas kernels, exchange(): pl.pallas_call(functools.partial(exchange_body, items, sizes, compute, le...  10.5 us
    unnamed x103, local copies, waits for them, and re-layouts  9.39 us

profile of v6, /device:TPU:1, one launch (start us, length us, event | category | flops | bytes accessed | tf_op | source)
XLA Modules:
  0.0 375.2 jit_solution(1711591406318152853)
XLA Ops:
  0.7 1.1 fusion.13
  3.2 1.3 copy.95
  4.5 1.4 fusion.26
  9.7 51.4 %attention_forward.1 = (bf16[32,128,128]{2,1,0:T(8,128)(2,1)}, bf16[4,128,128]{2,1,0:T(8,128)(2,1)}, bf16[8,128,1024]{2,1,0:T(8,128)(2,1)}, bf16[4,128,128]{2,1,...) custom-call(bf16[4,128,128]{2,1,0:T(8,128)(2,1)} %maximum_bitcast_fusion.refs_0_, ...), custom_call_target="tpu_custom_call" | custom-call | tf_op jit(solution)/shard_map/attention_forward/pallas_call | solution.py:287
  61.1 1.0 copy.105
  64.2 1.2 fusion.53
  67.1 85.1 %run_experts.1 = (f32[4,8,64,512]{3,2,1,0:T(8,128)}, f32[4,8,64,512]{3,2,1,0:T(8,128)}, f32[4,8,32,1024]{3,2,1,0:T(8,128)}, bf16[4,8,64,512]{3,2,1,0:T(8,128)(2,...) custom-call(bf16[128,1024]{1,0:T(8,128)(2,1)} %multiply_convert_fusi, ...), custom_call_target="tpu_custom_call" | custom-call | tf_op jit(solution)/shard_map/run_experts/pallas_call | solution.py:731
  153.9 1.9 fusion.42
  155.7 2.1 convert_reduce_fusion.1
  157.9 1.2 multiply_reduce_fusion
  161.4 10.5 %send_grad_mixture.1.refs_10_ = bf16[4,128,128]{2,1,0:T(8,128)(2,1)} custom-call(bf16[4,128,128]{2,1,0:T(8,128)(2,1)} %bitcast.132), custom_call_target="tpu_custom_call" | custom-call | tf_op jit(solution)/shard_map/send_grad_mixture/pallas_call | solution.py:149
  172.0 93.5 %attention_backward.1 = (bf16[8,128,1024]{2,1,0:T(8,128)(2,1)}, bf16[32,128,128]{2,1,0:T(8,128)(2,1)}, f32[4,128,128]{2,1,0:T(8,128)}, f32[4,64,512]{2,1,0:T(8,1...) custom-call(f32[4,8,64,512]{3,2,1,0:T(8,128)} %get-tuple-element.40.refs_0_, ...), custom_call_target="tpu_custom_call" | custom-call | tf_op jit(solution)/shard_map/attention_backward/pallas_call | solution.py:397
  265.5 2.0 convert_reduce_fusion
  269.2 1.5 convert_reduce_fusion.2
  272.3 1.5 fusion.12
  273.8 1.1 fusion.11
  276.0 1.4 fusion.30.refs_2_
  277.4 1.4 fusion.28.refs_1_
  278.8 1.7 fusion.34.refs_3_
  280.5 1.9 fusion.32.refs_0_
  282.4 80.7 %sum_everywhere.1.whole = bf16[2,64,16,896]{3,2,1,0:T(8,128)(2,1)} custom-call(f32[1024,512]{1,0:T(8,128)} %fusion.32.refs_0_, f32[1024,256]{1,0:T(8,128)} %fusion.28.refs_1_, f32[1024,256]{1,0:T(8,128)} %fusion.30.refs_2_, f32[512,1024]{1,0:T(8,128)} %fusion.34.refs_3_, f32[1024,128]{1,0:T(8,128)} %pad.4.refs_4_), custom_call_target="tpu_custom_call" | custom-call | tf_op jit(solution)/shard_map/sum_everywhere/pallas_call | solution.py:939
  363.1 5.3 %unpack_sums.1 = (f32[1024,512]{1,0:T(8,128)}, f32[1024,256]{1,0:T(8,128)}, f32[1024,256]{1,0:T(8,128)}, f32[512,1024]{1,0:T(8,128)}, f32[1024,128]{1,0:T(8,128)}) custom-call(bf16[2,64,16,896]{3,2,1,0:T(8,128)(2,1)} %sum_everywhere.1.whole), custom_call_target="tpu_custom_call" | custom-call | tf_op jit(solution)/shard_map/unpack_sums/pallas_call | solution.py:953
  368.4 2.5 slice_reduce_fusion
  370.9 1.9 copy.113
  (147 shorter events, 19.3 us)
Async XLA Ops:
  0.6 5.5 %copy-start = (bf16[1,128,1024]{2,1,0:T(8,128)(2,1)S(1)}, bf16[1,128,1024]{2,1,0:T(8,128)(2,1)}, u32[]{:S(2)}) copy-start(bf16[1,128,1024]{2,1,0:T(8,128)(2,1)} %param.13) | copy-start | bytes 786436
  0.7 5.5 %copy-start.35 = (f32[1024]{0:T(1024)S(1)}, f32[1024]{0:T(1024)}, u32[]{:S(2)}) copy-start(f32[1024]{0:T(1024)} %param.14) | copy-start | bytes 12292
  0.7 5.2 %copy-start.12 = (bf16[1024,256]{1,0:T(8,128)(2,1)S(1)}, bf16[1024,256]{1,0:T(8,128)(2,1)}, u32[]{:S(2)}) copy-start(bf16[1024,256]{1,0:T(8,128)(2,1)} %param.17) | copy-start | bytes 1572868
  1.9 6.4 %copy-start.41 = (f32[128]{0:T(128)}, f32[128]{0:T(128)S(1)}, u32[]{:S(2)}) copy-start(f32[128]{0:T(128)S(1)} %add_rsqrt_fusion.1) | copy-start | bytes 1540
  3.0 3.8 %copy-start.16 = (f32[128,64]{1,0:T(8,128)}, f32[128,64]{1,0:T(8,128)S(1)}, u32[]{:S(2)}) copy-start(f32[128,64]{1,0:T(8,128)S(1)} %get-tuple-element.141) | copy-start | bytes 98308
  3.0 3.8 %copy-start.19 = (f32[128,64]{1,0:T(8,128)}, f32[128,64]{1,0:T(8,128)S(1)}, u32[]{:S(2)}) copy-start(f32[128,64]{1,0:T(8,128)S(1)} %get-tuple-element.140) | copy-start | bytes 98308
  3.1 5.8 %copy-start.28 = (f32[128,64]{0,1:T(8,128)}, f32[128,64]{0,1:T(8,128)S(1)}, u32[]{:S(2)}) copy-start(f32[128,64]{0,1:T(8,128)S(1)} %copy.102) | copy-start | bytes 98308
  3.2 5.7 %copy-start.30 = (f32[128,64]{0,1:T(8,128)}, f32[128,64]{0,1:T(8,128)S(1)}, u32[]{:S(2)}) copy-start(f32[128,64]{0,1:T(8,128)S(1)} %copy.103) | copy-start | bytes 98308
  8.3 53.9 %copy-start.9 = (bf16[512,1024]{1,0:T(8,128)(2,1)S(1)}, bf16[512,1024]{1,0:T(8,128)(2,1)}, u32[]{:S(2)}) copy-start(bf16[512,1024]{1,0:T(8,128)(2,1)} %param.18) | copy-start | bytes 3145732
  8.8 54.5 %copy-start.37 = (f32[1024]{0:T(1024)S(1)}, f32[1024]{0:T(1024)}, u32[]{:S(2)}) copy-start(f32[1024]{0:T(1024)} %param.19) | copy-start | bytes 12292
  8.9 55.3 %copy-start.33 = (bf16[1024,32]{0,1:T(8,128)(2,1)S(1)}, bf16[1024,32]{0,1:T(8,128)(2,1)}, u32[]{:S(2)}) copy-start(bf16[1024,32]{0,1:T(8,128)(2,1)} %param.20) | copy-start | bytes 196612
  152.2 5.6 %copy-start.3 = (f32[128,1024]{1,0:T(8,128)S(1)}, f32[128,1024]{1,0:T(8,128)}, u32[]{:S(2)}) copy-start(f32[128,1024]{1,0:T(8,128)} %copy-done.2) | copy-start | bytes 1572868
  152.3 5.6 %copy-start.22 = (f32[32,128]{1,0:T(8,128)S(1)}, f32[32,128]{1,0:T(8,128)}, u32[]{:S(2)}) copy-start(f32[32,128]{1,0:T(8,128)} %copy-done.21) | copy-start | bytes 49156
  152.3 5.6 %copy-start.34 = (bf16[1024,32]{0,1:T(8,128)(2,1)S(1)}, bf16[1024,32]{0,1:T(8,128)(2,1)}, u32[]{:S(2)}) copy-start(bf16[1024,32]{0,1:T(8,128)(2,1)} %param.20) | copy-start | bytes 196612
  152.3 5.6 %copy-start.38 = (f32[1024]{0:T(1024)S(1)}, f32[1024]{0:T(1024)}, u32[]{:S(2)}) copy-start(f32[1024]{0:T(1024)} %param.19) | copy-start | bytes 12292
  152.3 5.6 %copy-start.40 = (f32[128]{0:T(128)S(1)}, f32[128]{0:T(128)}, u32[]{:S(2)}) copy-start(f32[128]{0:T(128)} %copy-done.39) | copy-start | bytes 1540
  152.3 5.6 %copy-start.45 = (f32[128]{0:T(128)S(1)}, f32[128]{0:T(128)}, u32[]{:S(2)}) copy-start(f32[128]{0:T(128)} %copy-done.44) | copy-start | bytes 1540
  152.3 5.6 %copy-start.47 = (f32[128]{0:T(128)S(1)}, f32[128]{0:T(128)}, u32[]{:S(2)}) copy-start(f32[128]{0:T(128)} %copy-done.46) | copy-start | bytes 1540
  155.7 3.3 copy-start.18
  267.7 3.1 copy-start.17
  275.0 3.8 %copy-start.15 = (bf16[128,4,128]{0,2,1:T(8,128)(2,1)S(1)}, bf16[128,4,128]{0,2,1:T(8,128)(2,1)}, u32[]{:S(2)}) copy-start(bf16[128,4,128]{0,2,1:T(8,128)(2,1)} %copy-done.14) | copy-start | bytes 393220
  363.1 9.7 %copy-start.25 = (f32[4,64,512]{2,1,0:T(8,128)S(1)}, f32[4,64,512]{2,1,0:T(8,128)}, u32[]{:S(2)}) copy-start(f32[4,64,512]{2,1,0:T(8,128)} %get-tuple-element.171) | copy-start | bytes 1572868
  368.4 5.2 %copy-start.24 = (f32[4,64,512]{2,1,0:T(8,128)S(1)}, f32[4,64,512]{2,1,0:T(8,128)}, u32[]{:S(2)}) copy-start(f32[4,64,512]{2,1,0:T(8,128)} %get-tuple-element.172) | copy-start | bytes 1572868
  368.4 6.0 %copy-start.23 = (f32[4,32,1024]{2,1,0:T(8,128)S(1)}, f32[4,32,1024]{2,1,0:T(8,128)}, u32[]{:S(2)}) copy-start(f32[4,32,1024]{2,1,0:T(8,128)} %get-tuple-element.173) | copy-start | bytes 1572868
  (24 other events, 38.5 us)

commit v7 on v6

--- a/solution.py
+++ b/solution.py
@@ -115,48 +115,6 @@
         own.start()
         started.append(own)
     return started
-
-
-def exchange_body(items, sizes, compute, more_ins, more_outs, *refs):
-    count = len(items)
-    ins, refs = refs[:count], refs[count:]
-    data_ins, refs = refs[:more_ins], refs[more_ins:]
-    outs, refs = refs[:count], refs[count:]
-    data_outs, refs = refs[:more_outs], refs[more_outs:]
-    sems, scratch = refs[: 2 * count], refs[2 * count :]
-
-    greet([item[0] for item in items], sizes)
-    waits = []
-    for number, item in enumerate(items):
-        pair = sems[2 * number : 2 * number + 2]
-        waits += launch(sizes, *item, ins[number], outs[number], *pair)
-    if compute is not None:
-        compute(data_ins, data_outs, scratch)
-    for copy in waits:
-        copy.wait()
-
-
-def exchange(cid, sizes, name, *specs, compute=None, data=(), results=(), scratch=(), cost=None):
-    vmem, hbm = pl.BlockSpec(memory_space=pltpu.VMEM), pl.BlockSpec(memory_space=pl.ANY)
-    items, shapes, spaces, sems = [], [], [], []
-    for array, axes, pick, *large in specs:
-        total = group_size(axes, sizes)
-        chunk = array.shape if pick is pick_whole else array.shape[1:]
-        shapes.append(jax.ShapeDtypeStruct((total, *chunk), array.dtype))
-        spaces.append(hbm if large else vmem)
-        items.append((axes, pick, not large))
-        sems += [pltpu.SemaphoreType.DMA((total,)), pltpu.SemaphoreType.DMA((total,))]
-    return pl.pallas_call(
-        functools.partial(exchange_body, items, sizes, compute, len(data), len(results)),
-        out_shape=[*shapes, *results],
-        in_specs=[*spaces, *([vmem] * len(data))],
-        out_specs=[*spaces, *([vmem] * len(results))],
-        scratch_shapes=[*sems, *scratch],
-        name=name,
-        compiler_params=pltpu.CompilerParams(
-            collective_id=cid, has_side_effects=True, vmem_limit_bytes=60_000_000
-        ),
-    )(*[spec[0] for spec in specs], *data)
 
 
 def stack_heads(block, low):
@@ -308,20 +266,37 @@
 
 
 def backward_body(sizes, *refs):
-    owns, others, y_ref, data, refs = refs[:3], refs[3:6], refs[6], refs[7:12], refs[12:]
+    owns_hbm, others_hbm, y_ref, refs = refs[:3], refs[3:6], refs[6], refs[7:]
+    queries, kv_all, mixtures, mix_send, sums, *refs = refs
     y_back, kv_back, query_back, *totals = refs[:6]
     sends, gots, sends_2, gots_2 = refs[6:9], refs[9:12], refs[12:15], refs[15:18]
-    grad_query, terms, sum_kv = refs[18:21]
-    sems = refs[21:]
+    grad_query, terms, sum_kv, grad_mix = refs[18:22]
+    owns, others, sems = refs[22:25], refs[25:28], refs[28:]
     dp, side = lax.axis_index("dp"), lax.axis_index("context") // 2
     experts = owns[0].shape[0]
     firsts = (("dp",), ("dp",), ("side",))
     seconds = (("side",), ("side",), ("dp",))
+    loads = [
+        (
+            pltpu.make_async_copy(owns_hbm[i], owns[i], sems[20].at[i]),
+            pltpu.make_async_copy(others_hbm[i], others[i], sems[20].at[3 + i]),
+        )
+        for i in range(3)
+    ]
+    for pair in loads:
+        for copy in pair:
+            copy.start()
+    greet([SEQ_AXES, ("dp",)], sizes)
+    mixes = launch(sizes, ("context",), pick_target, True, mix_send, grad_mix, *sems[18:20])
+    rest = launch(sizes, ("expert",), pick_target, True, y_ref, y_back, *sems[6:8])
 
     def chip_sum(i, expert, place):
         return owns[i][expert, place] + others[i][expert, place].astype(F32)
 
+    stage_1 = []
     for i, axes in enumerate(firsts):
+        for copy in loads[i]:
+            copy.wait()
 
         def fill(expert, carry, i=i, axes=axes):
             for d in range(4):
@@ -334,13 +309,10 @@
             return carry
 
         lax.fori_loop(0, experts, fill, 0)
-    greet([SEQ_AXES, ("dp",)], sizes)
-    stage_1 = []
-    for i, axes in enumerate(firsts):
         stage_1 += launch(sizes, axes, pick_target, False, sends[i], gots[i], *sems[2 * i : 2 * i + 2])
-    rest = launch(sizes, ("expert",), pick_target, True, y_ref, y_back, *sems[6:8])
-
-    attention_backward(data, (grad_query, terms), (sum_kv,))
+    for copy in mixes:
+        copy.wait()
+    attention_backward((queries, kv_all, mixtures, grad_mix, sums), (grad_query, terms), (sum_kv,))
     rest += launch(sizes, SEQ_AXES, pick_target, True, terms, kv_back, *sems[8:10])
     rest += launch(sizes, ("context",), pick_target, True, grad_query, query_back, *sems[10:12])
     for copy in stage_1:
@@ -392,7 +364,8 @@
     tiles = [own.shape[2:] for own in owns]
     stage_1 = [(4, experts, 2, *tiles[0]), (4, experts, 2, *tiles[1]), (2, experts, 4, *tiles[2])]
     stage_2 = [(2, experts, *tiles[0]), (2, experts, *tiles[1]), (4, experts, *tiles[2])]
-    sizes_of = [4, 4, 2, sizes["expert"], group_size(SEQ_AXES, sizes), sizes["context"], 2, 2, 4]
+    context = sizes["context"]
+    sizes_of = [4, 4, 2, sizes["expert"], group_size(SEQ_AXES, sizes), context, 2, 2, 4, context]
     dma = pltpu.SemaphoreType.DMA
     return pl.pallas_call(
         functools.partial(backward_body, sizes),
@@ -402,14 +375,18 @@
             jax.ShapeDtypeStruct(queries.shape, F32),
             *[jax.ShapeDtypeStruct((experts, *tile), F32) for tile in tiles],
         ],
-        in_specs=[vmem] * 12,
+        in_specs=[*([pl.BlockSpec(memory_space=pl.ANY)] * 6), *([vmem] * 6)],
         out_specs=[vmem] * 6,
         scratch_shapes=[
             *[pltpu.VMEM(shape, BF16) for shape in stage_1 * 2 + stage_2 * 2],
             pltpu.VMEM(queries.shape, F32),
             pltpu.VMEM(kv_all.shape, BF16),
             pltpu.VMEM((kv_all.shape[0] * tokens, 2 * HEAD_DIM), F32),
+            pltpu.VMEM(queries.shape, BF16),
+            *[pltpu.VMEM(own.shape, F32) for own in owns],
+            *[pltpu.VMEM(own.shape, BF16) for own in owns],
             *[dma((n,)) for n in sizes_of for _ in range(2)],
+            dma((6,)),
         ],
         name="attention_backward",
         compiler_params=pltpu.CompilerParams(
@@ -418,9 +395,16 @@
     )(*owns, *others, y_terms, *data)
 
 
+NEAR = ((0, 0), (1, 0), (0, 1), (0, 3), (0, 2), (1, 1), (1, 3), (1, 2))
+
+
+def owner_at(owner, steps, sign):
+    half = lax.rem(owner // 4 + steps[0], 2)
+    return half * 4 + lax.rem(owner + 4 + sign * steps[1], 4)
+
+
 def moe_copies(sizes, refs):
     moe_ref, table_ref, moe_land, table_land, d_send, d_back, dots, dot_back, g_sends, g_backs, sems = refs
-    owners = sizes["expert"]
     owner, context = lax.axis_index("expert"), lax.axis_index("context")
 
     def pair_of(copies, target, number):
@@ -441,10 +425,10 @@
             (table_ref, table_land.at[number], sems[7], sems[8]),
             (moe_ref, moe_land.at[number], sems[9], sems[10]),
         )
-        return pair_of(pairs, lax.rem(owner + number, owners), number)
+        return pair_of(pairs, owner_at(owner, NEAR[number], 1), number)
 
     def results_of(number):
-        target = lax.rem(owner + owners - number, owners)
+        target = owner_at(owner, NEAR[number], -1)
         pairs = (
             (d_send.at[target], d_back.at[owner], sems[0], sems[1]),
             (dots.at[target], dot_back.at[owner], sems[2], sems[3]),
@@ -553,7 +537,7 @@
             barrier, inc=1, device_id={"context": context + 1 - 2 * core}, device_id_type=MESH_ID
         )
         pl.semaphore_wait(barrier, owners)
-        for number in range(1, owners):
+        for number in range(1, group):
             for copy in tokens_to(number):
                 copy.start()
         dots[...] = jnp.zeros_like(dots)
@@ -562,6 +546,9 @@
         for number in range(1, group):
             for copy in tokens_to(number):
                 copy.wait_recv()
+        for number in range(group, owners):
+            for copy in tokens_to(number):
+                copy.start()
 
     @pl.when(step == mine)
     def _():
@@ -595,6 +582,11 @@
         spot = pl.ds(place, CAP)
         here = pl.ds(pl.multiple_of(tile * rows, rows), rows)
         part = pl.ds(tile * group, group)
+
+        def source_of(j):
+            near, far = owner_at(owner, NEAR[j], -1), owner_at(owner, NEAR[group + j], -1)
+            return near + tile * (far - near)
+
         table = jnp.concatenate(
             [table_land[tile * group + j, pl.ds(owner * mine + expert, 1), :] for j in range(group)], axis=0
         )
@@ -608,7 +600,7 @@
         counts = lax.broadcasted_iota(jnp.int32, (CAP, tokens), 0).astype(F32)
         for j in range(group):
             position = tile * group + j
-            source = lax.rem(owner + owners - position, owners)
+            source = source_of(j)
             chosen = counts == slots[j : j + 1]
             onehot = jnp.where(chosen, 1.0, 0.0).astype(BF16)
             weight = jnp.where(chosen, table[j : j + 1], 0.0)
@@ -644,7 +636,7 @@
         dbuf_all[part, spot, :] = grad_buffer.reshape(group, CAP, width)
         for j in range(group):
             position = tile * group + j
-            source = lax.rem(owner + owners - position, owners)
+            source = source_of(j)
             onehot = picks[position, spot, :].astype(F32)
             dots[source, pl.ds(expert, 1), :] = jnp.sum(
                 onehot * dot_col[j * CAP : (j + 1) * CAP, :], axis=0, keepdims=True
@@ -652,15 +644,11 @@
 
         @pl.when(expert == mine - 1)
         def _():
-            def combine(j, carry):
-                position = tile * group + j
-                source = lax.rem(owner + owners - position, owners)
+            for j in range(group):
+                position, source = tile * group + j, source_of(j)
                 d_send[source] = t_dot(picks[position], dbuf_all[position]).astype(BF16)
                 moved = t_dot(highs[position], eo_all[position]) + t_dot(lows[position], eo_all[position])
                 y_send[source] = moved.astype(BF16)
-                return carry
-
-            lax.fori_loop(0, group, combine, 0)
 
     @pl.when((step >= 2 * mine) & (step < 3 * mine))
     def _():
@@ -858,17 +846,19 @@
             barrier, inc=1, device_id=place(step)[1], device_id_type=MESH_ID
         ),
     )
-    for number in range(2):
-
-        @pl.when(core == 1 - number)
-        def _(number=number):
-            def fill(chunk):
-                load[chunk] = pack(number, chunk).astype(BF16)
-
-            each(0, total, fill)
-
-    pl.semaphore_wait(barrier, total)
     for turn in range(sizes["dp"]):
+        base = lax.rem(lax.axis_index("dp") + turn, sizes["dp"]) * plane
+        for number in range(2):
+
+            @pl.when(core == 1 - number)
+            def _(number=number, base=base):
+                def fill(chunk):
+                    load[chunk] = pack(number, chunk).astype(BF16)
+
+                each(base, base + plane, fill)
+
+        if turn == 0:
+            pl.semaphore_wait(barrier, total)
         near_copy(turn).start()
 
     for turn in range(sizes["dp"]):
@@ -1064,14 +1054,13 @@
     output_grad = t_dot(mixture_flat, grad_after_half)
     grad_mix = dot_t(grad_after_half, output_weight).astype(BF16)
     grad_mix = grad_mix.reshape(tokens, KV_HEADS, 2 * HEAD_DIM).transpose(1, 0, 2)
-    (grad_mixtures,) = exchange(4, sizes, "send_grad_mixture", (grad_mix, ("context",), pick_target))
     moe_back, kv_back, grad_query, gate_sum, up_sum, down_sum = run_backward(
         8,
         sizes,
         (own_g, own_u, own_d),
         (other_g, other_u, other_d),
         moe_terms,
-        (queries, kv_all, mixtures, grad_mixtures, sums),
+        (queries, kv_all, mixtures, grad_mix, sums),
     )
     outputs = (after_attn + jnp.sum(moe_back.astype(F32), axis=0)).astype(BF16)
     grad_kv = jnp.sum(kv_back.astype(F32).reshape(KV_HEADS, owners, tokens, 2 * HEAD_DIM), axis=1)

time: 376 us -> 349 us (0.928)
  Pallas kernels: 327 us -> 302 us
    pallas_call x1, Pallas kernels: 85.1 us -> 72.4 us  [run_experts(): pl.pallas_call(functools.partial(moe_body, sizes), grid=(3 * mine + 1,),...]
    pallas_call x1, Pallas kernels: 93.5 us -> 81.1 us  [run_backward(): pl.pallas_call(functools.partial(backward_body, sizes), out_shape=[jax.Sh...]
    pallas_call x1, Pallas kernels: 80.7 us -> 92.1 us  [sum_everywhere(): pl.pallas_call(functools.partial(sum_body, sizes), out_shape=jax.ShapeDty...]
    pallas_call x1 -> x0, Pallas kernels: 10.5 us -> none  [exchange(): pl.pallas_call(functools.partial(exchange_body, items, sizes, compute, le...]
    unnamed x103 -> x107, local copies, waits for them, and re-layouts: 9.39 us -> 10.6 us
where the time goes in v7:
time: 349 us; the launch traced here: 348 us
  Pallas kernels  302 us (87%)
  local copies, waits for them, and re-layouts  18.4 us (5%)
  matrix products  14 us (4%)
  other arithmetic  11.6 us (3%)
    pallas_call x1, Pallas kernels, sum_everywhere(): pl.pallas_call(functools.partial(sum_body, sizes), out_shape=jax.ShapeDty...  92.1 us
    pallas_call x1, Pallas kernels, run_backward(): pl.pallas_call(functools.partial(backward_body, sizes), out_shape=[jax.Sh...  81.1 us
    pallas_call x1, Pallas kernels, run_experts(): pl.pallas_call(functools.partial(moe_body, sizes), grid=(3 * mine + 1,),...  72.4 us
    pallas_call x1, Pallas kernels, run_forward(): pl.pallas_call(functools.partial(forward_body, sizes), out_shape=[jax.Sha...  51.4 us
    unnamed x107, local copies, waits for them, and re-layouts  10.6 us

profile of v7, /device:TPU:1, one launch (start us, length us, event | category | flops | bytes accessed | tf_op | source)
XLA Modules:
  0.0 347.7 jit_solution(10517539074119375727)
XLA Ops:
  0.7 1.1 fusion.13
  3.2 1.3 copy.95
  4.5 1.4 fusion.26
  9.7 51.4 %attention_forward.1 = (bf16[32,128,128]{2,1,0:T(8,128)(2,1)}, bf16[4,128,128]{2,1,0:T(8,128)(2,1)}, bf16[8,128,1024]{2,1,0:T(8,128)(2,1)}, bf16[4,128,128]{2,1,...) custom-call(bf16[4,128,128]{2,1,0:T(8,128)(2,1)} %maximum_bitcast_fusion.refs_0_, ...), custom_call_target="tpu_custom_call" | custom-call | tf_op jit(solution)/shard_map/attention_forward/pallas_call | solution.py:245
  61.1 1.0 copy.105
  66.2 72.4 %run_experts.1 = (f32[4,8,64,512]{3,2,1,0:T(8,128)}, f32[4,8,64,512]{3,2,1,0:T(8,128)}, f32[4,8,32,1024]{3,2,1,0:T(8,128)}, bf16[4,8,64,512]{3,2,1,0:T(8,128)(2,...) custom-call(bf16[128,1024]{1,0:T(8,128)(2,1)} %copy-done.7, ...), custom_call_target="tpu_custom_call" | custom-call | tf_op jit(solution)/shard_map/run_experts/pallas_call | solution.py:719
  138.6 0.8 slice.46
  140.2 1.9 fusion.42
  142.1 2.1 convert_reduce_fusion.1
  144.2 1.2 multiply_reduce_fusion
  147.8 81.1 %attention_backward.1 = (bf16[8,128,1024]{2,1,0:T(8,128)(2,1)}, bf16[32,128,128]{2,1,0:T(8,128)(2,1)}, f32[4,128,128]{2,1,0:T(8,128)}, f32[4,64,512]{2,1,0:T(8,1...) custom-call(f32[4,8,64,512]{3,2,1,0:T(8,128)} %get-tuple-element.40.refs_0_, ...), custom_call_target="tpu_custom_call" | custom-call | tf_op jit(solution)/shard_map/attention_backward/pallas_call | solution.py:370
  228.9 2.0 convert_reduce_fusion
  234.9 1.1 fusion.11
  236.3 0.8 pad.4.refs_4_
  237.1 1.4 fusion.30.refs_2_
  238.5 1.4 fusion.28.refs_1_
  239.8 1.7 fusion.34.refs_3_
  241.6 1.9 fusion.32.refs_0_
  243.4 92.1 %sum_everywhere.1.whole = bf16[2,64,16,896]{3,2,1,0:T(8,128)(2,1)} custom-call(f32[1024,512]{1,0:T(8,128)} %fusion.32.refs_0_, f32[1024,256]{1,0:T(8,128)} %fusion.28.refs_1_, f32[1024,256]{1,0:T(8,128)} %fusion.30.refs_2_, f32[512,1024]{1,0:T(8,128)} %fusion.34.refs_3_, f32[1024,128]{1,0:T(8,128)} %pad.4.refs_4_), custom_call_target="tpu_custom_call" | custom-call | tf_op jit(solution)/shard_map/sum_everywhere/pallas_call | solution.py:929
  335.6 5.3 %unpack_sums.1 = (f32[1024,512]{1,0:T(8,128)}, f32[1024,256]{1,0:T(8,128)}, f32[1024,256]{1,0:T(8,128)}, f32[512,1024]{1,0:T(8,128)}, f32[1024,128]{1,0:T(8,128)}) custom-call(bf16[2,64,16,896]{3,2,1,0:T(8,128)(2,1)} %sum_everywhere.1.whole), custom_call_target="tpu_custom_call" | custom-call | tf_op jit(solution)/shard_map/unpack_sums/pallas_call | solution.py:943
  340.9 2.5 slice_reduce_fusion
  343.4 1.9 copy.113
  345.3 0.8 copy.118
  346.1 0.8 copy.119
  (150 shorter events, 16.9 us)
Async XLA Ops:
  0.6 5.5 %copy-start = (bf16[1,128,1024]{2,1,0:T(8,128)(2,1)S(1)}, bf16[1,128,1024]{2,1,0:T(8,128)(2,1)}, u32[]{:S(2)}) copy-start(bf16[1,128,1024]{2,1,0:T(8,128)(2,1)} %param.13) | copy-start | bytes 786436
  0.7 5.5 %copy-start.37 = (f32[1024]{0:T(1024)S(1)}, f32[1024]{0:T(1024)}, u32[]{:S(2)}) copy-start(f32[1024]{0:T(1024)} %param.14) | copy-start | bytes 12292
  0.7 5.2 %copy-start.13 = (bf16[1024,256]{1,0:T(8,128)(2,1)S(1)}, bf16[1024,256]{1,0:T(8,128)(2,1)}, u32[]{:S(2)}) copy-start(bf16[1024,256]{1,0:T(8,128)(2,1)} %param.17) | copy-start | bytes 1572868
  1.9 6.4 %copy-start.43 = (f32[128]{0:T(128)}, f32[128]{0:T(128)S(1)}, u32[]{:S(2)}) copy-start(f32[128]{0:T(128)S(1)} %add_rsqrt_fusion.1) | copy-start | bytes 1540
  3.0 3.8 %copy-start.17 = (f32[128,64]{1,0:T(8,128)}, f32[128,64]{1,0:T(8,128)S(1)}, u32[]{:S(2)}) copy-start(f32[128,64]{1,0:T(8,128)S(1)} %get-tuple-element.141) | copy-start | bytes 98308
  3.0 3.8 %copy-start.21 = (f32[128,64]{1,0:T(8,128)}, f32[128,64]{1,0:T(8,128)S(1)}, u32[]{:S(2)}) copy-start(f32[128,64]{1,0:T(8,128)S(1)} %get-tuple-element.140) | copy-start | bytes 98308
  3.1 5.8 %copy-start.30 = (f32[128,64]{0,1:T(8,128)}, f32[128,64]{0,1:T(8,128)S(1)}, u32[]{:S(2)}) copy-start(f32[128,64]{0,1:T(8,128)S(1)} %copy.102) | copy-start | bytes 98308
  3.2 5.7 %copy-start.32 = (f32[128,64]{0,1:T(8,128)}, f32[128,64]{0,1:T(8,128)S(1)}, u32[]{:S(2)}) copy-start(f32[128,64]{0,1:T(8,128)S(1)} %copy.103) | copy-start | bytes 98308
  8.3 53.9 %copy-start.10 = (bf16[512,1024]{1,0:T(8,128)(2,1)S(1)}, bf16[512,1024]{1,0:T(8,128)(2,1)}, u32[]{:S(2)}) copy-start(bf16[512,1024]{1,0:T(8,128)(2,1)} %param.18) | copy-start | bytes 3145732
  8.8 54.5 %copy-start.39 = (f32[1024]{0:T(1024)S(1)}, f32[1024]{0:T(1024)}, u32[]{:S(2)}) copy-start(f32[1024]{0:T(1024)} %param.19) | copy-start | bytes 12292
  8.9 55.3 %copy-start.35 = (bf16[1024,32]{0,1:T(8,128)(2,1)S(1)}, bf16[1024,32]{0,1:T(8,128)(2,1)}, u32[]{:S(2)}) copy-start(bf16[1024,32]{0,1:T(8,128)(2,1)} %param.20) | copy-start | bytes 196612
  138.6 5.6 %copy-start.3 = (f32[128,1024]{1,0:T(8,128)S(1)}, f32[128,1024]{1,0:T(8,128)}, u32[]{:S(2)}) copy-start(f32[128,1024]{1,0:T(8,128)} %copy-done.2) | copy-start | bytes 1572868
  138.6 5.6 %copy-start.24 = (f32[32,128]{1,0:T(8,128)S(1)}, f32[32,128]{1,0:T(8,128)}, u32[]{:S(2)}) copy-start(f32[32,128]{1,0:T(8,128)} %copy-done.23) | copy-start | bytes 49156
  138.6 5.6 %copy-start.36 = (bf16[1024,32]{0,1:T(8,128)(2,1)S(1)}, bf16[1024,32]{0,1:T(8,128)(2,1)}, u32[]{:S(2)}) copy-start(bf16[1024,32]{0,1:T(8,128)(2,1)} %param.20) | copy-start | bytes 196612
  138.6 5.6 %copy-start.40 = (f32[1024]{0:T(1024)S(1)}, f32[1024]{0:T(1024)}, u32[]{:S(2)}) copy-start(f32[1024]{0:T(1024)} %param.19) | copy-start | bytes 12292
  138.6 5.6 %copy-start.42 = (f32[128]{0:T(128)S(1)}, f32[128]{0:T(128)}, u32[]{:S(2)}) copy-start(f32[128]{0:T(128)} %copy-done.41) | copy-start | bytes 1540
  138.6 5.6 %copy-start.47 = (f32[128]{0:T(128)S(1)}, f32[128]{0:T(128)}, u32[]{:S(2)}) copy-start(f32[128]{0:T(128)} %copy-done.46) | copy-start | bytes 1540
  138.6 5.6 %copy-start.49 = (f32[128]{0:T(128)S(1)}, f32[128]{0:T(128)}, u32[]{:S(2)}) copy-start(f32[128]{0:T(128)} %copy-done.48) | copy-start | bytes 1540
  142.1 3.3 copy-start.20
  236.1 3.8 %copy-start.16 = (bf16[128,4,128]{0,2,1:T(8,128)(2,1)S(1)}, bf16[128,4,128]{0,2,1:T(8,128)(2,1)}, u32[]{:S(2)}) copy-start(bf16[128,4,128]{0,2,1:T(8,128)(2,1)} %copy-done.15) | copy-start | bytes 393220
  238.5 3.1 copy-start.29
  335.5 9.7 %copy-start.27 = (f32[4,64,512]{2,1,0:T(8,128)S(1)}, f32[4,64,512]{2,1,0:T(8,128)}, u32[]{:S(2)}) copy-start(f32[4,64,512]{2,1,0:T(8,128)} %get-tuple-element.171) | copy-start | bytes 1572868
  340.9 5.2 %copy-start.26 = (f32[4,64,512]{2,1,0:T(8,128)S(1)}, f32[4,64,512]{2,1,0:T(8,128)}, u32[]{:S(2)}) copy-start(f32[4,64,512]{2,1,0:T(8,128)} %get-tuple-element.172) | copy-start | bytes 1572868
  340.9 6.0 %copy-start.25 = (f32[4,32,1024]{2,1,0:T(8,128)S(1)}, f32[4,32,1024]{2,1,0:T(8,128)}, u32[]{:S(2)}) copy-start(f32[4,32,1024]{2,1,0:T(8,128)} %get-tuple-element.173) | copy-start | bytes 1572868
  (26 other events, 34.3 us)

commit v8 on v7

--- a/solution.py
+++ b/solution.py
@@ -33,8 +33,11 @@
     return lax.dot_general(left, right, (((0,), (0,)), ((), ())), preferred_element_type=F32)
 
 
+PARTS = {"side": ("context", 2, 2), "half": ("expert", 2, 4), "place": ("expert", 4, 1)}
+
+
 def axis_size(sizes, name):
-    return 2 if name == "side" else sizes[name]
+    return PARTS[name][1] if name in PARTS else sizes[name]
 
 
 def group_size(axes, sizes):
@@ -44,11 +47,17 @@
     return total
 
 
+def part_index(name):
+    if name not in PARTS:
+        return lax.axis_index(name)
+    axis, size, stride = PARTS[name]
+    return lax.rem(lax.axis_index(axis) // stride, size)
+
+
 def own_index(axes, sizes):
     index = 0
     for name in axes:
-        own = lax.axis_index("context") // 2 if name == "side" else lax.axis_index(name)
-        index = index * axis_size(sizes, name) + own
+        index = index * axis_size(sizes, name) + part_index(name)
     return index
 
 
@@ -56,8 +65,9 @@
     out = {}
     for name in reversed(axes):
         place = lax.rem(index, axis_size(sizes, name))
-        if name == "side":
-            out["context"] = place * 2 + lax.rem(lax.axis_index("context"), 2)
+        if name in PARTS:
+            axis, _, stride = PARTS[name]
+            out[axis] = lax.axis_index(axis) + (place - part_index(name)) * stride
         else:
             out[name] = place
         index = index // axis_size(sizes, name)
@@ -70,6 +80,10 @@
 
 def pick_target(ref, target, peer):
     return ref.at[target]
+
+
+def pick_second(ref, target, peer):
+    return ref.at[:, target]
 
 
 def pick_context(ref, target, peer):
@@ -268,18 +282,19 @@
 def backward_body(sizes, *refs):
     owns_hbm, others_hbm, y_ref, refs = refs[:3], refs[3:6], refs[6], refs[7:]
     queries, kv_all, mixtures, mix_send, sums, *refs = refs
-    y_back, kv_back, query_back, *totals = refs[:6]
+    y_total, kv_back, query_back, *totals = refs[:6]
     sends, gots, sends_2, gots_2 = refs[6:9], refs[9:12], refs[12:15], refs[15:18]
     grad_query, terms, sum_kv, grad_mix = refs[18:22]
-    owns, others, sems = refs[22:25], refs[25:28], refs[28:]
+    owns, others, refs = refs[22:25], refs[25:28], refs[28:]
+    y_land, y_pass, y_got, *sems = refs
     dp, side = lax.axis_index("dp"), lax.axis_index("context") // 2
     experts = owns[0].shape[0]
     firsts = (("dp",), ("dp",), ("side",))
     seconds = (("side",), ("side",), ("dp",))
     loads = [
         (
-            pltpu.make_async_copy(owns_hbm[i], owns[i], sems[20].at[i]),
-            pltpu.make_async_copy(others_hbm[i], others[i], sems[20].at[3 + i]),
+            pltpu.make_async_copy(owns_hbm[i], owns[i], sems[22].at[i]),
+            pltpu.make_async_copy(others_hbm[i], others[i], sems[22].at[3 + i]),
         )
         for i in range(3)
     ]
@@ -288,7 +303,7 @@
             copy.start()
     greet([SEQ_AXES, ("dp",)], sizes)
     mixes = launch(sizes, ("context",), pick_target, True, mix_send, grad_mix, *sems[18:20])
-    rest = launch(sizes, ("expert",), pick_target, True, y_ref, y_back, *sems[6:8])
+    outputs = launch(sizes, ("place",), pick_second, True, y_ref, y_land, *sems[6:8])
 
     def chip_sum(i, expert, place):
         return owns[i][expert, place] + others[i][expert, place].astype(F32)
@@ -313,8 +328,20 @@
     for copy in mixes:
         copy.wait()
     attention_backward((queries, kv_all, mixtures, grad_mix, sums), (grad_query, terms), (sum_kv,))
-    rest += launch(sizes, SEQ_AXES, pick_target, True, terms, kv_back, *sems[8:10])
+    rest = launch(sizes, SEQ_AXES, pick_target, True, terms, kv_back, *sems[8:10])
     rest += launch(sizes, ("context",), pick_target, True, grad_query, query_back, *sems[10:12])
+    half = part_index("half")
+    for copy in outputs:
+        copy.wait()
+
+    def half_sum(number):
+        total = y_land[0, number].astype(F32)
+        for place in range(1, y_land.shape[0]):
+            total = total + y_land[place, number].astype(F32)
+        return total
+
+    y_pass[1 - half] = half_sum(1 - half).astype(BF16)
+    rest += launch(sizes, ("half",), pick_target, False, y_pass, y_got, *sems[20:22])
     for copy in stage_1:
         copy.wait()
 
@@ -354,6 +381,7 @@
         lax.fori_loop(0, experts, close, 0)
     for copy in rest:
         copy.wait()
+    y_total[...] = half_sum(half) + y_got[1 - half].astype(F32)
 
 
 def run_backward(cid, sizes, owns, others, y_terms, data):
@@ -365,12 +393,13 @@
     stage_1 = [(4, experts, 2, *tiles[0]), (4, experts, 2, *tiles[1]), (2, experts, 4, *tiles[2])]
     stage_2 = [(2, experts, *tiles[0]), (2, experts, *tiles[1]), (4, experts, *tiles[2])]
     context = sizes["context"]
-    sizes_of = [4, 4, 2, sizes["expert"], group_size(SEQ_AXES, sizes), context, 2, 2, 4, context]
+    sizes_of = [4, 4, 2, 4, group_size(SEQ_AXES, sizes), context, 2, 2, 4, context, 2]
+    places, rows = y_terms.shape[1], y_terms.shape[2:]
     dma = pltpu.SemaphoreType.DMA
     return pl.pallas_call(
         functools.partial(backward_body, sizes),
         out_shape=[
-            jax.ShapeDtypeStruct(y_terms.shape, BF16),
+            jax.ShapeDtypeStruct(rows, F32),
             jax.ShapeDtypeStruct(kv_all.shape, BF16),
             jax.ShapeDtypeStruct(queries.shape, F32),
             *[jax.ShapeDtypeStruct((experts, *tile), F32) for tile in tiles],
@@ -385,6 +414,9 @@
             pltpu.VMEM(queries.shape, BF16),
             *[pltpu.VMEM(own.shape, F32) for own in owns],
             *[pltpu.VMEM(own.shape, BF16) for own in owns],
+            pltpu.VMEM((places, 2, *rows), BF16),
+            pltpu.VMEM((2, *rows), BF16),
+            pltpu.VMEM((2, *rows), BF16),
             *[dma((n,)) for n in sizes_of for _ in range(2)],
             dma((6,)),
         ],
@@ -777,12 +809,15 @@
 
 
 CHIP_AXES = ("dp", "side", "expert")
+PLANE_AXES = ("side", "expert")
+CUT = 384
 
 
 def sum_body(sizes, *refs):
     query_in, key_in, value_in, output_in, narrow_in = refs[:5]
     whole, load, near, sums, got = refs[5:10]
-    near_send, near_recv, send_sems, recv_sems, give_sems, take_sems, pass_sems, land_sems = refs[10:]
+    near_send, near_recv, send_sems, recv_sems = refs[10:14]
+    gather_sems = refs[14:]
     core = lax.rem(lax.axis_index("context"), 2)
     partner = {"context": lax.axis_index("context") + 1 - 2 * core}
     me, total = own_index(CHIP_AXES, sizes), group_size(CHIP_AXES, sizes)
@@ -804,14 +839,37 @@
         target, peer = place(step)
         return remote(sums.at[target], got.at[me], send_sems.at[step], recv_sems.at[step], peer)
 
-    def gather_copy(step):
-        _, peer = place(step)
-        own = whole.at[core, me]
-        return remote(own, own, give_sems.at[step], take_sems.at[step], peer)
-
-    def pass_copy(step):
-        source = whole.at[core, lax.rem(me - step + total, total)]
-        return remote(source, source, pass_sems.at[step], land_sems.at[step], partner)
+    dp, spot = lax.axis_index("dp"), own_index(PLANE_AXES, sizes)
+    planes, cut = sizes["dp"], CUT
+    low, high = pl.ds(0, cut), pl.ds(cut, whole.shape[4] - cut)
+
+    def across(step, view, pair):
+        peer = {"dp": lax.rem(dp + step, planes)}
+        return remote(view, view, pair[0].at[step], pair[1].at[step], peer)
+
+    def along(step, view, pair):
+        peer = coords_of(PLANE_AXES, sizes, lax.rem(spot + step, plane))
+        return remote(view, view, pair[0].at[step], pair[1].at[step], peer)
+
+    def low_first(step):
+        return across(step, whole.at[core, dp, spot, :, low], gather_sems[0:2])
+
+    def low_second(step):
+        return along(step, whole.at[core, :, spot, :, low], gather_sems[2:4])
+
+    def low_pass(step):
+        view = whole.at[core, :, lax.rem(spot - step + plane, plane), :, low]
+        return remote(view, view, gather_sems[4].at[step], gather_sems[5].at[step], partner)
+
+    def high_first(step):
+        return along(step, whole.at[core, dp, spot, :, high], gather_sems[6:8])
+
+    def high_second(step):
+        return across(step, whole.at[core, dp, :, :, high], gather_sems[8:10])
+
+    def high_pass(step):
+        view = whole.at[core, lax.rem(dp - step + planes, planes), :, :, high]
+        return remote(view, view, gather_sems[10].at[step], gather_sems[11].at[step], partner)
 
     def near_copy(turn):
         chunks = pl.ds(lax.rem(lax.axis_index("dp") + turn, sizes["dp"]) * plane, plane)
@@ -887,17 +945,32 @@
     result = lax.fori_loop(
         0, total, lambda i, held: held + got[i].astype(F32), jnp.zeros(got.shape[1:], F32)
     )
-    whole[core, me] = result.astype(BF16)
-    each(1, total, lambda step: gather_copy(step).start())
-    pass_copy(0).start()
-
-    def forward(step):
-        gather_copy(step).wait_recv()
-        pass_copy(step).start()
-
-    each(1, total, forward)
-    each(1, total, lambda step: gather_copy(step).wait_send())
-    each(0, total, lambda step: pass_copy(step).wait())
+    whole[core, dp, spot] = result.astype(BF16)
+    each(1, planes, lambda step: low_first(step).start())
+    each(1, plane, lambda step: high_first(step).start())
+    each(1, planes, lambda step: low_first(step).wait_recv())
+    each(1, plane, lambda step: low_second(step).start())
+    low_pass(0).start()
+    each(1, plane, lambda step: high_first(step).wait_recv())
+    each(1, planes, lambda step: high_second(step).start())
+    high_pass(0).start()
+
+    def forward_low(step):
+        low_second(step).wait_recv()
+        low_pass(step).start()
+
+    def forward_high(step):
+        high_second(step).wait_recv()
+        high_pass(step).start()
+
+    each(1, plane, forward_low)
+    each(1, planes, forward_high)
+    each(1, planes, lambda step: low_first(step).wait_send())
+    each(1, plane, lambda step: low_second(step).wait_send())
+    each(1, plane, lambda step: high_first(step).wait_send())
+    each(1, planes, lambda step: high_second(step).wait_send())
+    each(0, plane, lambda step: low_pass(step).wait())
+    each(0, planes, lambda step: high_pass(step).wait())
 
 
 def unpack_body(whole, query_out, key_out, value_out, output_out, narrow_out):
@@ -926,14 +999,17 @@
     half = (total, depth // total, wide + wide // 2 + arrays[4].shape[1])
     dma = pltpu.SemaphoreType.DMA
     vmem = pl.BlockSpec(memory_space=pltpu.VMEM)
+    planes = sizes["dp"]
+    plane = total // planes
     whole = pl.pallas_call(
         functools.partial(sum_body, sizes),
-        out_shape=jax.ShapeDtypeStruct((2, *half), BF16),
+        out_shape=jax.ShapeDtypeStruct((2, planes, total // planes, *half[1:]), BF16),
         in_specs=[vmem] * 5,
         out_specs=vmem,
         scratch_shapes=[pltpu.VMEM(half, BF16)] * 4
-        + [dma((sizes["dp"],))] * 2
-        + [dma((total,))] * 6,
+        + [dma((planes,))] * 2
+        + [dma((total,))] * 2
+        + [dma((n,)) for n in (planes, plane, plane, plane, planes, planes) for _ in range(2)],
         name="sum_everywhere",
         compiler_params=pltpu.CompilerParams(
             collective_id=cid, has_side_effects=True, vmem_limit_bytes=60_000_000
@@ -949,7 +1025,7 @@
             pl.BlockSpec((array.shape[0] // parts, array.shape[1]), lambda i: (i, 0)) for array in arrays
         ],
         name="unpack_sums",
-    )(whole)
+    )(whole.reshape(2, *half))
 
 
 def rope_tables(positions, head_size):
@@ -1054,15 +1130,15 @@
     output_grad = t_dot(mixture_flat, grad_after_half)
     grad_mix = dot_t(grad_after_half, output_weight).astype(BF16)
     grad_mix = grad_mix.reshape(tokens, KV_HEADS, 2 * HEAD_DIM).transpose(1, 0, 2)
-    moe_back, kv_back, grad_query, gate_sum, up_sum, down_sum = run_backward(
+    moe_out, kv_back, grad_query, gate_sum, up_sum, down_sum = run_backward(
         8,
         sizes,
         (own_g, own_u, own_d),
         (other_g, other_u, other_d),
-        moe_terms,
+        moe_terms.reshape(2, owners // 2, tokens, width),
         (queries, kv_all, mixtures, grad_mix, sums),
     )
-    outputs = (after_attn + jnp.sum(moe_back.astype(F32), axis=0)).astype(BF16)
+    outputs = (after_attn + moe_out).astype(BF16)
     grad_kv = jnp.sum(kv_back.astype(F32).reshape(KV_HEADS, owners, tokens, 2 * HEAD_DIM), axis=1)
     grad_kv = grad_kv.transpose(1, 0, 2)
     grad_query = grad_query.transpose(1, 0, 2).reshape(tokens, HEADS, HEAD_DIM)

time: 349 us -> 322 us (0.923)
  Pallas kernels: 302 us -> 273 us
    pallas_call x1, Pallas kernels: 92.1 us -> 69.7 us  [sum_everywhere(): pl.pallas_call(functools.partial(sum_body, sizes), out_shape=jax.ShapeDty...]
    pallas_call x1, Pallas kernels: 81.1 us -> 73.9 us  [run_backward(): pl.pallas_call(functools.partial(backward_body, sizes), out_shape=[jax.Sh...]
    unnamed x107 -> x105, local copies, waits for them, and re-layouts: 10.6 us -> 9.77 us
where the time goes in v8:
time: 322 us; the launch traced here: 320 us
  Pallas kernels  273 us (85%)
  local copies, waits for them, and re-layouts  18.6 us (6%)
  matrix products  14.9 us (5%)
  other arithmetic  12.4 us (4%)
    pallas_call x1, Pallas kernels, run_backward(): pl.pallas_call(functools.partial(backward_body, sizes), out_shape=[jax.Sh...  73.9 us
    pallas_call x1, Pallas kernels, run_experts(): pl.pallas_call(functools.partial(moe_body, sizes), grid=(3 * mine + 1,),...  72.4 us
    pallas_call x1, Pallas kernels, sum_everywhere(): pl.pallas_call(functools.partial(sum_body, sizes), out_shape=jax.ShapeDty...  69.7 us
    pallas_call x1, Pallas kernels, run_forward(): pl.pallas_call(functools.partial(forward_body, sizes), out_shape=[jax.Sha...  51.3 us
    unnamed x105, local copies, waits for them, and re-layouts  9.77 us

profile of v8, /device:TPU:1, one launch (start us, length us, event | category | flops | bytes accessed | tf_op | source)
XLA Modules:
  0.0 320.0 jit_solution(13159383595847556699)
XLA Ops:
  0.7 1.1 fusion.13
  3.2 1.3 copy.95
  4.5 1.4 fusion.26
  9.7 51.3 %attention_forward.1 = (bf16[32,128,128]{2,1,0:T(8,128)(2,1)}, bf16[4,128,128]{2,1,0:T(8,128)(2,1)}, bf16[8,128,1024]{2,1,0:T(8,128)(2,1)}, bf16[4,128,128]{2,1,...) custom-call(bf16[4,128,128]{2,1,0:T(8,128)(2,1)} %maximum_bitcast_fusion.refs_0_, ...), custom_call_target="tpu_custom_call" | custom-call | tf_op jit(solution)/shard_map/attention_forward/pallas_call | solution.py:259
  61.1 1.0 copy.105
  63.3 0.8 multiply_convert_fusion.moe_ref
  64.2 1.2 fusion.53
  67.1 72.4 %run_experts.1 = (f32[4,8,64,512]{3,2,1,0:T(8,128)}, f32[4,8,64,512]{3,2,1,0:T(8,128)}, f32[4,8,32,1024]{3,2,1,0:T(8,128)}, bf16[4,8,64,512]{3,2,1,0:T(8,128)(2,...) custom-call(bf16[128,1024]{1,0:T(8,128)(2,1)} %multiply_convert_fusi, ...), custom_call_target="tpu_custom_call" | custom-call | tf_op jit(solution)/shard_map/run_experts/pallas_call | solution.py:751
  141.1 1.9 fusion.42
  143.0 2.1 convert_reduce_fusion
  145.1 1.2 multiply_reduce_fusion
  148.7 73.9 %attention_backward.1 = (f32[128,1024]{1,0:T(8,128)}, bf16[32,128,128]{2,1,0:T(8,128)(2,1)}, f32[4,128,128]{2,1,0:T(8,128)}, f32[4,64,512]{2,1,0:T(8,128)}, f32[...) custom-call(f32[4,8,64,512]{3,2,1,0:T(8,128)} %get-tuple-element.40.refs_0_, f32[4,8,64,512]{3,2,1,0:T(8,128)} %get-tuple-element.41.refs_1_, ...), custom_call_target="tpu_custom_call" | custom-call | tf_op jit(solution)/shard_map/attention_backward/pallas_call | solution.py:399
  222.6 1.2 copy.108
  224.6 1.5 add_convert_fusion.1
  229.6 1.1 fusion.11
  231.0 0.8 pad.4.refs_4_
  231.8 1.4 fusion.30.refs_2_
  233.2 1.4 fusion.28.refs_1_
  234.6 1.7 fusion.34.refs_3_
  236.3 1.9 fusion.32.refs_0_
  238.2 69.7 %sum_everywhere.1 = bf16[2,4,16,16,896]{4,3,2,1,0:T(8,128)(2,1)} custom-call(f32[1024,512]{1,0:T(8,128)} %fusion.32.refs_0_, f32[1024,256]{1,0:T(8,128)} %fusion.28.refs_1_, f32[1024,256]{1,0:T(8,128)} %fusion.30.refs_2_, f32[512,1024]{1,0:T(8,128)} %fusion.34.refs_3_, f32[1024,128]{1,0:T(8,128)} %pad.4.refs_4_), custom_call_target="tpu_custom_call" | custom-call | tf_op jit(solution)/shard_map/sum_everywhere/pallas_call | solution.py:1004
  307.9 5.3 %unpack_sums.1 = (f32[1024,512]{1,0:T(8,128)}, f32[1024,256]{1,0:T(8,128)}, f32[1024,256]{1,0:T(8,128)}, f32[512,1024]{1,0:T(8,128)}, f32[1024,128]{1,0:T(8,128)}) custom-call(bf16[2,64,16,896]{3,2,1,0:T(8,128)(2,1)} %bitcast.117), custom_call_target="tpu_custom_call" | custom-call | tf_op jit(solution)/shard_map/unpack_sums/pallas_call | solution.py:1019
  313.2 2.5 slice_reduce_fusion
  315.7 1.9 copy.113
  (147 shorter events, 18.7 us)
Async XLA Ops:
  0.6 5.5 %copy-start = (bf16[1,128,1024]{2,1,0:T(8,128)(2,1)S(1)}, bf16[1,128,1024]{2,1,0:T(8,128)(2,1)}, u32[]{:S(2)}) copy-start(bf16[1,128,1024]{2,1,0:T(8,128)(2,1)} %param.13) | copy-start | bytes 786436
  0.7 5.5 %copy-start.36 = (f32[1024]{0:T(1024)S(1)}, f32[1024]{0:T(1024)}, u32[]{:S(2)}) copy-start(f32[1024]{0:T(1024)} %param.14) | copy-start | bytes 12292
  0.7 5.2 %copy-start.12 = (bf16[1024,256]{1,0:T(8,128)(2,1)S(1)}, bf16[1024,256]{1,0:T(8,128)(2,1)}, u32[]{:S(2)}) copy-start(bf16[1024,256]{1,0:T(8,128)(2,1)} %param.17) | copy-start | bytes 1572868
  1.9 6.4 %copy-start.42 = (f32[128]{0:T(128)}, f32[128]{0:T(128)S(1)}, u32[]{:S(2)}) copy-start(f32[128]{0:T(128)S(1)} %add_rsqrt_fusion.1) | copy-start | bytes 1540
  3.0 3.8 %copy-start.16 = (f32[128,64]{1,0:T(8,128)}, f32[128,64]{1,0:T(8,128)S(1)}, u32[]{:S(2)}) copy-start(f32[128,64]{1,0:T(8,128)S(1)} %get-tuple-element.141) | copy-start | bytes 98308
  3.0 3.8 %copy-start.20 = (f32[128,64]{1,0:T(8,128)}, f32[128,64]{1,0:T(8,128)S(1)}, u32[]{:S(2)}) copy-start(f32[128,64]{1,0:T(8,128)S(1)} %get-tuple-element.140) | copy-start | bytes 98308
  3.1 58.0 %copy-start.31 = (f32[128,64]{0,1:T(8,128)}, f32[128,64]{0,1:T(8,128)S(1)}, u32[]{:S(2)}) copy-start(f32[128,64]{0,1:T(8,128)S(1)} %copy.102) | copy-start | bytes 98308
  3.2 5.7 %copy-start.33 = (f32[128,64]{0,1:T(8,128)}, f32[128,64]{0,1:T(8,128)S(1)}, u32[]{:S(2)}) copy-start(f32[128,64]{0,1:T(8,128)S(1)} %copy.103) | copy-start | bytes 98308
  8.3 53.8 %copy-start.9 = (bf16[512,1024]{1,0:T(8,128)(2,1)S(1)}, bf16[512,1024]{1,0:T(8,128)(2,1)}, u32[]{:S(2)}) copy-start(bf16[512,1024]{1,0:T(8,128)(2,1)} %param.18) | copy-start | bytes 3145732
  8.8 54.5 %copy-start.38 = (f32[1024]{0:T(1024)S(1)}, f32[1024]{0:T(1024)}, u32[]{:S(2)}) copy-start(f32[1024]{0:T(1024)} %param.19) | copy-start | bytes 12292
  8.9 55.3 %copy-start.34 = (bf16[1024,32]{0,1:T(8,128)(2,1)S(1)}, bf16[1024,32]{0,1:T(8,128)(2,1)}, u32[]{:S(2)}) copy-start(bf16[1024,32]{0,1:T(8,128)(2,1)} %param.20) | copy-start | bytes 196612
  139.5 5.6 %copy-start.3 = (f32[128,1024]{1,0:T(8,128)S(1)}, f32[128,1024]{1,0:T(8,128)}, u32[]{:S(2)}) copy-start(f32[128,1024]{1,0:T(8,128)} %copy-done.2) | copy-start | bytes 1572868
  139.5 5.6 %copy-start.23 = (f32[32,128]{1,0:T(8,128)S(1)}, f32[32,128]{1,0:T(8,128)}, u32[]{:S(2)}) copy-start(f32[32,128]{1,0:T(8,128)} %copy-done.22) | copy-start | bytes 49156
  139.5 5.6 %copy-start.35 = (bf16[1024,32]{0,1:T(8,128)(2,1)S(1)}, bf16[1024,32]{0,1:T(8,128)(2,1)}, u32[]{:S(2)}) copy-start(bf16[1024,32]{0,1:T(8,128)(2,1)} %param.20) | copy-start | bytes 196612
  139.5 5.6 %copy-start.39 = (f32[1024]{0:T(1024)S(1)}, f32[1024]{0:T(1024)}, u32[]{:S(2)}) copy-start(f32[1024]{0:T(1024)} %param.19) | copy-start | bytes 12292
  139.5 5.6 %copy-start.41 = (f32[128]{0:T(128)S(1)}, f32[128]{0:T(128)}, u32[]{:S(2)}) copy-start(f32[128]{0:T(128)} %copy-done.40) | copy-start | bytes 1540
  139.5 5.6 %copy-start.46 = (f32[128]{0:T(128)S(1)}, f32[128]{0:T(128)}, u32[]{:S(2)}) copy-start(f32[128]{0:T(128)} %copy-done.45) | copy-start | bytes 1540
  139.5 5.6 %copy-start.48 = (f32[128]{0:T(128)S(1)}, f32[128]{0:T(128)}, u32[]{:S(2)}) copy-start(f32[128]{0:T(128)} %copy-done.47) | copy-start | bytes 1540
  222.6 3.5 %copy-start.32 = (f32[128,64]{0,1:T(8,128)S(1)}, f32[128,64]{0,1:T(8,128)}, u32[]{:S(2)}) copy-start(f32[128,64]{0,1:T(8,128)} %copy-done.31) | copy-start | bytes 98308
  222.6 4.2 %copy-start.18 = (bf16[32,128,128]{2,1,0:T(8,128)(2,1)S(1)}, bf16[32,128,128]{2,1,0:T(8,128)(2,1)}, u32[]{:S(2)}) copy-start(bf16[32,128,128]{2,1,0:T(8,128)(2,1)} %get-tuple-element.55) | copy-start | bytes 3145732
  230.8 3.8 %copy-start.15 = (bf16[128,4,128]{0,2,1:T(8,128)(2,1)S(1)}, bf16[128,4,128]{0,2,1:T(8,128)(2,1)}, u32[]{:S(2)}) copy-start(bf16[128,4,128]{0,2,1:T(8,128)(2,1)} %copy-done.14) | copy-start | bytes 393220
  307.9 9.7 %copy-start.26 = (f32[4,64,512]{2,1,0:T(8,128)S(1)}, f32[4,64,512]{2,1,0:T(8,128)}, u32[]{:S(2)}) copy-start(f32[4,64,512]{2,1,0:T(8,128)} %get-tuple-element.171) | copy-start | bytes 1572868
  313.2 5.2 %copy-start.25 = (f32[4,64,512]{2,1,0:T(8,128)S(1)}, f32[4,64,512]{2,1,0:T(8,128)}, u32[]{:S(2)}) copy-start(f32[4,64,512]{2,1,0:T(8,128)} %get-tuple-element.172) | copy-start | bytes 1572868
  313.2 6.0 %copy-start.24 = (f32[4,32,1024]{2,1,0:T(8,128)S(1)}, f32[4,32,1024]{2,1,0:T(8,128)}, u32[]{:S(2)}) copy-start(f32[4,32,1024]{2,1,0:T(8,128)} %get-tuple-element.173) | copy-start | bytes 1572868
  (25 other events, 37.5 us)

commit v9 on v8

--- a/solution.py
+++ b/solution.py
@@ -238,15 +238,41 @@
 def forward_body(sizes, *refs):
     kv_send, query_send, grad_ref = refs[:3]
     kv_all, queries, grad_all, mixtures, sums, mixture_back = refs[3:9]
-    sems, scores = refs[9:17], refs[17]
+    sems, scores = refs[9:21], refs[21]
+    mix_sems = refs[22:24]
     greet([SEQ_AXES], sizes)
     early = launch(sizes, ("context",), pick_target, True, query_send, queries, *sems[0:2])
     early += launch(sizes, SEQ_AXES, pick_context, True, kv_send, kv_all, *sems[2:4])
-    late = launch(sizes, ("expert",), pick_whole, True, grad_ref, grad_all, *sems[4:6])
-    for copy in early:
+    half, place = part_index("half"), part_index("place")
+    some = grad_ref.shape[0] // 2
+    upper, lower = pl.ds(0, some), pl.ds(some, some)
+
+    def grad_copies(axis, source, landing, pair):
+        found = []
+        for step in range(1, axis_size(sizes, axis)):
+            target = lax.rem(part_index(axis) + step, axis_size(sizes, axis))
+            copy = pltpu.make_async_remote_copy(
+                src_ref=source,
+                dst_ref=landing,
+                send_sem=pair[0].at[step],
+                recv_sem=pair[1].at[step],
+                device_id=coords_of((axis,), sizes, target),
+                device_id_type=MESH_ID,
+            )
+            copy.start()
+            found.append(copy)
+        return found
+
+    near = grad_copies("half", grad_ref.at[upper], grad_all.at[half, place, upper], sems[4:6])
+    near += grad_copies("place", grad_ref.at[lower], grad_all.at[half, place, lower], sems[6:8])
+    grad_all[half, place] = grad_ref[...]
+    for copy in early + near:
         copy.wait()
+    columns, line = grad_all.at[:, place, upper], grad_all.at[half, :, lower]
+    late = grad_copies("place", columns, columns, sems[8:10])
+    late += grad_copies("half", line, line, sems[10:12])
     attention_forward((queries, kv_all), (mixtures, sums), (scores,))
-    late += launch(sizes, ("context",), pick_target, True, mixtures, mixture_back, *sems[6:8])
+    late += launch(sizes, ("context",), pick_target, True, mixtures, mixture_back, *mix_sems)
     for copy in late:
         copy.wait()
 
@@ -261,7 +287,7 @@
         out_shape=[
             jax.ShapeDtypeStruct((total, tokens, columns), BF16),
             jax.ShapeDtypeStruct(query_send.shape, BF16),
-            jax.ShapeDtypeStruct((owners, *cotangent.shape), BF16),
+            jax.ShapeDtypeStruct((2, owners // 2, *cotangent.shape), BF16),
             jax.ShapeDtypeStruct(query_send.shape, BF16),
             jax.ShapeDtypeStruct((heads, 1, 2 * tokens), F32),
             jax.ShapeDtypeStruct(query_send.shape, BF16),
@@ -269,8 +295,9 @@
         in_specs=[vmem] * 3,
         out_specs=[vmem] * 6,
         scratch_shapes=[
-            *[dma((n,)) for n in (heads, total, owners, heads) for _ in range(2)],
+            *[dma((n,)) for n in (heads, total, 2, owners // 2, owners // 2, 2) for _ in range(2)],
             pltpu.VMEM((total * tokens, 2 * tokens), F32),
+            *[dma((heads,))] * 2,
         ],
         name="attention_forward",
         compiler_params=pltpu.CompilerParams(
@@ -815,9 +842,10 @@
 
 def sum_body(sizes, *refs):
     query_in, key_in, value_in, output_in, narrow_in = refs[:5]
-    whole, load, near, sums, got = refs[5:10]
-    near_send, near_recv, send_sems, recv_sems = refs[10:14]
-    gather_sems = refs[14:]
+    whole, load, near, sums = refs[5:9]
+    low_land, low_mid, low_got, high_land, high_mid, high_got = refs[9:15]
+    near_send, near_recv = refs[15:17]
+    gather_sems, reduce_sems = refs[17:29], refs[29:]
     core = lax.rem(lax.axis_index("context"), 2)
     partner = {"context": lax.axis_index("context") + 1 - 2 * core}
     me, total = own_index(CHIP_AXES, sizes), group_size(CHIP_AXES, sizes)
@@ -835,10 +863,6 @@
             src_ref=src, dst_ref=dst, send_sem=send, recv_sem=recv, device_id=peer, device_id_type=MESH_ID
         )
 
-    def reduce_copy(step):
-        target, peer = place(step)
-        return remote(sums.at[target], got.at[me], send_sems.at[step], recv_sems.at[step], peer)
-
     dp, spot = lax.axis_index("dp"), own_index(PLANE_AXES, sizes)
     planes, cut = sizes["dp"], CUT
     low, high = pl.ds(0, cut), pl.ds(cut, whole.shape[4] - cut)
@@ -870,6 +894,31 @@
     def high_pass(step):
         view = whole.at[core, lax.rem(dp - step + planes, planes), :, :, high]
         return remote(view, view, gather_sems[10].at[step], gather_sems[11].at[step], partner)
+
+    def dp_at(step):
+        return lax.rem(dp + step, planes)
+
+    def spot_at(step):
+        return lax.rem(spot + step, plane)
+
+    def reduce_along(step, source, landing, pair):
+        peer = coords_of(PLANE_AXES, sizes, spot_at(step))
+        return remote(source, landing.at[spot], pair[0].at[step], pair[1].at[step], peer)
+
+    def reduce_across(step, source, landing, pair):
+        return remote(source, landing.at[dp], pair[0].at[step], pair[1].at[step], {"dp": dp_at(step)})
+
+    def low_reduce(step):
+        return reduce_along(step, sums.at[:, spot_at(step), :, low], low_land, reduce_sems[0:2])
+
+    def low_finish(step):
+        return reduce_across(step, low_mid.at[dp_at(step)], low_got, reduce_sems[2:4])
+
+    def high_reduce(step):
+        return reduce_across(step, sums.at[dp_at(step), :, :, high], high_land, reduce_sems[4:6])
+
+    def high_finish(step):
+        return reduce_along(step, high_mid.at[spot_at(step)], high_got, reduce_sems[6:8])
 
     def near_copy(turn):
         chunks = pl.ds(lax.rem(lax.axis_index("dp") + turn, sizes["dp"]) * plane, plane)
@@ -926,25 +975,45 @@
 
             @pl.when(core == number)
             def _(number=number, base=base):
-                def add(chunk):
-                    sums[chunk] = (pack(number, chunk) + near[chunk].astype(F32)).astype(BF16)
+                def add(chunk, base=base, turn=turn):
+                    place_now = lax.rem(lax.axis_index("dp") + turn, planes)
+                    both = pack(number, chunk) + near[chunk].astype(F32)
+                    sums[place_now, chunk - base] = both.astype(BF16)
 
                 each(base, base + plane, add)
 
-        def send(i, base=base):
-            target = base + lax.rem(me + i, plane)
-
-            @pl.when(target != me)
-            def _():
-                reduce_copy(lax.rem(target - me + total, total)).start()
-
-        each(0, plane, send)
-
-    got[me] = sums[me]
-    each(1, total, lambda step: reduce_copy(step).wait())
-    result = lax.fori_loop(
-        0, total, lambda i, held: held + got[i].astype(F32), jnp.zeros(got.shape[1:], F32)
-    )
+        if turn > 0:
+            high_reduce(turn).start()
+
+    each(1, plane, lambda step: low_reduce(step).start())
+    each(1, planes, lambda step: high_reduce(step).wait())
+
+    def high_add(i):
+        held = sums[dp, i, :, high].astype(F32)
+        for step in range(1, planes):
+            held = held + high_land[dp_at(step), i].astype(F32)
+        high_mid[i] = held.astype(BF16)
+
+    each(0, plane, high_add)
+    each(1, plane, lambda step: high_finish(step).start())
+    each(1, plane, lambda step: low_reduce(step).wait())
+
+    def low_add(i):
+        held = sums[i, spot, :, low].astype(F32)
+        for step in range(1, plane):
+            held = held + low_land[spot_at(step), i].astype(F32)
+        low_mid[i] = held.astype(BF16)
+
+    each(0, planes, low_add)
+    each(1, planes, lambda step: low_finish(step).start())
+    each(1, plane, lambda step: high_finish(step).wait())
+    each(1, planes, lambda step: low_finish(step).wait())
+    result_low, result_high = low_mid[dp].astype(F32), high_mid[spot].astype(F32)
+    for step in range(1, planes):
+        result_low = result_low + low_got[dp_at(step)].astype(F32)
+    for step in range(1, plane):
+        result_high = result_high + high_got[spot_at(step)].astype(F32)
+    result = jnp.concatenate([result_low, result_high], axis=1)
     whole[core, dp, spot] = result.astype(BF16)
     each(1, planes, lambda step: low_first(step).start())
     each(1, plane, lambda step: high_first(step).start())
@@ -1001,15 +1070,26 @@
     vmem = pl.BlockSpec(memory_space=pltpu.VMEM)
     planes = sizes["dp"]
     plane = total // planes
+    rows, less, more = half[1], CUT, half[2] - CUT
+    shapes = [
+        (planes, plane, *half[1:]),
+        (plane, planes, rows, less),
+        (planes, rows, less),
+        (planes, rows, less),
+        (planes, plane, rows, more),
+        (plane, rows, more),
+        (plane, rows, more),
+    ]
     whole = pl.pallas_call(
         functools.partial(sum_body, sizes),
         out_shape=jax.ShapeDtypeStruct((2, planes, total // planes, *half[1:]), BF16),
         in_specs=[vmem] * 5,
         out_specs=vmem,
-        scratch_shapes=[pltpu.VMEM(half, BF16)] * 4
+        scratch_shapes=[pltpu.VMEM(half, BF16)] * 2
+        + [pltpu.VMEM(shape, BF16) for shape in shapes]
         + [dma((planes,))] * 2
-        + [dma((total,))] * 2
-        + [dma((n,)) for n in (planes, plane, plane, plane, planes, planes) for _ in range(2)],
+        + [dma((n,)) for n in (planes, plane, plane, plane, planes, planes) for _ in range(2)]
+        + [dma((n,)) for n in (plane, planes, planes, plane) for _ in range(2)],
         name="sum_everywhere",
         compiler_params=pltpu.CompilerParams(
             collective_id=cid, has_side_effects=True, vmem_limit_bytes=60_000_000
@@ -1113,7 +1193,7 @@
     gate_table = jnp.where(chosen, gates, -1.0)
 
     own_g, own_u, own_d, other_g, other_u, other_d, moe_terms, grad_back, dot_back = run_experts(
-        3, sizes, moe_input, gate_table, grad_all, gate_weight, up_weight, down_weight
+        3, sizes, moe_input, gate_table, grad_all.reshape(owners, tokens, width), gate_weight, up_weight, down_weight
     )
     grad_gates = dot_back[:, :mine].reshape(EXPERTS, tokens)
     grad_logits = gates * (grad_gates - jnp.sum(gates * grad_gates, axis=0, keepdims=True))

time: 322 us -> 298 us (0.925)
  Pallas kernels: 273 us -> 249 us
    pallas_call x1, Pallas kernels: 69.7 us -> 58 us  [sum_everywhere(): pl.pallas_call(functools.partial(sum_body, sizes), out_shape=jax.ShapeDty...]
    pallas_call x1, Pallas kernels: 51.3 us -> 43.6 us  [run_forward(): pl.pallas_call(functools.partial(forward_body, sizes), out_shape=[jax.Sha...]
    pallas_call x1, Pallas kernels: 72.4 us -> 68.6 us  [run_experts(): pl.pallas_call(functools.partial(moe_body, sizes), grid=(3 * mine + 1,),...]
where the time goes in v9:
time: 298 us; the launch traced here: 297 us
  Pallas kernels  249 us (84%)
  local copies, waits for them, and re-layouts  18.6 us (6%)
  matrix products  14.9 us (5%)
  other arithmetic  12.4 us (4%)
    pallas_call x1, Pallas kernels, run_backward(): pl.pallas_call(functools.partial(backward_body, sizes), out_shape=[jax.Sh...  73.8 us
    pallas_call x1, Pallas kernels, run_experts(): pl.pallas_call(functools.partial(moe_body, sizes), grid=(3 * mine + 1,),...  68.6 us
    pallas_call x1, Pallas kernels, sum_everywhere(): pl.pallas_call(functools.partial(sum_body, sizes), out_shape=jax.ShapeDty...  58 us
    pallas_call x1, Pallas kernels, run_forward(): pl.pallas_call(functools.partial(forward_body, sizes), out_shape=[jax.Sha...  43.6 us
    unnamed x105, local copies, waits for them, and re-layouts  9.77 us
    dot_general x4, matrix products, t_dot(): lax.dot_general(left, right, (((0,), (0,)), ((), ())), preferred_element_...  6.32 us

profile of v9, /device:TPU:1, one launch (start us, length us, event | category | flops | bytes accessed | tf_op | source)
XLA Modules:
  0.0 296.6 jit_solution(16385549984405711815)
XLA Ops:
  0.7 1.1 fusion.13
  3.2 1.3 copy.95
  4.5 1.4 fusion.26
  9.7 43.6 %attention_forward.1 = (bf16[32,128,128]{2,1,0:T(8,128)(2,1)}, bf16[4,128,128]{2,1,0:T(8,128)(2,1)}, bf16[2,4,128,1024]{3,2,1,0:T(8,128)(2,1)}, bf16[4,128,128]{...) custom-call(bf16[4,128,128]{2,1,0:T(8,128)(2,1)} %maximum_bitcast_fusion.refs_0_, ...), custom_call_target="tpu_custom_call" | custom-call | tf_op jit(solution)/shard_map/attention_forward/pallas_call | solution.py:285
  53.4 1.0 copy.105
  55.6 0.8 multiply_convert_fusion.moe_ref
  56.5 1.2 fusion.53
  59.4 68.6 %run_experts.1 = (f32[4,8,64,512]{3,2,1,0:T(8,128)}, f32[4,8,64,512]{3,2,1,0:T(8,128)}, f32[4,8,32,1024]{3,2,1,0:T(8,128)}, bf16[4,8,64,512]{3,2,1,0:T(8,128)(2,...) custom-call(bf16[128,1024]{1,0:T(8,128)(2,1)} %multiply_convert_fusi, ...), custom_call_target="tpu_custom_call" | custom-call | tf_op jit(solution)/shard_map/run_experts/pallas_call | solution.py:778
  129.6 1.9 fusion.42
  131.5 2.1 convert_reduce_fusion
  133.6 1.2 multiply_reduce_fusion
  137.2 73.8 %attention_backward.1 = (f32[128,1024]{1,0:T(8,128)}, bf16[32,128,128]{2,1,0:T(8,128)(2,1)}, f32[4,128,128]{2,1,0:T(8,128)}, f32[4,64,512]{2,1,0:T(8,128)}, f32[...) custom-call(f32[4,8,64,512]{3,2,1,0:T(8,128)} %get-tuple-element.40.refs_0_, f32[4,8,64,512]{3,2,1,0:T(8,128)} %get-tuple-element.41.refs_1_, ...), custom_call_target="tpu_custom_call" | custom-call | tf_op jit(solution)/shard_map/attention_backward/pallas_call | solution.py:426
  211.0 1.2 copy.108
  213.0 1.5 add_convert_fusion.1
  218.0 1.1 fusion.11
  219.3 0.8 pad.4.refs_4_
  220.2 1.4 fusion.30.refs_2_
  221.5 1.4 fusion.28.refs_1_
  222.9 1.7 fusion.34.refs_3_
  224.6 1.9 fusion.32.refs_0_
  226.5 58.0 %sum_everywhere.1 = bf16[2,4,16,16,896]{4,3,2,1,0:T(8,128)(2,1)} custom-call(f32[1024,512]{1,0:T(8,128)} %fusion.32.refs_0_, f32[1024,256]{1,0:T(8,128)} %fusion.28.refs_1_, f32[1024,256]{1,0:T(8,128)} %fusion.30.refs_2_, f32[512,1024]{1,0:T(8,128)} %fusion.34.refs_3_, f32[1024,128]{1,0:T(8,128)} %pad.4.refs_4_), custom_call_target="tpu_custom_call" | custom-call | tf_op jit(solution)/shard_map/sum_everywhere/pallas_call | solution.py:1083
  284.5 5.3 %unpack_sums.1 = (f32[1024,512]{1,0:T(8,128)}, f32[1024,256]{1,0:T(8,128)}, f32[1024,256]{1,0:T(8,128)}, f32[512,1024]{1,0:T(8,128)}, f32[1024,128]{1,0:T(8,128)}) custom-call(bf16[2,64,16,896]{3,2,1,0:T(8,128)(2,1)} %bitcast.118), custom_call_target="tpu_custom_call" | custom-call | tf_op jit(solution)/shard_map/unpack_sums/pallas_call | solution.py:1099
  289.9 2.5 slice_reduce_fusion
  292.4 1.9 copy.113
  (147 shorter events, 18.7 us)
Async XLA Ops:
  0.6 5.5 %copy-start = (bf16[1,128,1024]{2,1,0:T(8,128)(2,1)S(1)}, bf16[1,128,1024]{2,1,0:T(8,128)(2,1)}, u32[]{:S(2)}) copy-start(bf16[1,128,1024]{2,1,0:T(8,128)(2,1)} %param.13) | copy-start | bytes 786436
  0.7 5.5 %copy-start.36 = (f32[1024]{0:T(1024)S(1)}, f32[1024]{0:T(1024)}, u32[]{:S(2)}) copy-start(f32[1024]{0:T(1024)} %param.14) | copy-start | bytes 12292
  0.7 5.2 %copy-start.12 = (bf16[1024,256]{1,0:T(8,128)(2,1)S(1)}, bf16[1024,256]{1,0:T(8,128)(2,1)}, u32[]{:S(2)}) copy-start(bf16[1024,256]{1,0:T(8,128)(2,1)} %param.17) | copy-start | bytes 1572868
  1.9 6.4 %copy-start.42 = (f32[128]{0:T(128)}, f32[128]{0:T(128)S(1)}, u32[]{:S(2)}) copy-start(f32[128]{0:T(128)S(1)} %add_rsqrt_fusion.1) | copy-start | bytes 1540
  3.0 3.8 %copy-start.16 = (f32[128,64]{1,0:T(8,128)}, f32[128,64]{1,0:T(8,128)S(1)}, u32[]{:S(2)}) copy-start(f32[128,64]{1,0:T(8,128)S(1)} %get-tuple-element.141) | copy-start | bytes 98308
  3.0 3.8 %copy-start.20 = (f32[128,64]{1,0:T(8,128)}, f32[128,64]{1,0:T(8,128)S(1)}, u32[]{:S(2)}) copy-start(f32[128,64]{1,0:T(8,128)S(1)} %get-tuple-element.140) | copy-start | bytes 98308
  3.1 50.2 %copy-start.31 = (f32[128,64]{0,1:T(8,128)}, f32[128,64]{0,1:T(8,128)S(1)}, u32[]{:S(2)}) copy-start(f32[128,64]{0,1:T(8,128)S(1)} %copy.102) | copy-start | bytes 98308
  3.2 5.7 %copy-start.33 = (f32[128,64]{0,1:T(8,128)}, f32[128,64]{0,1:T(8,128)S(1)}, u32[]{:S(2)}) copy-start(f32[128,64]{0,1:T(8,128)S(1)} %copy.103) | copy-start | bytes 98308
  8.3 46.1 %copy-start.9 = (bf16[512,1024]{1,0:T(8,128)(2,1)S(1)}, bf16[512,1024]{1,0:T(8,128)(2,1)}, u32[]{:S(2)}) copy-start(bf16[512,1024]{1,0:T(8,128)(2,1)} %param.18) | copy-start | bytes 3145732
  8.8 46.8 %copy-start.38 = (f32[1024]{0:T(1024)S(1)}, f32[1024]{0:T(1024)}, u32[]{:S(2)}) copy-start(f32[1024]{0:T(1024)} %param.19) | copy-start | bytes 12292
  8.9 47.6 %copy-start.34 = (bf16[1024,32]{0,1:T(8,128)(2,1)S(1)}, bf16[1024,32]{0,1:T(8,128)(2,1)}, u32[]{:S(2)}) copy-start(bf16[1024,32]{0,1:T(8,128)(2,1)} %param.20) | copy-start | bytes 196612
  128.0 5.6 %copy-start.3 = (f32[128,1024]{1,0:T(8,128)S(1)}, f32[128,1024]{1,0:T(8,128)}, u32[]{:S(2)}) copy-start(f32[128,1024]{1,0:T(8,128)} %copy-done.2) | copy-start | bytes 1572868
  128.0 5.6 %copy-start.23 = (f32[32,128]{1,0:T(8,128)S(1)}, f32[32,128]{1,0:T(8,128)}, u32[]{:S(2)}) copy-start(f32[32,128]{1,0:T(8,128)} %copy-done.22) | copy-start | bytes 49156
  128.0 5.6 %copy-start.35 = (bf16[1024,32]{0,1:T(8,128)(2,1)S(1)}, bf16[1024,32]{0,1:T(8,128)(2,1)}, u32[]{:S(2)}) copy-start(bf16[1024,32]{0,1:T(8,128)(2,1)} %param.20) | copy-start | bytes 196612
  128.0 5.6 %copy-start.39 = (f32[1024]{0:T(1024)S(1)}, f32[1024]{0:T(1024)}, u32[]{:S(2)}) copy-start(f32[1024]{0:T(1024)} %param.19) | copy-start | bytes 12292
  128.0 5.6 %copy-start.41 = (f32[128]{0:T(128)S(1)}, f32[128]{0:T(128)}, u32[]{:S(2)}) copy-start(f32[128]{0:T(128)} %copy-done.40) | copy-start | bytes 1540
  128.0 5.6 %copy-start.46 = (f32[128]{0:T(128)S(1)}, f32[128]{0:T(128)}, u32[]{:S(2)}) copy-start(f32[128]{0:T(128)} %copy-done.45) | copy-start | bytes 1540
  128.0 5.6 %copy-start.48 = (f32[128]{0:T(128)S(1)}, f32[128]{0:T(128)}, u32[]{:S(2)}) copy-start(f32[128]{0:T(128)} %copy-done.47) | copy-start | bytes 1540
  211.0 3.5 %copy-start.32 = (f32[128,64]{0,1:T(8,128)S(1)}, f32[128,64]{0,1:T(8,128)}, u32[]{:S(2)}) copy-start(f32[128,64]{0,1:T(8,128)} %copy-done.31) | copy-start | bytes 98308
  211.0 4.2 %copy-start.18 = (bf16[32,128,128]{2,1,0:T(8,128)(2,1)S(1)}, bf16[32,128,128]{2,1,0:T(8,128)(2,1)}, u32[]{:S(2)}) copy-start(bf16[32,128,128]{2,1,0:T(8,128)(2,1)} %get-tuple-element.55) | copy-start | bytes 3145732
  219.1 3.8 %copy-start.15 = (bf16[128,4,128]{0,2,1:T(8,128)(2,1)S(1)}, bf16[128,4,128]{0,2,1:T(8,128)(2,1)}, u32[]{:S(2)}) copy-start(bf16[128,4,128]{0,2,1:T(8,128)(2,1)} %copy-done.14) | copy-start | bytes 393220
  284.5 9.7 %copy-start.26 = (f32[4,64,512]{2,1,0:T(8,128)S(1)}, f32[4,64,512]{2,1,0:T(8,128)}, u32[]{:S(2)}) copy-start(f32[4,64,512]{2,1,0:T(8,128)} %get-tuple-element.171) | copy-start | bytes 1572868
  289.9 5.2 %copy-start.25 = (f32[4,64,512]{2,1,0:T(8,128)S(1)}, f32[4,64,512]{2,1,0:T(8,128)}, u32[]{:S(2)}) copy-start(f32[4,64,512]{2,1,0:T(8,128)} %get-tuple-element.172) | copy-start | bytes 1572868
  289.9 6.0 %copy-start.24 = (f32[4,32,1024]{2,1,0:T(8,128)S(1)}, f32[4,32,1024]{2,1,0:T(8,128)}, u32[]{:S(2)}) copy-start(f32[4,32,1024]{2,1,0:T(8,128)} %get-tuple-element.173) | copy-start | bytes 1572868
  (25 other events, 37.5 us)

commit v10 on v9

--- a/solution.py
+++ b/solution.py
@@ -609,6 +609,11 @@
             for copy in tokens_to(number):
                 copy.start()
 
+    def combine_outputs(first):
+        for position in range(first, first + group):
+            moved = t_dot(highs[position], eo_all[position]) + t_dot(lows[position], eo_all[position])
+            y_send[owner_at(owner, NEAR[position], -1)] = moved.astype(BF16)
+
     @pl.when(step == mine)
     def _():
         for copy in own_results():
@@ -619,12 +624,17 @@
         for number in range(group, owners):
             for copy in tokens_to(number):
                 copy.wait_recv()
+        combine_outputs(0)
 
     @pl.when(step == 2 * mine)
     def _():
         for number in range(group, owners):
             for copy in results_of(number):
                 copy.start()
+        combine_outputs(group)
+
+    @pl.when(step == 2 * mine + 1)
+    def _():
         pltpu.make_async_copy(y_send, y_out, sems[6].at[0]).start()
 
     for number in range(mine):
@@ -706,8 +716,6 @@
             for j in range(group):
                 position, source = tile * group + j, source_of(j)
                 d_send[source] = t_dot(picks[position], dbuf_all[position]).astype(BF16)
-                moved = t_dot(highs[position], eo_all[position]) + t_dot(lows[position], eo_all[position])
-                y_send[source] = moved.astype(BF16)
 
     @pl.when((step >= 2 * mine) & (step < 3 * mine))
     def _():

time: 298 us -> 298 us (level)
  no operation moved by 1% of the time
where the time goes in v10:
time: 298 us; the launch traced here: 297 us
  Pallas kernels  250 us (84%)
  local copies, waits for them, and re-layouts  18.6 us (6%)
  matrix products  14.9 us (5%)
  other arithmetic  12.4 us (4%)
    pallas_call x1, Pallas kernels, run_backward(): pl.pallas_call(functools.partial(backward_body, sizes), out_shape=[jax.Sh...  73 us
    pallas_call x1, Pallas kernels, run_experts(): pl.pallas_call(functools.partial(moe_body, sizes), grid=(3 * mine + 1,),...  69.7 us
    pallas_call x1, Pallas kernels, sum_everywhere(): pl.pallas_call(functools.partial(sum_body, sizes), out_shape=jax.ShapeDty...  58 us
    pallas_call x1, Pallas kernels, run_forward(): pl.pallas_call(functools.partial(forward_body, sizes), out_shape=[jax.Sha...  43.6 us
    unnamed x105, local copies, waits for them, and re-layouts  9.77 us
    dot_general x4, matrix products, t_dot(): lax.dot_general(left, right, (((0,), (0,)), ((), ())), preferred_element_...  6.32 us

profile of v10, /device:TPU:1, one launch (start us, length us, event | category | flops | bytes accessed | tf_op | source)
XLA Modules:
  0.0 297.0 jit_solution(12775231930045778298)
XLA Ops:
  0.7 1.1 fusion.13
  3.2 1.3 copy.95
  4.5 1.4 fusion.26
  9.7 43.6 %attention_forward.1 = (bf16[32,128,128]{2,1,0:T(8,128)(2,1)}, bf16[4,128,128]{2,1,0:T(8,128)(2,1)}, bf16[2,4,128,1024]{3,2,1,0:T(8,128)(2,1)}, bf16[4,128,128]{...) custom-call(bf16[4,128,128]{2,1,0:T(8,128)(2,1)} %maximum_bitcast_fusion.refs_0_, ...), custom_call_target="tpu_custom_call" | custom-call | tf_op jit(solution)/shard_map/attention_forward/pallas_call | solution.py:285
  53.4 1.0 copy.105
  55.6 0.8 multiply_convert_fusion.moe_ref
  56.5 1.2 fusion.53
  59.4 69.7 %run_experts.1 = (f32[4,8,64,512]{3,2,1,0:T(8,128)}, f32[4,8,64,512]{3,2,1,0:T(8,128)}, f32[4,8,32,1024]{3,2,1,0:T(8,128)}, bf16[4,8,64,512]{3,2,1,0:T(8,128)(2,...) custom-call(bf16[128,1024]{1,0:T(8,128)(2,1)} %multiply_convert_fusi, ...), custom_call_target="tpu_custom_call" | custom-call | tf_op jit(solution)/shard_map/run_experts/pallas_call | solution.py:786
  130.7 1.9 fusion.42
  132.5 2.1 convert_reduce_fusion
  134.7 1.2 multiply_reduce_fusion
  138.2 73.0 %attention_backward.1 = (f32[128,1024]{1,0:T(8,128)}, bf16[32,128,128]{2,1,0:T(8,128)(2,1)}, f32[4,128,128]{2,1,0:T(8,128)}, f32[4,64,512]{2,1,0:T(8,128)}, f32[...) custom-call(f32[4,8,64,512]{3,2,1,0:T(8,128)} %get-tuple-element.40.refs_0_, f32[4,8,64,512]{3,2,1,0:T(8,128)} %get-tuple-element.41.refs_1_, ...), custom_call_target="tpu_custom_call" | custom-call | tf_op jit(solution)/shard_map/attention_backward/pallas_call | solution.py:426
  211.3 1.2 copy.108
  213.3 1.5 add_convert_fusion.1
  218.3 1.1 fusion.11
  219.6 0.8 pad.4.refs_4_
  220.5 1.4 fusion.30.refs_2_
  221.9 1.4 fusion.28.refs_1_
  223.2 1.7 fusion.34.refs_3_
  225.0 1.9 fusion.32.refs_0_
  226.8 58.0 %sum_everywhere.1 = bf16[2,4,16,16,896]{4,3,2,1,0:T(8,128)(2,1)} custom-call(f32[1024,512]{1,0:T(8,128)} %fusion.32.refs_0_, f32[1024,256]{1,0:T(8,128)} %fusion.28.refs_1_, f32[1024,256]{1,0:T(8,128)} %fusion.30.refs_2_, f32[512,1024]{1,0:T(8,128)} %fusion.34.refs_3_, f32[1024,128]{1,0:T(8,128)} %pad.4.refs_4_), custom_call_target="tpu_custom_call" | custom-call | tf_op jit(solution)/shard_map/sum_everywhere/pallas_call | solution.py:1091
  284.8 5.3 %unpack_sums.1 = (f32[1024,512]{1,0:T(8,128)}, f32[1024,256]{1,0:T(8,128)}, f32[1024,256]{1,0:T(8,128)}, f32[512,1024]{1,0:T(8,128)}, f32[1024,128]{1,0:T(8,128)}) custom-call(bf16[2,64,16,896]{3,2,1,0:T(8,128)(2,1)} %bitcast.118), custom_call_target="tpu_custom_call" | custom-call | tf_op jit(solution)/shard_map/unpack_sums/pallas_call | solution.py:1107
  290.2 2.5 slice_reduce_fusion
  292.7 1.9 copy.113
  (147 shorter events, 18.7 us)
Async XLA Ops:
  0.6 5.5 %copy-start = (bf16[1,128,1024]{2,1,0:T(8,128)(2,1)S(1)}, bf16[1,128,1024]{2,1,0:T(8,128)(2,1)}, u32[]{:S(2)}) copy-start(bf16[1,128,1024]{2,1,0:T(8,128)(2,1)} %param.13) | copy-start | bytes 786436
  0.7 5.5 %copy-start.36 = (f32[1024]{0:T(1024)S(1)}, f32[1024]{0:T(1024)}, u32[]{:S(2)}) copy-start(f32[1024]{0:T(1024)} %param.14) | copy-start | bytes 12292
  0.7 5.2 %copy-start.12 = (bf16[1024,256]{1,0:T(8,128)(2,1)S(1)}, bf16[1024,256]{1,0:T(8,128)(2,1)}, u32[]{:S(2)}) copy-start(bf16[1024,256]{1,0:T(8,128)(2,1)} %param.17) | copy-start | bytes 1572868
  1.9 6.4 %copy-start.42 = (f32[128]{0:T(128)}, f32[128]{0:T(128)S(1)}, u32[]{:S(2)}) copy-start(f32[128]{0:T(128)S(1)} %add_rsqrt_fusion.1) | copy-start | bytes 1540
  3.0 3.8 %copy-start.16 = (f32[128,64]{1,0:T(8,128)}, f32[128,64]{1,0:T(8,128)S(1)}, u32[]{:S(2)}) copy-start(f32[128,64]{1,0:T(8,128)S(1)} %get-tuple-element.141) | copy-start | bytes 98308
  3.0 3.8 %copy-start.20 = (f32[128,64]{1,0:T(8,128)}, f32[128,64]{1,0:T(8,128)S(1)}, u32[]{:S(2)}) copy-start(f32[128,64]{1,0:T(8,128)S(1)} %get-tuple-element.140) | copy-start | bytes 98308
  3.1 50.2 %copy-start.31 = (f32[128,64]{0,1:T(8,128)}, f32[128,64]{0,1:T(8,128)S(1)}, u32[]{:S(2)}) copy-start(f32[128,64]{0,1:T(8,128)S(1)} %copy.102) | copy-start | bytes 98308
  3.2 5.7 %copy-start.33 = (f32[128,64]{0,1:T(8,128)}, f32[128,64]{0,1:T(8,128)S(1)}, u32[]{:S(2)}) copy-start(f32[128,64]{0,1:T(8,128)S(1)} %copy.103) | copy-start | bytes 98308
  8.3 46.1 %copy-start.9 = (bf16[512,1024]{1,0:T(8,128)(2,1)S(1)}, bf16[512,1024]{1,0:T(8,128)(2,1)}, u32[]{:S(2)}) copy-start(bf16[512,1024]{1,0:T(8,128)(2,1)} %param.18) | copy-start | bytes 3145732
  8.8 46.8 %copy-start.38 = (f32[1024]{0:T(1024)S(1)}, f32[1024]{0:T(1024)}, u32[]{:S(2)}) copy-start(f32[1024]{0:T(1024)} %param.19) | copy-start | bytes 12292
  8.9 47.6 %copy-start.34 = (bf16[1024,32]{0,1:T(8,128)(2,1)S(1)}, bf16[1024,32]{0,1:T(8,128)(2,1)}, u32[]{:S(2)}) copy-start(bf16[1024,32]{0,1:T(8,128)(2,1)} %param.20) | copy-start | bytes 196612
  129.0 5.6 %copy-start.3 = (f32[128,1024]{1,0:T(8,128)S(1)}, f32[128,1024]{1,0:T(8,128)}, u32[]{:S(2)}) copy-start(f32[128,1024]{1,0:T(8,128)} %copy-done.2) | copy-start | bytes 1572868
  129.1 5.6 %copy-start.23 = (f32[32,128]{1,0:T(8,128)S(1)}, f32[32,128]{1,0:T(8,128)}, u32[]{:S(2)}) copy-start(f32[32,128]{1,0:T(8,128)} %copy-done.22) | copy-start | bytes 49156
  129.1 5.6 %copy-start.35 = (bf16[1024,32]{0,1:T(8,128)(2,1)S(1)}, bf16[1024,32]{0,1:T(8,128)(2,1)}, u32[]{:S(2)}) copy-start(bf16[1024,32]{0,1:T(8,128)(2,1)} %param.20) | copy-start | bytes 196612
  129.1 5.6 %copy-start.39 = (f32[1024]{0:T(1024)S(1)}, f32[1024]{0:T(1024)}, u32[]{:S(2)}) copy-start(f32[1024]{0:T(1024)} %param.19) | copy-start | bytes 12292
  129.1 5.6 %copy-start.41 = (f32[128]{0:T(128)S(1)}, f32[128]{0:T(128)}, u32[]{:S(2)}) copy-start(f32[128]{0:T(128)} %copy-done.40) | copy-start | bytes 1540
  129.1 5.6 %copy-start.46 = (f32[128]{0:T(128)S(1)}, f32[128]{0:T(128)}, u32[]{:S(2)}) copy-start(f32[128]{0:T(128)} %copy-done.45) | copy-start | bytes 1540
  129.1 5.6 %copy-start.48 = (f32[128]{0:T(128)S(1)}, f32[128]{0:T(128)}, u32[]{:S(2)}) copy-start(f32[128]{0:T(128)} %copy-done.47) | copy-start | bytes 1540
  211.3 3.5 %copy-start.32 = (f32[128,64]{0,1:T(8,128)S(1)}, f32[128,64]{0,1:T(8,128)}, u32[]{:S(2)}) copy-start(f32[128,64]{0,1:T(8,128)} %copy-done.31) | copy-start | bytes 98308
  211.3 4.2 %copy-start.18 = (bf16[32,128,128]{2,1,0:T(8,128)(2,1)S(1)}, bf16[32,128,128]{2,1,0:T(8,128)(2,1)}, u32[]{:S(2)}) copy-start(bf16[32,128,128]{2,1,0:T(8,128)(2,1)} %get-tuple-element.55) | copy-start | bytes 3145732
  219.4 3.8 %copy-start.15 = (bf16[128,4,128]{0,2,1:T(8,128)(2,1)S(1)}, bf16[128,4,128]{0,2,1:T(8,128)(2,1)}, u32[]{:S(2)}) copy-start(bf16[128,4,128]{0,2,1:T(8,128)(2,1)} %copy-done.14) | copy-start | bytes 393220
  284.8 9.7 %copy-start.26 = (f32[4,64,512]{2,1,0:T(8,128)S(1)}, f32[4,64,512]{2,1,0:T(8,128)}, u32[]{:S(2)}) copy-start(f32[4,64,512]{2,1,0:T(8,128)} %get-tuple-element.171) | copy-start | bytes 1572868
  290.2 5.2 %copy-start.25 = (f32[4,64,512]{2,1,0:T(8,128)S(1)}, f32[4,64,512]{2,1,0:T(8,128)}, u32[]{:S(2)}) copy-start(f32[4,64,512]{2,1,0:T(8,128)} %get-tuple-element.172) | copy-start | bytes 1572868
  290.2 6.0 %copy-start.24 = (f32[4,32,1024]{2,1,0:T(8,128)S(1)}, f32[4,32,1024]{2,1,0:T(8,128)}, u32[]{:S(2)}) copy-start(f32[4,32,1024]{2,1,0:T(8,128)} %get-tuple-element.173) | copy-start | bytes 1572868
  (25 other events, 37.5 us)
